TPU v7x, 128 devices: a whole 4x4x4 slice. The times are simulated.
128 devices in a mesh: blk: 4 (over x_lo, core), shard: 32 (over x_hi, y, z).
Axes of the slice: x: 4 (x_hi: 2, x_lo: 2; x = x_hi * 2 + x_lo), y: 4, z: 4, core: 2. Of those that a mesh axis runs over, the one named last changes fastest.
Arguments:
- item_features: bfloat16 [131072, 1024], P('shard'), may hold values from -6 to 6
- tower_weight: bfloat16 [1024, 512], replicated, may hold values from -0.1875 to 0.1875
- gate_in: bfloat16 [64, 128], replicated, may hold values from -0.75 to 0.75
- gate_in_bias: bfloat16 [128], replicated, may hold values from -4 to 4
- gate_out: bfloat16 [128, 64], replicated, may hold values from -0.5 to 0.5
- gate_out_bias: bfloat16 [64], replicated, may hold values from -4 to 4
- user_table: bfloat16 [16384, 512], P(('blk', 'shard')), may hold values from -6 to 6
- user_ids: int32 [512], P(('blk', 'shard')), may hold values from 0 to 127
- positive_item: int32 [512, 16], P(('blk', 'shard')), may hold values from 0 to 7167
- listed_owner: int32 [1792, 1], P(('blk', 'shard')), may hold values from 0 to 31; in each aligned block of 14 rows (0 to 13, 14 to 27, ...) at most 2 rows name the same one
- listed_slot: int32 [1792], P(('blk', 'shard')), may hold values from 0 to 31
Outputs:
- tower_gradient: float32 [1024, 512], P('shard')
- user_gradient: float32 [16384, 512], P(('blk', 'shard'))
Inputs may be any that keep to these rules, and one draw needn't show every extreme that they name: `listed_owner`: at most 2 of the 14 listings of one trainer name the same owner. `user_ids`: A row of the trainer's own 128 rows of user_table. `positive_item`: A position among the rows of the user's circle.
All inputs are finite; a program needn't handle non-finite values.
Results may differ from a plain program's by a relative error of at most 0.0055.
Values may be sent and summed in bfloat16 or wider, within the bound.
No kernel may reach another device: no remote copies, remote signals or barrier semaphores. Data moves between devices by JAX's collectives and lax.ppermute only.
A program may use at most 128 MiB of HBM per device.

v0:
```python
import math

import jax
import jax.numpy as jnp
from jax import lax
from jax.sharding import PartitionSpec as P

K = 8
H = 64
BLK = 128
CAP = 2
OWN = 32
USERS = 4
UTAB = 128
E = 512


def from_behind(x, axis, by):
    peers = lax.axis_size(axis)
    return lax.ppermute(x, axis, [(i, (i + by) % peers) for i in range(peers)])


def pair_terms(user_rows, item_rows, targets, gate_in, gate_in_bias, gate_out, gate_out_bias):
    count_users = user_rows.shape[0]
    count_items = item_rows.shape[0]
    scaling = 1.0 / math.sqrt(H)
    user_parts = user_rows.reshape(count_users * K, H)
    item_parts = item_rows.reshape(count_items, K, H)
    logits = (
        jnp.einsum("xh,ibh->xbi", user_parts, item_parts, preferred_element_type=jnp.float32)
        * scaling
    )
    logits = logits.reshape(count_users, K * K, count_items)
    gate_input = logits.astype(jnp.bfloat16)
    hidden_pre = jnp.einsum("pg,upi->ugi", gate_in, gate_input, preferred_element_type=jnp.float32)
    hidden_pre = hidden_pre + gate_in_bias.astype(jnp.float32)[None, :, None]
    hidden = jax.nn.silu(hidden_pre).astype(jnp.bfloat16)
    gate_logit = jnp.einsum("gp,ugi->upi", gate_out, hidden, preferred_element_type=jnp.float32)
    gate_logit = gate_logit + gate_out_bias.astype(jnp.float32)[None, :, None]
    exp_terms = jnp.exp(gate_logit)
    mixture = exp_terms / jnp.sum(exp_terms, axis=1, keepdims=True)
    scores = jnp.sum(mixture * logits, axis=1)
    score_grad = jax.nn.sigmoid(scores) - targets
    weighted = score_grad[:, None, :] * mixture
    logit_grad = (weighted * (logits - scores[:, None, :])).astype(jnp.bfloat16)
    gate_sig = jax.nn.sigmoid(hidden_pre)
    hidden_grad = jnp.einsum(
        "gp,upi->ugi", gate_out, logit_grad, preferred_element_type=jnp.float32
    )
    hidden_grad = (hidden_grad * gate_sig * (1.0 + hidden_pre * (1.0 - gate_sig))).astype(
        jnp.bfloat16
    )
    pair_grad = weighted + jnp.einsum(
        "pg,ugi->upi", gate_in, hidden_grad, preferred_element_type=jnp.float32
    )
    pair_grad = pair_grad.astype(jnp.bfloat16).reshape(count_users * K, K, count_items)
    user_delta = jnp.einsum(
        "xbi,ibh->xh", pair_grad, item_parts, preferred_element_type=jnp.float32
    )
    item_delta = jnp.einsum(
        "xbi,xh->ibh", pair_grad, user_parts, preferred_element_type=jnp.float32
    )
    return (
        user_delta.reshape(count_users, K * H) * scaling,
        item_delta.reshape(count_items, K * H) * scaling,
    )


def match_targets(positives, first_column, count):
    columns = first_column + jnp.arange(count, dtype=jnp.int32)
    return jnp.any(positives[:, :, None] == columns[None, None, :], axis=1).astype(jnp.float32)


def split_product(left_bf16, right_f32):
    upper = right_f32.astype(jnp.bfloat16)
    lower = (right_f32 - upper.astype(jnp.float32)).astype(jnp.bfloat16)
    dims = (((0,), (0,)), ((), ()))
    first = lax.dot_general(left_bf16, upper, dims, preferred_element_type=jnp.float32)
    second = lax.dot_general(left_bf16, lower, dims, preferred_element_type=jnp.float32)
    return first + second


def shards(
    item_features,
    tower_weight,
    gate_in,
    gate_in_bias,
    gate_out,
    gate_out_bias,
    user_table,
    user_ids,
    positive_item,
    listed_owner,
    listed_slot,
):
    block_groups = lax.axis_size("blk")
    owner_count = lax.axis_size("shard")
    group_index = lax.axis_index("blk")
    listings = listed_slot.shape[0]
    circle_part = listings * BLK
    owner_ids = listed_owner[:, 0]
    listing_order = jnp.arange(listings, dtype=jnp.int32)
    same_owner = owner_ids[:, None] == owner_ids[None, :]
    earlier = listing_order[None, :] < listing_order[:, None]
    rank_within = jnp.sum(jnp.logical_and(same_owner, earlier), axis=1)
    owner_match = owner_ids[:, None] == jnp.arange(owner_count, dtype=jnp.int32)[None, :]
    rank_match = rank_within[:, None] == jnp.arange(CAP, dtype=jnp.int32)[None, :]
    placement = jnp.logical_and(owner_match[:, :, None], rank_match[:, None, :])
    wanted = jnp.sum(jnp.where(placement, listed_slot[:, None, None] + 1, 0), axis=0) - 1
    asked_slots = lax.all_to_all(wanted, "shard", split_axis=0, concat_axis=0, tiled=True)
    slot_pick = jnp.clip(asked_slots, 0, OWN - 1).reshape(-1)
    slot_of = owner_ids * CAP + rank_within
    own_vectors = jnp.dot(item_features, tower_weight, preferred_element_type=jnp.float32).astype(
        jnp.bfloat16
    )
    own_vectors = own_vectors.reshape(OWN, BLK, E)
    outgoing = jnp.take(own_vectors, slot_pick, axis=0).reshape(owner_count, CAP, BLK, E)
    arrived = lax.all_to_all(outgoing, "shard", split_axis=0, concat_axis=0, tiled=True).reshape(
        owner_count * CAP, BLK, E
    )
    listed = jnp.take(arrived, slot_of, axis=0).reshape(circle_part, E)
    row_match = user_ids[:, None] == jnp.arange(UTAB, dtype=jnp.int32)[None, :]
    user_rows = jnp.dot(
        row_match.astype(jnp.bfloat16), user_table, preferred_element_type=jnp.float32
    ).astype(jnp.bfloat16)
    moving = listed
    accumulator = jnp.zeros((circle_part, E), jnp.float32)
    user_delta = jnp.zeros((USERS, E), jnp.float32)
    for rotation in range(block_groups):
        anchor = jnp.mod(group_index - rotation, block_groups)
        targets = match_targets(positive_item, anchor * circle_part, circle_part)
        user_term, item_term = pair_terms(
            user_rows, moving, targets, gate_in, gate_in_bias, gate_out, gate_out_bias
        )
        user_delta = user_delta + user_term
        accumulator = from_behind(accumulator + item_term, "blk", 1)
        if rotation + 1 < block_groups:
            moving = from_behind(moving, "blk", 1)
    listing_grads = accumulator.astype(jnp.bfloat16)
    returning = jnp.zeros((owner_count * CAP, BLK, E), jnp.bfloat16)
    returning = returning.at[slot_of].set(listing_grads.reshape(listings, BLK, E))
    returned = lax.all_to_all(
        returning.reshape(owner_count, CAP, BLK, E),
        "shard",
        split_axis=0,
        concat_axis=0,
        tiled=True,
    )
    returned = returned.reshape(owner_count * CAP, BLK * E)
    slot_hot = (
        asked_slots.reshape(-1)[None, :] == jnp.arange(OWN, dtype=jnp.int32)[:, None]
    ).astype(jnp.bfloat16)
    summed = jnp.dot(slot_hot, returned, preferred_element_type=jnp.float32).reshape(OWN * BLK, E)
    partial_value = split_product(item_features, summed)
    tower_part = lax.psum_scatter(partial_value, "shard", scatter_dimension=0, tiled=True)
    tower_gradient = lax.psum(tower_part, "blk")
    user_gradient = split_product(row_match.astype(jnp.bfloat16), user_delta)
    return (tower_gradient, user_gradient)


def solution(mesh):
    return jax.shard_map(
        shards,
        mesh=mesh,
        in_specs=(
            P("shard", None),
            P(),
            P(),
            P(),
            P(),
            P(),
            P(("blk", "shard"), None),
            P(("blk", "shard")),
            P(("blk", "shard"), None),
            P(("blk", "shard"), None),
            P(("blk", "shard")),
        ),
        out_specs=(P("shard", None), P(("blk", "shard"), None)),
        check_vma=False,
    )
```

profile of v0, /device:TPU:1, one launch (start us, length us, event | category | flops | bytes accessed | tf_op | source)
XLA Modules:
  0.0 868.9 jit_solution(14057466203700951652)
XLA Ops:
  10.4 11.3 %all-to-all-start = ((s32[32,1,2]{2,1,0:T(1,128)}), s32[32,1,2]{2,1,0:T(1,128)S(1)}, u32[]{:S(2)}, u32[]{:S(2)}) async-start(s32[32,1,2]{2,1,0:T(1,128)} %copy.99), calls=%async_computation | async-start | bytes 32768 | tf_op jit(solution)/shard_map/all_to_all | solution.py:110
  21.8 9.5 %convolution_convert_fusion = bf16[4096,512]{1,0:T(8,128)(2,1)} fusion(bf16[4096,1024]{1,0:T(8,128)(2,1)} %param.11, bf16[1024,512]{1,0:T(8,128)(2,1)S(1)} %copy-done), kind=kOutput, calls=%fused_computation.9 | convolution fusion | flops 4297064448 | bytes 13631488 | tf_op jit(solution)/shard_map/dot_general | solution.py:113
  32.8 7.5 gather_fusion
  40.3 7.5 broadcast_select_fusion
  47.8 9.5 %all-to-all-start.1 = ((bf16[32,2,128,512]{3,2,1,0:T(8,128)(2,1)}), bf16[32,2,128,512]{3,2,1,0:T(8,128)(2,1)}, u32[]{:S(2)}, u32[]{:S(2)}) async-start(bf16[32,2,128,512]{3,2,1,0:T(8,128)(2,1)} %broadcast_select_fusion), calls=%async_computation.1 | async-start | bytes 16777216 | tf_op jit(solution)/shard_map/all_to_all | solution.py:118
  58.4 108.5 %all-to-all-done.1 = bf16[32,2,128,512]{3,2,1,0:T(8,128)(2,1)} async-done(((bf16[32,2,128,512]{3,2,1,0:T(8,128)(2,1)}), bf16[32,2,128,512]{3,2,1,0:T(8,128)(2,1)}, u32[]{:S(2)}, u32[]{:S(2)}) %all-to-all-start.1) | async-done | bytes 8388640 | tf_op jit(solution)/shard_map/all_to_all | solution.py:118
  174.4 13.1 %collective-permute-start.1 = (bf16[1792,512]{1,0:T(8,128)(2,1)}, bf16[1792,512]{1,0:T(8,128)(2,1)}, u32[]{:S(2)}, u32[]{:S(2)}) collective-permute-start(bf16[1792,512]{1,0:T(8,128)(2,1)} %bitcast_select_fusion), channel_id=1, source_target_pairs={{0,32},{32,64},{64,96},{96,0},{1,33},{33,65},{65,97},{97,1},{2,34}... | collective-permute-start | bytes 5505032 | tf_op jit(solution)/shard_map/ppermute | solution.py:20
  223.0 5.2 fusion.53
  233.2 5.1 copy.107
  241.0 5.2 fusion.54
  248.7 5.5 copy.113
  261.0 4.6 fusion.35
  270.0 40.2 %collective-permute-done.5 = bf16[1792,512]{1,0:T(8,128)(2,1)} collective-permute-done((bf16[1792,512]{1,0:T(8,128)(2,1)}, bf16[1792,512]{1,0:T(8,128)(2,1)}, u32[]{:S(2)}, u32[]{:S(2)}) %collective-permute-start.5) | collective-permute-done | bytes 1835040 | tf_op jit(solution)/shard_map/ppermute | solution.py:20
  316.7 4.8 add.308
  333.4 6.1 fusion.55
  343.2 5.1 copy.119
  348.3 15.8 %collective-permute-done.2 = f32[1792,512]{1,0:T(8,128)} collective-permute-done((f32[1792,512]{1,0:T(8,128)}, f32[1792,512]{1,0:T(8,128)}, u32[]{:S(2)}, u32[]{:S(2)}) %collective-permute-start.2) | collective-permute-done | bytes 3670048 | tf_op jit(solution)/shard_map/ppermute | solution.py:20
  364.2 5.9 add.319
  376.5 5.2 fusion.56
  384.2 5.1 copy.125
  389.4 23.4 %collective-permute-done.4 = f32[1792,512]{1,0:T(8,128)} collective-permute-done((f32[1792,512]{1,0:T(8,128)}, f32[1792,512]{1,0:T(8,128)}, u32[]{:S(2)}, u32[]{:S(2)}) %collective-permute-start.4) | collective-permute-done | bytes 3670048 | tf_op jit(solution)/shard_map/ppermute | solution.py:20
  419.3 20.2 %collective-permute-done.6 = bf16[1792,512]{1,0:T(8,128)(2,1)S(1)} collective-permute-done((bf16[1792,512]{1,0:T(8,128)(2,1)S(1)}, bf16[1792,512]{1,0:T(8,128)(2,1)S(1)}, u32[]{:S(2)}, u32[]{:S(2)}) %collective-permute-start.6) | collective-permute-done | bytes 1835040 | tf_op jit(solution)/shard_map/ppermute | solution.py:20
  443.7 5.1 scatter_fusion
  448.8 9.0 %all-to-all-start.2 = ((bf16[32,2,128,512]{3,2,1,0:T(8,128)(2,1)}), bf16[32,2,128,512]{3,2,1,0:T(8,128)(2,1)}, u32[]{:S(2)}, u32[]{:S(2)}) async-start(bf16[32,2,128,512]{3,2,1,0:T(8,128)(2,1)} %bitcast.404), calls=%async_computation.2 | async-start | bytes 16777216 | tf_op jit(solution)/shard_map/all_to_all | solution.py:142
  458.0 136.9 %all-to-all-done.2 = bf16[32,2,128,512]{3,2,1,0:T(8,128)(2,1)} async-done(((bf16[32,2,128,512]{3,2,1,0:T(8,128)(2,1)}), bf16[32,2,128,512]{3,2,1,0:T(8,128)(2,1)}, u32[]{:S(2)}, u32[]{:S(2)}) %all-to-all-start.2) | async-done | bytes 8388640 | tf_op jit(solution)/shard_map/all_to_all | solution.py:142
  594.9 11.7 %copy.142 = bf16[8,8,128,512]{3,1,2,0:T(8,128)(2,1)} copy(bf16[8,8,128,512]{3,2,1,0:T(8,128)(2,1)} %bitcast.67) | data formatting | bytes 16777216
  606.6 7.8 fusion.121
  614.4 7.5 reshape.288
  621.9 10.8 %fusion.4 = f32[512,1024]{1,0:T(8,128)S(1)} fusion(bf16[4096,1024]{1,0:T(8,128)(2,1)} %param.11, f32[4096,512]{1,0:T(8,128)} %reshape.288), kind=kOutput, calls=%fused_computation.10 | convolution fusion | flops 4303355904 | bytes 18874368 | tf_op jit(solution)/shard_map/dot_general | solution.py:79
  632.7 7.1 add_bitcast_fusion
  654.7 147.8 %reduce-scatter.4.cloned.1.call-done = f32[32,512]{1,0:T(8,128)} async-done(((f32[1024,512]{1,0:T(8,128)}), f32[32,512]{1,0:T(8,128)}) %reduce-scatter.4.cloned.1.call-update) | async-done | bytes 65552
  805.1 55.0 %all-reduce.2.cloned.1.call-done = f32[32,512]{0,1:T(8,128)} async-done(((f32[32,512]{0,1:T(8,128)}), f32[32,512]{0,1:T(8,128)}) %all-reduce.2.cloned.1.call-update) | async-done | bytes 65552 | tf_op jit(solution)/shard_map/psum | solution.py:156
  (171 shorter events, 130.9 us)
Async XLA Ops:
  7.2 14.6 %copy-start = (bf16[1024,512]{1,0:T(8,128)(2,1)S(1)}, bf16[1024,512]{1,0:T(8,128)(2,1)}, u32[]{:S(2)}) copy-start(bf16[1024,512]{1,0:T(8,128)(2,1)} %param.12) | copy-start | bytes 3145732
  10.4 20.8 %all-to-all-start = ((s32[32,1,2]{2,1,0:T(1,128)}), s32[32,1,2]{2,1,0:T(1,128)S(1)}, u32[]{:S(2)}, u32[]{:S(2)}) async-start(s32[32,1,2]{2,1,0:T(1,128)} %copy.99), calls=%async_computation | async-start | bytes 32768 | tf_op jit(solution)/shard_map/all_to_all | solution.py:110
  47.8 9.6 %copy-start.29 = (s32[4]{0:T(128)S(1)}, s32[4]{0:T(128)}, u32[]{:S(2)}) copy-start(s32[4]{0:T(128)} %param.18) | copy-start | bytes 52
  47.8 9.6 %copy-start.33 = (bf16[128,512]{1,0:T(8,128)(2,1)S(1)}, bf16[128,512]{1,0:T(8,128)(2,1)}, u32[]{:S(2)}) copy-start(bf16[128,512]{1,0:T(8,128)(2,1)} %param.17) | copy-start | bytes 393220
  47.8 9.9 %copy-start.35 = (bf16[128]{0:T(256)(128)(2,1)S(1)}, bf16[128]{0:T(256)(128)(2,1)}, u32[]{:S(2)}) copy-start(bf16[128]{0:T(256)(128)(2,1)} %param.14) | copy-start | bytes 772
  47.8 9.9 %copy-start.36 = (bf16[64]{0:T(256)(128)(2,1)S(1)}, bf16[64]{0:T(256)(128)(2,1)}, u32[]{:S(2)}) copy-start(bf16[64]{0:T(256)(128)(2,1)} %param.16) | copy-start | bytes 388
  47.8 9.9 %copy-start.32 = (s32[14,1]{0,1:T(1,128)S(1)}, s32[14,1]{0,1:T(1,128)}, u32[]{:S(2)}) copy-start(s32[14,1]{0,1:T(1,128)} %param.20) | copy-start | bytes 172
  47.8 10.0 %copy-start.31 = (s32[4,16]{1,0:T(4,128)S(1)}, s32[4,16]{1,0:T(4,128)}, u32[]{:S(2)}) copy-start(s32[4,16]{1,0:T(4,128)} %param.19) | copy-start | bytes 772
  47.8 119.1 %all-to-all-start.1 = ((bf16[32,2,128,512]{3,2,1,0:T(8,128)(2,1)}), bf16[32,2,128,512]{3,2,1,0:T(8,128)(2,1)}, u32[]{:S(2)}, u32[]{:S(2)}) async-start(bf16[32,2,128,512]{3,2,1,0:T(8,128)(2,1)} %broadcast_select_fusion), calls=%async_computation.1 | async-start | bytes 16777216 | tf_op jit(solution)/shard_map/all_to_all | solution.py:118
  58.4 114.4 %copy-start.27 = (pred[1792]{0:T(1024)(128)(4,1)}, pred[1792]{0:T(1024)(128)(4,1)S(1)}, u32[]{:S(2)}) copy-start(pred[1792]{0:T(1024)(128)(4,1)S(1)} %broadcast_bitcast_fusion) | copy-start | bytes 5380
  171.0 3.4 copy-start.7
  174.4 33.6 %collective-permute-start.1 = (bf16[1792,512]{1,0:T(8,128)(2,1)}, bf16[1792,512]{1,0:T(8,128)(2,1)}, u32[]{:S(2)}, u32[]{:S(2)}) collective-permute-start(bf16[1792,512]{1,0:T(8,128)(2,1)} %bitcast_select_fusion), channel_id=1, source_target_pairs={{0,32},{32,64},{64,96},{96,0},{1,33},{33,65},{65,97},{97,1},{2,34}... | collective-permute-start | bytes 5505032 | tf_op jit(solution)/shard_map/ppermute | solution.py:20
  196.1 4.1 copy-start.5
  217.1 2.6 copy-start.18
  228.1 5.0 copy-start.25
  228.2 26.1 %collective-permute-start.3 = (bf16[1792,512]{1,0:T(8,128)(2,1)}, bf16[1792,512]{1,0:T(8,128)(2,1)}, u32[]{:S(2)}, u32[]{:S(2)}) collective-permute-start(bf16[1792,512]{1,0:T(8,128)(2,1)} %collective-permute-done.1), channel_id=1, source_target_pairs={{0,32},{32,64},{64,96},{96,0},{1,33},{33,65},{65,97},{97,1},{2,34}... | collective-permute-start | bytes 5505032 | tf_op jit(solution)/shard_map/ppermute | solution.py:20
  238.3 77.4 %collective-permute-start = (f32[1792,512]{1,0:T(8,128)}, f32[1792,512]{1,0:T(8,128)}, u32[]{:S(2)}, u32[]{:S(2)}) collective-permute-start(f32[1792,512]{1,0:T(8,128)} %copy.107), channel_id=1, source_target_pairs={{0,32},{32,64},{64,96},{96,0},{1,33},{33,65},{65,97},{97,1},{2,34}... | collective-permute-start | bytes 11010056 | tf_op jit(solution)/shard_map/ppermute | solution.py:20
  259.8 5.8 copy-start.3
  259.8 50.4 %collective-permute-start.5 = (bf16[1792,512]{1,0:T(8,128)(2,1)}, bf16[1792,512]{1,0:T(8,128)(2,1)}, u32[]{:S(2)}, u32[]{:S(2)}) collective-permute-start(bf16[1792,512]{1,0:T(8,128)(2,1)} %collective-permute-done.3), channel_id=1, source_target_pairs={{0,32},{32,64},{64,96},{96,0},{1,33},{33,65},{65,97},{97,1},{2,34}... | collective-permute-start | bytes 5505032 | tf_op jit(solution)/shard_map/ppermute | solution.py:20
  321.4 42.8 %collective-permute-start.2 = (f32[1792,512]{1,0:T(8,128)}, f32[1792,512]{1,0:T(8,128)}, u32[]{:S(2)}, u32[]{:S(2)}) collective-permute-start(f32[1792,512]{1,0:T(8,128)} %add.308), channel_id=1, source_target_pairs={{0,32},{32,64},{64,96},{96,0},{1,33},{33,65},{65,97},{97,1},{2,34}... | collective-permute-start | bytes 11010056 | tf_op jit(solution)/shard_map/ppermute | solution.py:20
  329.6 2.6 copy-start.17
  348.3 24.3 %copy-start.23 = (bf16[4,64,1792]{2,1,0:T(8,128)(2,1)S(1)}, bf16[4,64,1792]{2,1,0:T(8,128)(2,1)}, u32[]{:S(2)}) copy-start(bf16[4,64,1792]{2,1,0:T(8,128)(2,1)} %bitcast_convert_fusion) | copy-start | bytes 2752516
  370.1 5.0 copy-start.16
  370.1 42.6 %collective-permute-start.4 = (f32[1792,512]{1,0:T(8,128)}, f32[1792,512]{1,0:T(8,128)}, u32[]{:S(2)}, u32[]{:S(2)}) collective-permute-start(f32[1792,512]{1,0:T(8,128)} %add.319), channel_id=1, source_target_pairs={{0,32},{32,64},{64,96},{96,0},{1,33},{33,65},{65,97},{97,1},{2,34}... | collective-permute-start | bytes 11010056 | tf_op jit(solution)/shard_map/ppermute | solution.py:20
  416.6 22.9 %collective-permute-start.6 = (bf16[1792,512]{1,0:T(8,128)(2,1)S(1)}, bf16[1792,512]{1,0:T(8,128)(2,1)S(1)}, u32[]{:S(2)}, u32[]{:S(2)}) collective-permute-start(bf16[1792,512]{1,0:T(8,128)(2,1)S(1)} %add.330), channel_id=1, source_target_pairs={{0,32},{32,64},{64,96},{96,0},{1,33},{33,65},{65,97},{97,1},{2,34}... | collective-permute-start | bytes 5505032 | tf_op jit(solution)/shard_map/ppermute | solution.py:20
  448.8 146.0 %all-to-all-start.2 = ((bf16[32,2,128,512]{3,2,1,0:T(8,128)(2,1)}), bf16[32,2,128,512]{3,2,1,0:T(8,128)(2,1)}, u32[]{:S(2)}, u32[]{:S(2)}) async-start(bf16[32,2,128,512]{3,2,1,0:T(8,128)(2,1)} %bitcast.404), calls=%async_computation.2 | async-start | bytes 16777216 | tf_op jit(solution)/shard_map/all_to_all | solution.py:142
  457.8 344.6 %reduce-scatter.4.cloned.1.call-start = ((), (), s32[]{:S(2)}) async-start(), calls=%async_computation.5 | async-start | bytes 2162688
  621.9 10.8 %copy-start.2 = (f32[4096,512]{1,0:T(8,128)S(1)}, f32[4096,512]{1,0:T(8,128)}, u32[]{:S(2)}) copy-start(f32[4096,512]{1,0:T(8,128)} %reshape.288) | copy-start | bytes 25165828
  641.7 218.4 %all-reduce.2.cloned.1.call-start = ((), (), s32[]{:S(2)}) async-start(), calls=%async_computation.4 | async-start | bytes 524288 | tf_op jit(solution)/shard_map/psum | solution.py:156
  646.2 3.2 copy-start.28
  649.4 2.6 copy-start.20
  652.9 208.9 %copy-start.1 = (bf16[1024,512]{1,0:T(8,128)(2,1)S(1)}, bf16[1024,512]{1,0:T(8,128)(2,1)}, u32[]{:S(2)}) copy-start(bf16[1024,512]{1,0:T(8,128)(2,1)} %param.12) | copy-start | bytes 3145732
  (17 other events, 27.4 us)
Sparse Core Ops, SparseCore 0:
  641.8 160.5 reduce-scatter.3
  805.1 54.9 all-reduce.1
where the time goes:
time: 878 us; the launch traced here: 869 us
  waiting for transfers between devices  551 us (63%)
  local copies, waits for them, and re-layouts  103 us (12%)
  matrix products  102 us (12%)
  starting transfers between devices  53.8 us (6%)
  other arithmetic  43.6 us (5%)
  between operations  15 us (2%)
    unnamed x3, waiting for transfers between devices  148 us
    all_to_all x1, waiting for transfers between devices, shards(): lax.all_to_all(returning.reshape(owner_count, CAP, BLK, E), 'shard', spli...  137 us
    all_to_all x1, waiting for transfers between devices, shards(): lax.all_to_all(outgoing, 'shard', split_axis=0, concat_axis=0, tiled=True)  109 us
    ppermute x7, waiting for transfers between devices, from_behind(): return lax.ppermute(x, axis, [(i, (i + by) % peers) for i in range(peers)])  103 us
    psum x1, waiting for transfers between devices, shards(): tower_gradient = lax.psum(tower_part, 'blk')  55 us
    unnamed x78, local copies, waits for them, and re-layouts  27 us
    ppermute x7, starting transfers between devices, from_behind(): return lax.ppermute(x, axis, [(i, (i + by) % peers) for i in range(peers)])  23.6 us
    dot_general x4, matrix products, pair_terms(): jnp.einsum('pg,ugi->upi', gate_in, hidden_grad, preferred_element_type=jn...  21.7 us
  transfers between devices with their start and end apart: 12, of which 9 were waited for; matrix products, arithmetic and copies ran while one was open for 14% of the time, Pallas kernels for 0%

commit v1 on v0

v1 whole, which is shorter than its diff:
```python
import math

import jax
import jax.numpy as jnp
from jax import lax
from jax.experimental import pallas as pl
from jax.experimental.pallas import tpu as pltpu
from jax.sharding import PartitionSpec as P

K = 8
H = 64
BLK = 128
CAP = 2
OWN = 32
USERS = 4
UTAB = 128
E = 512
GROUPS = 4
CIRCLE_USERS = GROUPS * USERS
ROWS = CIRCLE_USERS * K
PAIRS = K * K
F32 = jnp.float32
BF = jnp.bfloat16
VMEM_SPEC = pl.BlockSpec(memory_space=pltpu.VMEM)


def shifted(x, by):
    return lax.ppermute(x, "blk", [(i, (i + by) % GROUPS) for i in range(GROUPS)])


def tower_kernel(weight_t, features, out):
    product = lax.dot_general(
        weight_t[...], features[...], (((1,), (1,)), ((), ())), preferred_element_type=F32
    ).astype(BF)
    for c in range(2):
        for b in range(K):
            out[c, :, b * BLK : (b + 1) * BLK] = product[
                b * H : (b + 1) * H, c * BLK : (c + 1) * BLK
            ]


def tower_vectors(features, weight_t):
    width = features.shape[1]
    return pl.pallas_call(
        tower_kernel,
        grid=(OWN // 2,),
        in_specs=[
            pl.BlockSpec((E, width), lambda i: (0, 0)),
            pl.BlockSpec((2 * BLK, width), lambda i: (i, 0)),
        ],
        out_specs=pl.BlockSpec((2, H, K * BLK), lambda i: (i, 0, 0)),
        out_shape=jax.ShapeDtypeStruct((OWN, H, K * BLK), BF),
        compiler_params=pltpu.CompilerParams(vmem_limit_bytes=32 << 20),
        cost_estimate=pl.CostEstimate(
            flops=2 * OWN * BLK * E * width, bytes_accessed=13 << 20, transcendentals=0
        ),
        name="tower",
    )(weight_t, features)


def pair_kernel(codes, arrived, vt, first_half, first, second_t, second_half, bias1, bias2,
                user_out, grad_out, logits, pair_grad, grads, deltas):
    grads[...] = jnp.zeros_like(grads)
    deltas[...] = jnp.zeros_like(deltas)
    lane = lax.broadcasted_iota(jnp.int32, (16, BLK), 1).astype(F32)
    n = CIRCLE_USERS

    def step(position, carry):
        shard = position // CAP
        rank = position % CAP
        slot = codes[shard, rank]

        @pl.when(slot >= 0)
        def _():
            start = codes[shard, CAP + rank].astype(F32) * BLK
            packed = arrived[shard, 0 : ROWS // 2, :]
            users = jnp.concatenate([packed[:, :H], packed[:, H:]], axis=0)
            items = vt[slot]
            logits[...] = jnp.dot(users, items, preferred_element_type=F32)
            meta = arrived[shard, ROWS // 2 : ROWS // 2 + 16, :].astype(F32)
            offset = meta[:, 0:16] * BLK + meta[:, 16:32] - start
            lk = jnp.concatenate(
                [
                    jnp.concatenate(
                        [
                            logits[u * K : (u + 1) * K, b * BLK : (b + 1) * BLK]
                            for b in range(K)
                        ],
                        axis=0,
                    )
                    for u in range(n)
                ],
                axis=1,
            )
            y = jnp.concatenate(
                [
                    jnp.max(
                        jnp.where(offset[:, u : u + 1] == lane, 1.0, 0.0), axis=0, keepdims=True
                    )
                    for u in range(n)
                ],
                axis=1,
            )
            h = jnp.dot(first_half[...], lk.astype(BF), preferred_element_type=F32)
            h = h + jnp.concatenate([bias1[...]] * n, axis=1)
            t = jnp.tanh(h)
            q = 1.0 + t
            silu = h * q
            slope = q + silu * (1.0 - t)
            gate = jnp.dot(second_t[...], silu.astype(BF), preferred_element_type=F32)
            e = jnp.exp(gate + jnp.concatenate([bias2[...]] * n, axis=1))
            inverse = 1.0 / jnp.sum(e, axis=0, keepdims=True)
            score = jnp.sum(e * lk, axis=0, keepdims=True) * inverse
            score_grad = 0.5 + 0.5 * jnp.tanh(0.5 * score) - y
            weighted = e * (score_grad * inverse)
            logit_grad = (weighted * (lk - score)).astype(BF)
            hidden_grad = jnp.dot(second_half[...], logit_grad, preferred_element_type=F32)
            hidden_grad = (hidden_grad * slope).astype(BF)
            pg = jnp.dot(first[...], hidden_grad, preferred_element_type=F32) + weighted
            for b in range(K):
                pair_grad[:, b * BLK : (b + 1) * BLK] = jnp.concatenate(
                    [pg[b * K : (b + 1) * K, u * BLK : (u + 1) * BLK] for u in range(n)], axis=0
                ).astype(BF)
            pgv = pair_grad[...]
            deltas[shard] += lax.dot_general(
                pgv, items, (((1,), (1,)), ((), ())), preferred_element_type=F32
            )
            grads[slot] += jnp.dot(users.T, pgv, preferred_element_type=F32)

        return carry

    lax.fori_loop(0, codes.shape[0] * CAP, step, 0)
    scaling = 1.0 / math.sqrt(H)
    user_out[:, :, :H] = (deltas[:, : ROWS // 2, :] * scaling).astype(BF)
    user_out[:, :, H:] = (deltas[:, ROWS // 2 :, :] * scaling).astype(BF)
    grad_out[...] = grads[...].astype(BF)


def pair_terms(codes, arrived, vt, gates):
    owners = codes.shape[0]
    return pl.pallas_call(
        pair_kernel,
        out_shape=(
            jax.ShapeDtypeStruct((owners, ROWS // 2, 2 * H), BF),
            jax.ShapeDtypeStruct((OWN, H, K * BLK), BF),
        ),
        in_specs=[pl.BlockSpec(memory_space=pltpu.SMEM)] + [VMEM_SPEC] * 8,
        out_specs=(VMEM_SPEC, VMEM_SPEC),
        scratch_shapes=[
            pltpu.VMEM((ROWS, K * BLK), F32),
            pltpu.VMEM((ROWS, K * BLK), BF),
            pltpu.VMEM((OWN, H, K * BLK), F32),
            pltpu.VMEM((owners, ROWS, H), F32),
        ],
        compiler_params=pltpu.CompilerParams(vmem_limit_bytes=56 << 20),
        cost_estimate=pl.CostEstimate(
            flops=40 << 30, bytes_accessed=12 << 20, transcendentals=1 << 24
        ),
        name="pairs",
    )(codes, arrived, vt, *gates)


def tower_gradient_kernel(grads, features, out, total):
    step = pl.program_id(0)

    @pl.when(step == 0)
    def _():
        total[...] = jnp.zeros_like(total)

    left = jnp.concatenate(
        [
            jnp.concatenate([grads[c, :, b * BLK : (b + 1) * BLK] for b in range(K)], axis=0)
            for c in range(grads.shape[0])
        ],
        axis=1,
    )
    total[...] += jnp.dot(left, features[...], preferred_element_type=F32)

    @pl.when(step == pl.num_programs(0) - 1)
    def _():
        out[...] = total[...].T.astype(BF)


def tower_gradient_terms(grads, features):
    width = features.shape[1]
    blocks = 4
    return pl.pallas_call(
        tower_gradient_kernel,
        grid=(OWN // blocks,),
        in_specs=[
            pl.BlockSpec((blocks, H, K * BLK), lambda i: (i, 0, 0)),
            pl.BlockSpec((blocks * BLK, width), lambda i: (i, 0)),
        ],
        out_specs=pl.BlockSpec((width, E), lambda i: (0, 0)),
        out_shape=jax.ShapeDtypeStruct((width, E), BF),
        scratch_shapes=[pltpu.VMEM((E, width), F32)],
        compiler_params=pltpu.CompilerParams(vmem_limit_bytes=40 << 20),
        cost_estimate=pl.CostEstimate(
            flops=2 * OWN * BLK * E * width, bytes_accessed=13 << 20, transcendentals=0
        ),
        name="tower_gradient",
    )(grads, features)


def gate_layers(gate_in, gate_in_bias, gate_out, gate_out_bias):
    hidden = gate_in.shape[1]
    first = gate_in.reshape(K, K, hidden).transpose(1, 0, 2).reshape(PAIRS, hidden)
    second = gate_out.reshape(hidden, K, K).transpose(0, 2, 1).reshape(hidden, PAIRS)
    bias2 = gate_out_bias.reshape(K, K).T.reshape(PAIRS)
    half = jnp.asarray(0.5, BF)
    return (
        first.T * half,
        first,
        second.T,
        second * half,
        jnp.broadcast_to(gate_in_bias.astype(F32)[:, None] * 0.5, (hidden, BLK)),
        jnp.broadcast_to(bias2.astype(F32)[:, None], (PAIRS, BLK)),
    )


def split_product(left_bf16, right_f32):
    upper = right_f32.astype(BF)
    lower = (right_f32 - upper.astype(F32)).astype(BF)
    dims = (((0,), (0,)), ((), ()))
    first = lax.dot_general(left_bf16, upper, dims, preferred_element_type=F32)
    second = lax.dot_general(left_bf16, lower, dims, preferred_element_type=F32)
    return first + second


def shards(
    item_features,
    tower_weight,
    gate_in,
    gate_in_bias,
    gate_out,
    gate_out_bias,
    user_table,
    user_ids,
    positive_item,
    listed_owner,
    listed_slot,
):
    owner_count = lax.axis_size("shard")
    group = lax.axis_index("blk")
    listings = listed_slot.shape[0]
    owner_ids = listed_owner[:, 0]
    order = jnp.arange(listings, dtype=jnp.int32)
    same_owner = owner_ids[:, None] == owner_ids[None, :]
    earlier = order[None, :] < order[:, None]
    rank_within = jnp.sum(jnp.logical_and(same_owner, earlier), axis=1)
    owner_match = owner_ids[:, None] == jnp.arange(owner_count, dtype=jnp.int32)[None, :]
    rank_match = rank_within[:, None] == jnp.arange(CAP, dtype=jnp.int32)[None, :]
    placement = jnp.logical_and(owner_match[:, :, None], rank_match[:, None, :])
    wanted = jnp.sum(jnp.where(placement, listed_slot[:, None, None] + 1, 0), axis=0) - 1
    place = group * listings + order
    wanted_place = jnp.sum(jnp.where(placement, place[:, None, None], 0), axis=0)
    codes = jnp.concatenate([wanted, wanted_place], axis=1).astype(BF)

    row_match = user_ids[:, None] == jnp.arange(UTAB, dtype=jnp.int32)[None, :]
    user_rows = jnp.dot(row_match.astype(BF), user_table, preferred_element_type=F32)
    user_rows = (user_rows * (1.0 / math.sqrt(H))).astype(BF).reshape(USERS * K, H)
    positives = positive_item.T
    marks = jnp.concatenate([positives // BLK, positives % BLK], axis=1).astype(BF)
    own = jnp.concatenate([user_rows, jnp.pad(marks, ((0, 0), (0, H - 2 * USERS)))], axis=0)
    pieces = [own] + [shifted(own, by) for by in range(1, GROUPS)]
    rows = [piece[: USERS * K] for piece in pieces]
    marks = [piece[USERS * K :] for piece in pieces]
    packed = jnp.concatenate(
        [jnp.concatenate(rows[0:2], axis=0), jnp.concatenate(rows[2:4], axis=0)], axis=1
    )
    meta = jnp.concatenate(
        [m[:, :USERS] for m in marks] + [m[:, USERS : 2 * USERS] for m in marks], axis=1
    )
    meta = jnp.pad(meta, ((0, 0), (0, 2 * H - 2 * CIRCLE_USERS)))
    common = jnp.concatenate([packed, meta], axis=0)
    sent = jnp.broadcast_to(common[None], (owner_count,) + common.shape)
    codes = jnp.pad(
        codes[:, None, :],
        ((0, 0), (ROWS // 2, 15), (2 * CIRCLE_USERS, 2 * H - 2 * CIRCLE_USERS - 2 * CAP)),
    )
    arrived = lax.all_to_all(sent + codes, "shard", split_axis=0, concat_axis=0, tiled=True)
    asked = arrived[:, ROWS // 2, 2 * CIRCLE_USERS : 2 * CIRCLE_USERS + 2 * CAP].astype(jnp.int32)

    vt = tower_vectors(item_features, tower_weight.T)
    gates = gate_layers(gate_in, gate_in_bias, gate_out, gate_out_bias)
    user_terms, grads = pair_terms(asked, arrived, vt, gates)

    user_terms = lax.all_to_all(user_terms, "shard", split_axis=0, concat_axis=0, tiled=True)
    user_sum = jnp.sum(user_terms.astype(F32), axis=0)
    half_rows = ROWS // 4
    quarters = [
        user_sum[half_rows * (q % 2) : half_rows * (q % 2 + 1), H * (q // 2) : H * (q // 2 + 1)]
        for q in range(GROUPS)
    ]
    user_delta = quarters[0]
    for q in range(1, GROUPS):
        user_delta = user_delta + shifted(quarters[q], -q)
    user_delta = user_delta.reshape(USERS, E)
    user_gradient = split_product(row_match.astype(BF), user_delta)

    partial_value = tower_gradient_terms(grads, item_features)
    width = partial_value.shape[0]
    partial_value = lax.all_to_all(
        partial_value.reshape(owner_count, width // owner_count, E),
        "shard",
        split_axis=0,
        concat_axis=0,
        tiled=True,
    )
    tower_part = jnp.sum(partial_value.astype(F32), axis=0)
    others = [shifted(tower_part, by) for by in range(1, GROUPS)]
    by_group = [tower_part] + others
    tower_gradient = (by_group[0] + by_group[2]) + (by_group[1] + by_group[3])
    return (tower_gradient, user_gradient)


def solution(mesh):
    return jax.shard_map(
        shards,
        mesh=mesh,
        in_specs=(
            P("shard", None),
            P(),
            P(),
            P(),
            P(),
            P(),
            P(("blk", "shard"), None),
            P(("blk", "shard")),
            P(("blk", "shard"), None),
            P(("blk", "shard"), None),
            P(("blk", "shard")),
        ),
        out_specs=(P("shard", None), P(("blk", "shard"), None)),
        check_vma=False,
    )
```

time: 878 us -> 189 us (0.22)
  waiting for transfers between devices: 551 us -> 15.9 us
  matrix products: 102 us -> 2.13 us
  local copies, waits for them, and re-layouts: 103 us -> 15.5 us
  Pallas kernels: 0 us -> 65.5 us
  other arithmetic: 43.6 us -> 7.48 us
  starting transfers between devices: 53.8 us -> 80.2 us
  between operations: 15 us -> 0.88 us
    all_to_all x3, waiting for transfers between devices: 245 us -> 3.18 us  [the longest x1 3.17 us: shards(): lax.all_to_all(partial_value.reshape(owner_count, width // owner_count, E...]
    unnamed x3 -> x0, waiting for transfers between devices: 148 us -> none
    ppermute x7 -> x9, waiting for transfers between devices: 103 us -> 12.8 us  [shifted(): lax.ppermute(x, 'blk', [(i, (i + by) % GROUPS) for i in range(GROUPS)])]
    dot_general x27 -> x3, matrix products: 86.7 us -> 2.13 us  [the longest x1 1 us: split_product(): first = lax.dot_general(left_bf16, upper, dims, preferred_element_type=F32)]
    pallas_call x0 -> x3, Pallas kernels: none -> 65.5 us  [the longest x1 50.5 us: pair_terms(): pl.pallas_call(pair_kernel, out_shape=(jax.ShapeDtypeStruct((owners, ROWS...]
    psum x1 -> x0, waiting for transfers between devices: 55 us -> none  [shards(): tower_gradient = lax.psum(tower_part, 'blk')]
    all_to_all x3, starting transfers between devices: 29.9 us -> 70.1 us  [the longest x1 50.5 us: shards(): lax.all_to_all(user_terms, 'shard', split_axis=0, concat_axis=0, tiled=True)]
    mul x8 -> x1, local copies, waits for them, and re-layouts: 25.2 us -> 0.72 us  [gate_layers(): first.T * half]
  transfers between devices with their start and end apart: 12 -> 12, of which waited for: 9 -> 3; matrix products, arithmetic and copies ran while one was open for 14% -> 4% of each run, Pallas kernels for 0% -> 8%
where the time goes in v1:
time: 189 us; the launch traced here: 188 us
  starting transfers between devices  80.2 us (42%)
  Pallas kernels  65.5 us (35%)
  waiting for transfers between devices  15.9 us (8%)
  local copies, waits for them, and re-layouts  15.5 us (8%)
  other arithmetic  7.48 us (4%)
  matrix products  2.13 us (1%)
    pallas_call x1, Pallas kernels, pair_terms(): pl.pallas_call(pair_kernel, out_shape=(jax.ShapeDtypeStruct((owners, ROWS...  50.5 us
    all_to_all x1, starting transfers between devices, shards(): lax.all_to_all(user_terms, 'shard', split_axis=0, concat_axis=0, tiled=True)  50.5 us
    ppermute x9, waiting for transfers between devices, shifted(): lax.ppermute(x, 'blk', [(i, (i + by) % GROUPS) for i in range(GROUPS)])  12.8 us
    unnamed x27, local copies, waits for them, and re-layouts  11.5 us
    all_to_all x1, starting transfers between devices, shards(): lax.all_to_all(sent + codes, 'shard', split_axis=0, concat_axis=0, tiled=...  10.2 us
    ppermute x9, starting transfers between devices, shifted(): lax.ppermute(x, 'blk', [(i, (i + by) % GROUPS) for i in range(GROUPS)])  10.1 us
    all_to_all x1, starting transfers between devices, shards(): lax.all_to_all(partial_value.reshape(owner_count, width // owner_count, E...  9.4 us
    pallas_call x1, Pallas kernels, tower_vectors(): pl.pallas_call(tower_kernel, grid=(OWN // 2,), in_specs=[pl.BlockSpec((E,...  7.75 us
  transfers between devices with their start and end apart: 12, of which 3 were waited for; matrix products, arithmetic and copies ran while one was open for 4% of the time, Pallas kernels for 8%

profile of v1, /device:TPU:1, one launch (start us, length us, event | category | flops | bytes accessed | tf_op | source)
XLA Modules:
  0.0 187.6 jit_solution(4076536893278747955)
XLA Ops:
  0.7 0.8 fusion.13
  1.6 0.8 fusion
  2.7 1.4 collective-permute-start.2
  4.1 1.3 collective-permute-start.1
  5.4 1.3 collective-permute-start
  6.8 0.9 convert_reduce_fusion.2
  7.7 0.7 iota_compare_fusion.4
  8.4 0.7 broadcast_add_fusion
  9.1 0.7 multiply_bitcast_fusion
  10.7 1.0 pad_add_fusion
  11.6 10.2 %all-to-all-start = ((bf16[32,80,128]{2,1,0:T(8,128)(2,1)}), bf16[32,80,128]{2,1,0:T(8,128)(2,1)S(1)}, u32[]{:S(2)}, u32[]{:S(2)}) async-start(bf16[32,80,128]{2,1,0:T(8,128)(2,1)} %pad_add_fusion), calls=%async_computation | async-start | bytes 1310720 | tf_op jit(solution)/shard_map/all_to_all | solution.py:281
  22.8 0.7 copy.87.first_half
  24.8 3.4 %copy-done.1 = bf16[4096,1024]{1,0:T(8,128)(2,1)S(1)} copy-done((bf16[4096,1024]{1,0:T(8,128)(2,1)S(1)}, bf16[4096,1024]{1,0:T(8,128)(2,1)}, u32[]{:S(2)}) %copy-start.1) | copy-done | bytes 8388632
  28.1 7.7 %tower.1.vt = bf16[32,64,1024]{2,1,0:T(8,128)(2,1)S(1)} custom-call(bf16[512,1024]{1,0:T(8,128)(2,1)S(1)} %bitcast.54, bf16[4096,1024]{1,0:T(8,128)(2,1)S(1)} %copy-done.1), custom_call_target="tpu_custom_call" | custom-call | flops 4294967296 | bytes 13631488 | tf_op jit(solution)/shard_map/tower/pallas_call | solution.py:44
  35.9 1.9 %copy-done.3 = bf16[32,64,1024]{2,1,0:T(8,128)(2,1)} copy-done((bf16[32,64,1024]{2,1,0:T(8,128)(2,1)}, bf16[32,64,1024]{2,1,0:T(8,128)(2,1)S(1)}, u32[]{:S(2)}) %copy-start.3) | copy-done | bytes 4194328
  37.9 0.8 slice_convert_fusion
  38.7 0.7 broadcast_in_dim.29.bias2
  39.3 0.7 broadcast_in_dim.28.bias1
  40.1 50.5 %pairs.1 = (bf16[32,64,128]{2,1,0:T(8,128)(2,1)}, bf16[32,64,1024]{2,1,0:T(8,128)(2,1)}) custom-call(s32[32,4]{1,0:T(8,128)} %bitcast.64, bf16[32,80,128]{2,1,0:T(8,128)(2,1)} %copy-done.6, bf16[32,64,1024]{2,1,0:T(8,128)(2,1)} %copy-done.3, bf16[128,64]{1,0:T(8,128)(2,1)} %copy.87.first_half, bf16[64,128]{1,0:T(8,128)(2,1)} %bitcast.63, ...), custom_call_target="tpu_custom_call" | custom-call | flops 42949672960 | bytes 12582912 | tf_op jit(solution)/shard_map/pairs/pallas_call | solution.py:141
  90.6 50.5 %all-to-all-start.2 = ((bf16[32,64,128]{2,1,0:T(8,128)(2,1)}), bf16[32,64,128]{2,1,0:T(8,128)(2,1)S(1)}, u32[]{:S(2)}, u32[]{:S(2)}) async-start(bf16[32,64,128]{2,1,0:T(8,128)(2,1)} %get-tuple-element.5), calls=%async_computation.2 | async-start | bytes 1048576 | tf_op jit(solution)/shard_map/all_to_all | solution.py:288
  141.1 3.4 %copy-done.2 = bf16[4096,1024]{1,0:T(8,128)(2,1)S(1)} copy-done((bf16[4096,1024]{1,0:T(8,128)(2,1)S(1)}, bf16[4096,1024]{1,0:T(8,128)(2,1)}, u32[]{:S(2)}) %copy-start.2) | copy-done | bytes 8388632
  144.5 2.2 %copy-done.4 = bf16[32,64,1024]{2,1,0:T(8,128)(2,1)S(1)} copy-done((bf16[32,64,1024]{2,1,0:T(8,128)(2,1)S(1)}, bf16[32,64,1024]{2,1,0:T(8,128)(2,1)}, u32[]{:S(2)}) %copy-start.4) | copy-done | bytes 4194328
  146.6 7.3 %tower_gradient.1 = bf16[1024,512]{1,0:T(8,128)(2,1)} custom-call(bf16[32,64,1024]{2,1,0:T(8,128)(2,1)S(1)} %copy-done.4, bf16[4096,1024]{1,0:T(8,128)(2,1)S(1)} %copy-done.2), custom_call_target="tpu_custom_call" | custom-call | flops 4294967296 | bytes 13631488 | tf_op jit(solution)/shard_map/tower_gradient/pallas_call | solution.py:187
  153.9 9.4 %all-to-all-start.1 = ((bf16[32,32,512]{2,1,0:T(8,128)(2,1)}), bf16[32,32,512]{2,1,0:T(8,128)(2,1)S(1)}, u32[]{:S(2)}, u32[]{:S(2)}) async-start(bf16[32,32,512]{2,1,0:T(8,128)(2,1)} %bitcast.15), calls=%async_computation.1 | async-start | bytes 2097152 | tf_op jit(solution)/shard_map/all_to_all | solution.py:303
  164.1 1.1 collective-permute-start.8
  165.5 10.7 %collective-permute-done.6 = f32[32,64]{1,0:T(8,128)S(1)} collective-permute-done((f32[32,64]{1,0:T(8,128)S(1)}, f32[32,64]{1,0:T(8,128)S(1)}, u32[]{:S(2)}, u32[]{:S(2)}) %collective-permute-start.6) | collective-permute-done | bytes 8224 | tf_op jit(solution)/shard_map/ppermute | solution.py:28
  176.6 3.2 %all-to-all-done.1 = bf16[32,32,512]{2,1,0:T(8,128)(2,1)S(1)} async-done(((bf16[32,32,512]{2,1,0:T(8,128)(2,1)}), bf16[32,32,512]{2,1,0:T(8,128)(2,1)S(1)}, u32[]{:S(2)}, u32[]{:S(2)}) %all-to-all-start.1) | async-done | bytes 1048608 | tf_op jit(solution)/shard_map/all_to_all | solution.py:303
  180.0 2.5 %collective-permute-start.5 = (f32[32,512]{1,0:T(8,128)S(1)}, f32[32,512]{1,0:T(8,128)S(1)}, u32[]{:S(2)}, u32[]{:S(2)}) collective-permute-start(f32[32,512]{1,0:T(8,128)S(1)} %convert_reduce_fusion), channel_id=1, source_target_pairs={{0,96},{32,0},{64,32},{96,64},{1,97},{33,1},{65,33},{97,65},{2,98}... | collective-permute-start | bytes 196616 | tf_op jit(solution)/shard_map/ppermute | solution.py:28
  182.5 1.4 collective-permute-start.3
  183.9 1.0 convolution_add_fusion
  184.9 2.0 %collective-permute-done.3 = f32[32,512]{1,0:T(8,128)S(1)} collective-permute-done((f32[32,512]{1,0:T(8,128)S(1)}, f32[32,512]{1,0:T(8,128)S(1)}, u32[]{:S(2)}, u32[]{:S(2)}) %collective-permute-start.3) | collective-permute-done | bytes 65568 | tf_op jit(solution)/shard_map/ppermute | solution.py:28
  187.0 0.6 add_add_fusion
  (65 shorter events, 5.0 us)
Async XLA Ops:
  0.6 0.9 copy-start
  0.6 21.2 %copy-start.8 = (bf16[64,128]{1,0:T(8,128)(2,1)S(1)}, bf16[64,128]{1,0:T(8,128)(2,1)}, u32[]{:S(2)}) copy-start(bf16[64,128]{1,0:T(8,128)(2,1)} %param.13) | copy-start | bytes 49156
  0.7 21.2 %copy-start.12 = (bf16[128]{0:T(256)(128)(2,1)S(1)}, bf16[128]{0:T(256)(128)(2,1)}, u32[]{:S(2)}) copy-start(bf16[128]{0:T(256)(128)(2,1)} %param.14) | copy-start | bytes 772
  0.7 21.8 %copy-start.11 = (bf16[64]{0:T(256)(128)(2,1)S(1)}, bf16[64]{0:T(256)(128)(2,1)}, u32[]{:S(2)}) copy-start(bf16[64]{0:T(256)(128)(2,1)} %param.16) | copy-start | bytes 388
  0.7 22.1 %copy-start.9 = (bf16[128,64]{0,1:T(8,128)(2,1)S(1)}, bf16[128,64]{0,1:T(8,128)(2,1)}, u32[]{:S(2)}) copy-start(bf16[128,64]{0,1:T(8,128)(2,1)} %param.15) | copy-start | bytes 49156
  0.7 22.9 %copy-start.5 = (bf16[1024,512]{1,0:T(8,128)(2,1)S(1)}, bf16[1024,512]{1,0:T(8,128)(2,1)}, u32[]{:S(2)}) copy-start(bf16[1024,512]{1,0:T(8,128)(2,1)} %param.12) | copy-start | bytes 3145732
  2.7 7.4 %collective-permute-start.2 = (bf16[48,64]{0,1:T(8,128)(2,1)S(1)}, bf16[48,64]{0,1:T(8,128)(2,1)S(1)}, u32[]{:S(2)}, u32[]{:S(2)}) collective-permute-start(bf16[48,64]{0,1:T(8,128)(2,1)S(1)} %pad_maximum_fusion), channel_id=1, source_target_pairs={{0,96},{32,0},{64,32},{96,64},{1,97},{33,1},{65,33},{97,65},{2,98}... | collective-permute-start | bytes 18440 | tf_op jit(solution)/shard_map/ppermute | solution.py:28
  4.1 6.1 %collective-permute-start.1 = (bf16[48,64]{0,1:T(8,128)(2,1)S(1)}, bf16[48,64]{0,1:T(8,128)(2,1)S(1)}, u32[]{:S(2)}, u32[]{:S(2)}) collective-permute-start(bf16[48,64]{0,1:T(8,128)(2,1)S(1)} %pad_maximum_fusion), channel_id=1, source_target_pairs={{0,64},{32,96},{64,0},{96,32},{1,65},{33,97},{65,1},{97,33},{2,66}... | collective-permute-start | bytes 18440 | tf_op jit(solution)/shard_map/ppermute | solution.py:28
  5.4 4.9 %collective-permute-start = (bf16[48,64]{0,1:T(8,128)(2,1)S(1)}, bf16[48,64]{0,1:T(8,128)(2,1)S(1)}, u32[]{:S(2)}, u32[]{:S(2)}) collective-permute-start(bf16[48,64]{0,1:T(8,128)(2,1)S(1)} %pad_maximum_fusion), channel_id=1, source_target_pairs={{0,32},{32,64},{64,96},{96,0},{1,33},{33,65},{65,97},{97,1},{2,34}... | collective-permute-start | bytes 18440 | tf_op jit(solution)/shard_map/ppermute | solution.py:28
  11.6 26.2 %all-to-all-start = ((bf16[32,80,128]{2,1,0:T(8,128)(2,1)}), bf16[32,80,128]{2,1,0:T(8,128)(2,1)S(1)}, u32[]{:S(2)}, u32[]{:S(2)}) async-start(bf16[32,80,128]{2,1,0:T(8,128)(2,1)} %pad_add_fusion), calls=%async_computation | async-start | bytes 1310720 | tf_op jit(solution)/shard_map/all_to_all | solution.py:281
  22.8 13.2 %copy-start.7 = (bf16[128,8,8]{0,2,1:T(8,128)(2,1)}, bf16[128,8,8]{0,2,1:T(8,128)(2,1)S(1)}, u32[]{:S(2)}) copy-start(bf16[128,8,8]{0,2,1:T(8,128)(2,1)S(1)} %copy.95) | copy-start | bytes 49156
  24.8 3.4 %copy-start.1 = (bf16[4096,1024]{1,0:T(8,128)(2,1)S(1)}, bf16[4096,1024]{1,0:T(8,128)(2,1)}, u32[]{:S(2)}) copy-start(bf16[4096,1024]{1,0:T(8,128)(2,1)} %features.3) | copy-start | bytes 25165828
  35.9 1.9 %copy-start.3 = (bf16[32,64,1024]{2,1,0:T(8,128)(2,1)}, bf16[32,64,1024]{2,1,0:T(8,128)(2,1)S(1)}, u32[]{:S(2)}) copy-start(bf16[32,64,1024]{2,1,0:T(8,128)(2,1)S(1)} %tower.1.vt) | copy-start | bytes 12582916
  37.9 2.2 %copy-start.6 = (bf16[32,80,128]{2,1,0:T(8,128)(2,1)}, bf16[32,80,128]{2,1,0:T(8,128)(2,1)S(1)}, u32[]{:S(2)}) copy-start(bf16[32,80,128]{2,1,0:T(8,128)(2,1)S(1)} %all-to-all-done.arrived) | copy-start | bytes 1966084
  90.6 63.3 %all-to-all-start.2 = ((bf16[32,64,128]{2,1,0:T(8,128)(2,1)}), bf16[32,64,128]{2,1,0:T(8,128)(2,1)S(1)}, u32[]{:S(2)}, u32[]{:S(2)}) async-start(bf16[32,64,128]{2,1,0:T(8,128)(2,1)} %get-tuple-element.5), calls=%async_computation.2 | async-start | bytes 1048576 | tf_op jit(solution)/shard_map/all_to_all | solution.py:288
  141.1 3.4 %copy-start.2 = (bf16[4096,1024]{1,0:T(8,128)(2,1)S(1)}, bf16[4096,1024]{1,0:T(8,128)(2,1)}, u32[]{:S(2)}) copy-start(bf16[4096,1024]{1,0:T(8,128)(2,1)} %features.3) | copy-start | bytes 25165828
  144.5 2.2 %copy-start.4 = (bf16[32,64,1024]{2,1,0:T(8,128)(2,1)S(1)}, bf16[32,64,1024]{2,1,0:T(8,128)(2,1)}, u32[]{:S(2)}) copy-start(bf16[32,64,1024]{2,1,0:T(8,128)(2,1)} %get-tuple-element.4.grads) | copy-start | bytes 12582916
  153.9 22.4 %copy-start.10 = (s32[4]{0:T(128)S(1)}, s32[4]{0:T(128)}, u32[]{:S(2)}) copy-start(s32[4]{0:T(128)} %param.18) | copy-start | bytes 52
  153.9 25.9 %all-to-all-start.1 = ((bf16[32,32,512]{2,1,0:T(8,128)(2,1)}), bf16[32,32,512]{2,1,0:T(8,128)(2,1)S(1)}, u32[]{:S(2)}, u32[]{:S(2)}) async-start(bf16[32,32,512]{2,1,0:T(8,128)(2,1)} %bitcast.15), calls=%async_computation.1 | async-start | bytes 2097152 | tf_op jit(solution)/shard_map/all_to_all | solution.py:303
  163.5 12.7 %collective-permute-start.6 = (f32[32,64]{1,0:T(8,128)S(1)}, f32[32,64]{1,0:T(8,128)S(1)}, u32[]{:S(2)}, u32[]{:S(2)}) collective-permute-start(f32[32,64]{1,0:T(8,128)S(1)} %get-tuple-element.8), channel_id=1, source_target_pairs={{0,96},{32,0},{64,32},{96,64},{1,97},{33,1},{65,33},{97,65},{2,98}... | collective-permute-start | bytes 24584 | tf_op jit(solution)/shard_map/ppermute | solution.py:28
  164.1 12.1 %collective-permute-start.8 = (f32[32,64]{1,0:T(8,128)S(1)}, f32[32,64]{1,0:T(8,128)S(1)}, u32[]{:S(2)}, u32[]{:S(2)}) collective-permute-start(f32[32,64]{1,0:T(8,128)S(1)} %get-tuple-element.9), channel_id=1, source_target_pairs={{0,32},{32,64},{64,96},{96,0},{1,33},{33,65},{65,97},{97,1},{2,34}... | collective-permute-start | bytes 24584 | tf_op jit(solution)/shard_map/ppermute | solution.py:28
  165.3 11.0 %collective-permute-start.7 = (f32[32,64]{1,0:T(8,128)S(1)}, f32[32,64]{1,0:T(8,128)S(1)}, u32[]{:S(2)}, u32[]{:S(2)}) collective-permute-start(f32[32,64]{1,0:T(8,128)S(1)} %get-tuple-element.10), channel_id=1, source_target_pairs={{0,64},{32,96},{64,0},{96,32},{1,65},{33,97},{65,1},{97,33},{2,66}... | collective-permute-start | bytes 24584 | tf_op jit(solution)/shard_map/ppermute | solution.py:28
  180.0 4.9 %collective-permute-start.5 = (f32[32,512]{1,0:T(8,128)S(1)}, f32[32,512]{1,0:T(8,128)S(1)}, u32[]{:S(2)}, u32[]{:S(2)}) collective-permute-start(f32[32,512]{1,0:T(8,128)S(1)} %convert_reduce_fusion), channel_id=1, source_target_pairs={{0,96},{32,0},{64,32},{96,64},{1,97},{33,1},{65,33},{97,65},{2,98}... | collective-permute-start | bytes 196616 | tf_op jit(solution)/shard_map/ppermute | solution.py:28
  182.5 2.4 %collective-permute-start.4 = (f32[32,512]{1,0:T(8,128)S(1)}, f32[32,512]{1,0:T(8,128)S(1)}, u32[]{:S(2)}, u32[]{:S(2)}) collective-permute-start(f32[32,512]{1,0:T(8,128)S(1)} %convert_reduce_fusion), channel_id=1, source_target_pairs={{0,32},{32,64},{64,96},{96,0},{1,33},{33,65},{65,97},{97,1},{2,34}... | collective-permute-start | bytes 196616 | tf_op jit(solution)/shard_map/ppermute | solution.py:28
  182.5 4.4 %collective-permute-start.3 = (f32[32,512]{1,0:T(8,128)S(1)}, f32[32,512]{1,0:T(8,128)S(1)}, u32[]{:S(2)}, u32[]{:S(2)}) collective-permute-start(f32[32,512]{1,0:T(8,128)S(1)} %convert_reduce_fusion), channel_id=1, source_target_pairs={{0,64},{32,96},{64,0},{96,32},{1,65},{33,97},{65,1},{97,33},{2,66}... | collective-permute-start | bytes 196616 | tf_op jit(solution)/shard_map/ppermute | solution.py:28

commit v2 on v1

v2 whole, which is shorter than its diff:
```python
import math

import jax
import jax.numpy as jnp
from jax import lax
from jax.experimental import pallas as pl
from jax.experimental.pallas import tpu as pltpu
from jax.sharding import PartitionSpec as P

K = 8
H = 64
BLK = 128
CAP = 2
OWN = 32
USERS = 4
TILE_USERS = 2
UTAB = 128
E = 512
GROUPS = 4
CIRCLE_USERS = GROUPS * USERS
ROWS = CIRCLE_USERS * K
PAIRS = K * K
F32 = jnp.float32
BF = jnp.bfloat16
VMEM_SPEC = pl.BlockSpec(memory_space=pltpu.VMEM)


def shifted(x, by):
    return lax.ppermute(x, "blk", [(i, (i + by) % GROUPS) for i in range(GROUPS)])


def tower_kernel(weight_t, features, out):
    product = lax.dot_general(
        weight_t[...], features[...], (((1,), (1,)), ((), ())), preferred_element_type=F32
    ).astype(BF)
    for c in range(2):
        for b in range(K):
            out[c, :, b * BLK : (b + 1) * BLK] = product[
                b * H : (b + 1) * H, c * BLK : (c + 1) * BLK
            ]


def tower_vectors(features, weight_t):
    width = features.shape[1]
    return pl.pallas_call(
        tower_kernel,
        grid=(OWN // 2,),
        in_specs=[
            pl.BlockSpec((E, width), lambda i: (0, 0)),
            pl.BlockSpec((2 * BLK, width), lambda i: (i, 0)),
        ],
        out_specs=pl.BlockSpec((2, H, K * BLK), lambda i: (i, 0, 0)),
        out_shape=jax.ShapeDtypeStruct((OWN, H, K * BLK), BF),
        compiler_params=pltpu.CompilerParams(vmem_limit_bytes=58 << 20),
        cost_estimate=pl.CostEstimate(
            flops=2 * OWN * BLK * E * width, bytes_accessed=13 << 20, transcendentals=0
        ),
        name="tower",
    )(weight_t, features)


def pair_kernel(codes, arrived_any, vt_any, features_any, first_half, first, second_t,
                second_half, bias1, bias2, out, arrived, vt, features, grads, deltas, total,
                entry_slot, entry_shard, entry_start, sems, *buffers):
    copies = [
        pltpu.make_async_copy(source, target, sems.at[i])
        for i, (source, target) in enumerate(
            ((arrived_any, arrived), (vt_any, vt), (features_any, features))
        )
    ]
    for copy in copies:
        copy.start()
    owners = codes.shape[0]
    logits, hidden, slope, weights, back, pair_grad = [
        buffers[2 * i : 2 * i + 2] for i in range(6)
    ]
    tile = TILE_USERS * BLK
    tiles = CIRCLE_USERS // TILE_USERS

    def clear(position, carry):
        entry_slot[position] = OWN
        entry_shard[position] = owners
        entry_start[position] = 0
        return carry

    lax.fori_loop(0, owners * CAP + 8, clear, 0)

    def enter(position, count):
        shard = position // CAP
        rank = position % CAP
        slot = codes[shard, rank]
        entry_slot[count + 2] = jnp.where(slot >= 0, slot, OWN)
        entry_shard[count + 2] = jnp.where(slot >= 0, shard, owners)
        entry_start[count + 2] = codes[shard, CAP + rank] * BLK
        return count + jnp.where(slot >= 0, 1, 0)

    count = lax.fori_loop(0, owners * CAP, enter, 0)
    grads[...] = jnp.zeros_like(grads)
    deltas[...] = jnp.zeros_like(deltas)
    lane = lax.broadcasted_iota(jnp.int32, (16, BLK), 1).astype(F32)
    copies[0].wait()
    copies[1].wait()

    def users_of(shard):
        packed = arrived[jnp.minimum(shard, owners - 1), 0 : ROWS // 2, :]
        return jnp.concatenate([packed[:, :H], packed[:, H:]], axis=0)

    def items_of(slot):
        return vt[jnp.minimum(slot, OWN - 1)]

    def logits_of(ref, k):
        return jnp.concatenate(
            [
                jnp.concatenate(
                    [ref[u * K : (u + 1) * K, b * BLK : (b + 1) * BLK] for b in range(K)],
                    axis=0,
                )
                for u in range(TILE_USERS * k, TILE_USERS * (k + 1))
            ],
            axis=1,
        )

    def stages(n, even):
        odd = 1 - even
        start_slot, start_shard = entry_slot[n + 2], entry_shard[n + 2]
        middle_shard, middle_start = entry_shard[n + 1], entry_start[n + 1]
        end_slot, end_shard = entry_slot[n], entry_shard[n]
        meta = arrived[jnp.minimum(middle_shard, owners - 1), ROWS // 2 : ROWS // 2 + 16, :]
        meta = meta.astype(F32)
        offset = meta[:, 0:16] * BLK + meta[:, 16:32] - middle_start.astype(F32)

        def scores():
            logits[even][...] = jnp.dot(
                users_of(start_shard), items_of(start_slot), preferred_element_type=F32
            )

        def forward(k):
            columns = slice(k * tile, (k + 1) * tile)
            h = jnp.dot(
                first_half[...],
                logits_of(logits[even], k).astype(BF),
                preferred_element_type=F32,
            ) + jnp.concatenate([bias1[...]] * TILE_USERS, axis=1)
            t = jnp.tanh(h)
            q = 1.0 + t
            silu = h * q
            hidden[even][:, columns] = silu.astype(BF)
            slope[even][:, columns] = q + silu * (1.0 - t)

        def mix(k):
            columns = slice(k * tile, (k + 1) * tile)
            users = range(TILE_USERS * k, TILE_USERS * (k + 1))
            y = jnp.concatenate(
                [
                    jnp.max(
                        jnp.where(offset[:, u : u + 1] == lane, 1.0, 0.0), axis=0, keepdims=True
                    )
                    for u in users
                ],
                axis=1,
            )
            gate = jnp.dot(
                second_t[...], hidden[odd][:, columns], preferred_element_type=F32
            ) + jnp.concatenate([bias2[...]] * TILE_USERS, axis=1)
            e = jnp.exp(gate)
            lk = logits_of(logits[odd], k)
            inverse = 1.0 / jnp.sum(e, axis=0, keepdims=True)
            score = jnp.sum(e * lk, axis=0, keepdims=True) * inverse
            score_grad = 0.5 + 0.5 * jnp.tanh(0.5 * score) - y
            weighted = e * (score_grad * inverse)
            weights[odd][:, columns] = weighted
            return (weighted * (lk - score)).astype(BF)

        def gate_back(k, logit_grad):
            columns = slice(k * tile, (k + 1) * tile)
            hidden_grad = jnp.dot(second_half[...], logit_grad, preferred_element_type=F32)
            back[odd][:, columns] = (hidden_grad * slope[odd][:, columns]).astype(BF)

        def pair_back(k):
            columns = slice(k * tile, (k + 1) * tile)
            pg = jnp.dot(first[...], back[even][:, columns], preferred_element_type=F32)
            pg = pg + weights[even][:, columns]
            rows = slice(K * TILE_USERS * k, K * TILE_USERS * (k + 1))
            for b in range(K):
                pair_grad[even][rows, b * BLK : (b + 1) * BLK] = jnp.concatenate(
                    [
                        pg[b * K : (b + 1) * K, w * BLK : (w + 1) * BLK]
                        for w in range(TILE_USERS)
                    ],
                    axis=0,
                ).astype(BF)

        previous = None
        for k in range(tiles):
            pair_back(k)
            logit_grad = mix(k)
            if k == 0:
                scores()
            else:
                gate_back(k - 1, previous)
            if k >= tiles // 2:
                forward(2 * k - tiles)
                forward(2 * k - tiles + 1)
            previous = logit_grad
        gate_back(tiles - 1, previous)
        pgv = pair_grad[even][...]
        deltas[end_shard] += lax.dot_general(
            pgv, items_of(end_slot), (((1,), (1,)), ((), ())), preferred_element_type=F32
        )
        grads[end_slot] += jnp.dot(users_of(end_shard).T, pgv, preferred_element_type=F32)

    def step(i, carry):
        stages(2 * i, 0)
        stages(2 * i + 1, 1)
        return carry

    lax.fori_loop(0, (count + 3) // 2, step, 0)

    rows = out.shape[1] - ROWS // 8
    scaling = 1.0 / math.sqrt(H)
    for c in range(4):
        for half in range(2):
            first_row = half * (ROWS // 2) + c * (ROWS // 8)
            out[:, rows:, c * 2 * H + half * H : c * 2 * H + (half + 1) * H] = (
                deltas[0:owners, first_row : first_row + ROWS // 8, :] * scaling
            ).astype(BF)
    copies[2].wait()
    blocks = 4

    def add(i, carry):
        left = jnp.concatenate(
            [
                jnp.concatenate(
                    [
                        grads[i * blocks + c, :, b * BLK : (b + 1) * BLK].astype(BF)
                        for b in range(K)
                    ],
                    axis=0,
                )
                for c in range(blocks)
            ],
            axis=1,
        )
        start = pl.multiple_of(i * blocks * BLK, blocks * BLK)
        product = jnp.dot(
            left, features[pl.ds(start, blocks * BLK), :], preferred_element_type=F32
        )

        @pl.when(i == 0)
        def _():
            total[...] = product

        @pl.when(i > 0)
        def _():
            total[...] += product

        return carry

    lax.fori_loop(0, OWN // blocks, add, 0)
    for part in range(total.shape[1] // BLK):
        turned = total[:, part * BLK : (part + 1) * BLK].T.astype(BF)
        for c in range(BLK // rows):
            out[part * (BLK // rows) + c, 0:rows, :] = turned[c * rows : (c + 1) * rows, :]


def pair_terms(codes, arrived, vt, features, gates):
    owners = codes.shape[0]
    width = features.shape[1]
    any_spec = pl.BlockSpec(memory_space=pl.ANY)
    columns = CIRCLE_USERS * BLK
    hidden = gates[0].shape[0]

    def twice(shape, dtype):
        return [pltpu.VMEM(shape, dtype)] * 2

    return pl.pallas_call(
        pair_kernel,
        out_shape=jax.ShapeDtypeStruct((owners, width // owners + ROWS // 8, E), BF),
        in_specs=[pl.BlockSpec(memory_space=pltpu.SMEM)] + [any_spec] * 3 + [VMEM_SPEC] * 6,
        out_specs=VMEM_SPEC,
        scratch_shapes=[
            pltpu.VMEM(arrived.shape, BF),
            pltpu.VMEM(vt.shape, BF),
            pltpu.VMEM(features.shape, BF),
            pltpu.VMEM((OWN + 1, H, K * BLK), F32),
            pltpu.VMEM((owners + 1, ROWS, H), F32),
            pltpu.VMEM((E, width), F32),
            pltpu.SMEM((owners * CAP + 8,), jnp.int32),
            pltpu.SMEM((owners * CAP + 8,), jnp.int32),
            pltpu.SMEM((owners * CAP + 8,), jnp.int32),
            pltpu.SemaphoreType.DMA((3,)),
        ]
        + twice((ROWS, K * BLK), F32)
        + twice((hidden, columns), BF)
        + twice((hidden, columns), F32)
        + twice((PAIRS, columns), F32)
        + twice((hidden, columns), BF)
        + twice((ROWS, K * BLK), BF),
        compiler_params=pltpu.CompilerParams(vmem_limit_bytes=58 << 20),
        cost_estimate=pl.CostEstimate(
            flops=40 << 30, bytes_accessed=16 << 20, transcendentals=1 << 24
        ),
        name="pairs",
    )(codes, arrived, vt, features, *gates)


def gate_layers(gate_in, gate_in_bias, gate_out, gate_out_bias):
    hidden = gate_in.shape[1]
    first = gate_in.reshape(K, K, hidden).transpose(1, 0, 2).reshape(PAIRS, hidden)
    second = gate_out.reshape(hidden, K, K).transpose(0, 2, 1).reshape(hidden, PAIRS)
    bias2 = gate_out_bias.reshape(K, K).T.reshape(PAIRS)
    half = jnp.asarray(0.5, BF)
    return (
        first.T * half,
        first,
        second.T,
        second * half,
        jnp.broadcast_to(gate_in_bias.astype(F32)[:, None] * 0.5, (hidden, BLK)),
        jnp.broadcast_to(bias2.astype(F32)[:, None], (PAIRS, BLK)),
    )


def split_product(left_bf16, right_f32):
    upper = right_f32.astype(BF)
    lower = (right_f32 - upper.astype(F32)).astype(BF)
    dims = (((0,), (0,)), ((), ()))
    first = lax.dot_general(left_bf16, upper, dims, preferred_element_type=F32)
    second = lax.dot_general(left_bf16, lower, dims, preferred_element_type=F32)
    return first + second


def shards(
    item_features,
    tower_weight,
    gate_in,
    gate_in_bias,
    gate_out,
    gate_out_bias,
    user_table,
    user_ids,
    positive_item,
    listed_owner,
    listed_slot,
):
    owner_count = lax.axis_size("shard")
    group = lax.axis_index("blk")
    listings = listed_slot.shape[0]
    owner_ids = listed_owner[:, 0]
    order = jnp.arange(listings, dtype=jnp.int32)
    same_owner = owner_ids[:, None] == owner_ids[None, :]
    earlier = order[None, :] < order[:, None]
    rank_within = jnp.sum(jnp.logical_and(same_owner, earlier), axis=1)
    owner_match = owner_ids[:, None] == jnp.arange(owner_count, dtype=jnp.int32)[None, :]
    rank_match = rank_within[:, None] == jnp.arange(CAP, dtype=jnp.int32)[None, :]
    placement = jnp.logical_and(owner_match[:, :, None], rank_match[:, None, :])
    wanted = jnp.sum(jnp.where(placement, listed_slot[:, None, None] + 1, 0), axis=0) - 1
    place = group * listings + order
    wanted_place = jnp.sum(jnp.where(placement, place[:, None, None], 0), axis=0)
    codes = jnp.concatenate([wanted, wanted_place], axis=1).astype(BF)

    row_match = user_ids[:, None] == jnp.arange(UTAB, dtype=jnp.int32)[None, :]
    user_rows = jnp.dot(row_match.astype(BF), user_table, preferred_element_type=F32)
    user_rows = (user_rows * (1.0 / math.sqrt(H))).astype(BF).reshape(USERS * K, H)
    positives = positive_item.T
    marks = jnp.concatenate([positives // BLK, positives % BLK], axis=1).astype(BF)
    own = jnp.concatenate([user_rows, jnp.pad(marks, ((0, 0), (0, H - 2 * USERS)))], axis=0)
    pieces = [own] + [shifted(own, by) for by in range(1, GROUPS)]
    rows = [piece[: USERS * K] for piece in pieces]
    marks = [piece[USERS * K :] for piece in pieces]
    packed = jnp.concatenate(
        [jnp.concatenate(rows[0:2], axis=0), jnp.concatenate(rows[2:4], axis=0)], axis=1
    )
    meta = jnp.concatenate(
        [m[:, :USERS] for m in marks] + [m[:, USERS : 2 * USERS] for m in marks], axis=1
    )
    meta = jnp.pad(meta, ((0, 0), (0, 2 * H - 2 * CIRCLE_USERS)))
    common = jnp.concatenate([packed, meta], axis=0)
    sent = jnp.broadcast_to(common[None], (owner_count,) + common.shape)
    codes = jnp.pad(
        codes[:, None, :],
        ((0, 0), (ROWS // 2, 15), (2 * CIRCLE_USERS, 2 * H - 2 * CIRCLE_USERS - 2 * CAP)),
    )
    arrived = lax.all_to_all(sent + codes, "shard", split_axis=0, concat_axis=0, tiled=True)
    asked = arrived[:, ROWS // 2, 2 * CIRCLE_USERS : 2 * CIRCLE_USERS + 2 * CAP].astype(jnp.int32)

    vt = tower_vectors(item_features, tower_weight.T)
    gates = gate_layers(gate_in, gate_in_bias, gate_out, gate_out_bias)
    terms = pair_terms(asked, arrived, vt, item_features, gates)
    terms = lax.all_to_all(terms, "shard", split_axis=0, concat_axis=0, tiled=True)
    sums = jnp.sum(terms.astype(F32), axis=0)
    rows = sums.shape[0] - ROWS // 8
    user_sum = sums[rows:].reshape(ROWS // 8, 4, 2 * H).transpose(1, 0, 2)
    user_sum = user_sum.reshape(ROWS // 2, 2 * H)
    half_rows = ROWS // 4
    quarters = [
        user_sum[
            half_rows * (q % 2) : half_rows * (q % 2 + 1), H * (q // 2) : H * (q // 2 + 1)
        ].reshape(USERS, E)
        for q in range(GROUPS)
    ]
    parts = [jnp.concatenate([sums[:rows], quarter], axis=0) for quarter in quarters]
    parts = [parts[0]] + [shifted(parts[q], -q) for q in range(1, GROUPS)]
    total = (parts[0] + parts[2]) + (parts[1] + parts[3])
    tower_gradient = total[:rows]
    user_gradient = split_product(row_match.astype(BF), total[rows:])
    return (tower_gradient, user_gradient)


def solution(mesh):
    return jax.shard_map(
        shards,
        mesh=mesh,
        in_specs=(
            P("shard", None),
            P(),
            P(),
            P(),
            P(),
            P(),
            P(("blk", "shard"), None),
            P(("blk", "shard")),
            P(("blk", "shard"), None),
            P(("blk", "shard"), None),
            P(("blk", "shard")),
        ),
        out_specs=(P("shard", None), P(("blk", "shard"), None)),
        check_vma=False,
    )
```

time: 189 us -> 155 us (0.82)
  blocking collectives: 0 us -> 74.7 us
  starting transfers between devices: 80.2 us -> 17.2 us
  Pallas kernels: 65.5 us -> 40 us
  waiting for transfers between devices: 15.9 us -> 4.39 us
  local copies, waits for them, and re-layouts: 15.5 us -> 6.29 us
    all_to_all x0 -> x1, blocking collectives: none -> 74.7 us  [shards(): lax.all_to_all(terms, 'shard', split_axis=0, concat_axis=0, tiled=True)]
    all_to_all x2 -> x0, starting transfers between devices: 59.9 us -> none  [the longest x1 50.5 us: shards(): lax.all_to_all(user_terms, 'shard', split_axis=0, concat_axis=0, tiled=True)]
    pallas_call x2 -> x1, Pallas kernels: 57.8 us -> 25.2 us  [pair_terms(): pl.pallas_call(pair_kernel, out_shape=jax.ShapeDtypeStruct((owners, width...]
    unnamed x27 -> x19, local copies, waits for them, and re-layouts: 11.5 us -> 1.43 us
    ppermute x9 -> x6, waiting for transfers between devices: 12.8 us -> 4.38 us  [shifted(): lax.ppermute(x, 'blk', [(i, (i + by) % GROUPS) for i in range(GROUPS)])]
    pallas_call x1, Pallas kernels: 7.75 us -> 14.8 us  [tower_vectors(): pl.pallas_call(tower_kernel, grid=(OWN // 2,), in_specs=[pl.BlockSpec((E,...]
    all_to_all x2 -> x0, waiting for transfers between devices: 3.17 us -> none  [the longest x1 3.17 us: shards(): lax.all_to_all(partial_value.reshape(owner_count, width // owner_count, E...]
    ppermute x9 -> x6, starting transfers between devices: 10.1 us -> 6.97 us  [shifted(): lax.ppermute(x, 'blk', [(i, (i + by) % GROUPS) for i in range(GROUPS)])]
  transfers between devices with their start and end apart: 12 -> 7, of which waited for: 3 -> 3; matrix products, arithmetic and copies ran while one was open for 4% -> 5% of each run, Pallas kernels for 8% -> 10%
where the time goes in v2:
time: 155 us; the launch traced here: 152 us
  blocking collectives  74.7 us (48%)
  Pallas kernels  40 us (26%)
  starting transfers between devices  17.2 us (11%)
  other arithmetic  6.91 us (4%)
  local copies, waits for them, and re-layouts  6.29 us (4%)
  waiting for transfers between devices  4.39 us (3%)
  matrix products  2.13 us (1%)
    all_to_all x1, blocking collectives, shards(): lax.all_to_all(terms, 'shard', split_axis=0, concat_axis=0, tiled=True)  74.7 us
    pallas_call x1, Pallas kernels, pair_terms(): pl.pallas_call(pair_kernel, out_shape=jax.ShapeDtypeStruct((owners, width...  25.2 us
    pallas_call x1, Pallas kernels, tower_vectors(): pl.pallas_call(tower_kernel, grid=(OWN // 2,), in_specs=[pl.BlockSpec((E,...  14.8 us
    all_to_all x1, starting transfers between devices, shards(): lax.all_to_all(sent + codes, 'shard', split_axis=0, concat_axis=0, tiled=...  10.2 us
    ppermute x6, starting transfers between devices, shifted(): lax.ppermute(x, 'blk', [(i, (i + by) % GROUPS) for i in range(GROUPS)])  6.97 us
    ppermute x6, waiting for transfers between devices, shifted(): lax.ppermute(x, 'blk', [(i, (i + by) % GROUPS) for i in range(GROUPS)])  4.38 us
  transfers between devices with their start and end apart: 7, of which 3 were waited for; matrix products, arithmetic and copies ran while one was open for 5% of the time, Pallas kernels for 10%

profile of v2, /device:TPU:1, one launch (start us, length us, event | category | flops | bytes accessed | tf_op | source)
XLA Modules:
  0.0 152.4 jit_solution(10824122977331047791)
XLA Ops:
  0.7 0.8 fusion.13
  1.6 0.8 fusion
  2.7 1.4 collective-permute-start.2
  4.1 1.3 collective-permute-start.1
  5.4 1.3 collective-permute-start
  6.8 0.9 convert_reduce_fusion.1
  7.7 0.7 iota_compare_fusion.4
  8.4 0.7 broadcast_add_fusion
  9.1 0.7 multiply_bitcast_fusion
  9.9 0.1 fusion.8
  10.4 0.1 concatenate.54
  10.7 1.0 pad_add_fusion
  11.7 10.2 %all-to-all-start = ((bf16[32,80,128]{2,1,0:T(8,128)(2,1)}), bf16[32,80,128]{2,1,0:T(8,128)(2,1)S(1)}, u32[]{:S(2)}, u32[]{:S(2)}) async-start(bf16[32,80,128]{2,1,0:T(8,128)(2,1)} %pad_add_fusion), calls=%async_computation | async-start | bytes 1310720 | tf_op jit(solution)/shard_map/all_to_all | solution.py:383
  21.9 0.6 copy.100
  22.8 0.7 copy.92.first_half
  23.7 1.3 copy.85
  25.0 0.6 broadcast_multiply_fusion.second_half
  25.6 14.8 %tower.1.vt_any = bf16[32,64,1024]{2,1,0:T(8,128)(2,1)} custom-call(bf16[512,1024]{1,0:T(8,128)(2,1)} %bitcast.55, bf16[4096,1024]{1,0:T(8,128)(2,1)} %features_any.1), custom_call_target="tpu_custom_call" | custom-call | flops 4294967296 | bytes 13631488 | tf_op jit(solution)/shard_map/tower/pallas_call | solution.py:45
  40.4 0.8 slice_convert_fusion
  41.2 0.7 broadcast_in_dim.29.bias2
  41.9 0.7 broadcast_in_dim.28.bias1
  42.6 25.2 %pairs.1 = bf16[32,48,512]{2,1,0:T(8,128)(2,1)} custom-call(s32[32,4]{1,0:T(8,128)} %bitcast.67, bf16[32,80,128]{2,1,0:T(8,128)(2,1)} %copy-done.2, bf16[32,64,1024]{2,1,0:T(8,128)(2,1)} %tower.1.vt_any, bf16[4096,1024]{1,0:T(8,128)(2,1)} %features_any.1, bf16[128,64]{1,0:T(8,128)(2,1)} %copy.92.first_half, bf16[64,128]{1,0:T(8,128)(2,1)} %bitcast.66, ...), custom_call_target="tpu_custom_call" | custom-call | flops 42949672960 | bytes 16777216 | tf_op jit(solution)/shard_map/pairs/pallas_call | solution.py:276
  67.8 74.7 %all_to_all.10 = bf16[32,48,512]{2,1,0:T(8,128)(2,1)S(1)} all-to-all(bf16[32,48,512]{2,1,0:T(8,128)(2,1)} %pairs.1), channel_id=1, replica_groups=mesh['blk'=4,'shard'=32] {'shard'}, dimensions={0} | all-to-all | bytes 3145728 | tf_op jit(solution)/shard_map/all_to_all | solution.py:389
  142.5 0.2 convert_reduce_fusion
  143.1 1.6 %collective-permute-start.5 = (f32[36,512]{1,0:T(8,128)S(1)}, f32[36,512]{1,0:T(8,128)S(1)}, u32[]{:S(2)}, u32[]{:S(2)}) collective-permute-start(f32[36,512]{1,0:T(8,128)S(1)} %get-tuple-element.4), channel_id=1, source_target_pairs={{0,32},{32,64},{64,96},{96,0},{1,33},{33,65},{65,97},{97,1},{2,34}... | collective-permute-start | bytes 221192 | tf_op jit(solution)/shard_map/ppermute | solution.py:29
  144.7 1.3 collective-permute-start.3
  146.1 0.1 collective-permute-done.5
  146.2 3.6 %collective-permute-done.3 = f32[36,512]{1,0:T(8,128)S(1)} collective-permute-done((f32[36,512]{1,0:T(8,128)S(1)}, f32[36,512]{1,0:T(8,128)S(1)}, u32[]{:S(2)}, u32[]{:S(2)}) %collective-permute-start.3) | collective-permute-done | bytes 73760 | tf_op jit(solution)/shard_map/ppermute | solution.py:29
  149.8 0.6 collective-permute-done.4
  150.5 0.6 slice.110
  151.1 0.3 fusion.11
  151.4 1.0 convolution_add_fusion
  (54 shorter events, 1.8 us)
Async XLA Ops:
  0.6 0.9 copy-start
  0.6 21.3 %copy-start.4 = (bf16[64,128]{1,0:T(8,128)(2,1)S(1)}, bf16[64,128]{1,0:T(8,128)(2,1)}, u32[]{:S(2)}) copy-start(bf16[64,128]{1,0:T(8,128)(2,1)} %param.13) | copy-start | bytes 49156
  0.7 21.2 %copy-start.8 = (bf16[128]{0:T(256)(128)(2,1)S(1)}, bf16[128]{0:T(256)(128)(2,1)}, u32[]{:S(2)}) copy-start(bf16[128]{0:T(256)(128)(2,1)} %param.14) | copy-start | bytes 772
  0.7 21.9 %copy-start.7 = (bf16[64]{0:T(256)(128)(2,1)S(1)}, bf16[64]{0:T(256)(128)(2,1)}, u32[]{:S(2)}) copy-start(bf16[64]{0:T(256)(128)(2,1)} %param.16) | copy-start | bytes 388
  0.7 22.1 %copy-start.5 = (bf16[128,64]{0,1:T(8,128)(2,1)S(1)}, bf16[128,64]{0,1:T(8,128)(2,1)}, u32[]{:S(2)}) copy-start(bf16[128,64]{0,1:T(8,128)(2,1)} %param.15) | copy-start | bytes 49156
  0.7 23.0 %copy-start.1 = (bf16[1024,512]{1,0:T(8,128)(2,1)S(1)}, bf16[1024,512]{1,0:T(8,128)(2,1)}, u32[]{:S(2)}) copy-start(bf16[1024,512]{1,0:T(8,128)(2,1)} %param.12) | copy-start | bytes 3145732
  2.7 7.4 %collective-permute-start.2 = (bf16[48,64]{0,1:T(8,128)(2,1)S(1)}, bf16[48,64]{0,1:T(8,128)(2,1)S(1)}, u32[]{:S(2)}, u32[]{:S(2)}) collective-permute-start(bf16[48,64]{0,1:T(8,128)(2,1)S(1)} %pad_maximum_fusion.4), channel_id=1, source_target_pairs={{0,96},{32,0},{64,32},{96,64},{1,97},{33,1},{65,33},{97,65},{2,98}... | collective-permute-start | bytes 18440 | tf_op jit(solution)/shard_map/ppermute | solution.py:29
  4.1 6.1 %collective-permute-start.1 = (bf16[48,64]{0,1:T(8,128)(2,1)S(1)}, bf16[48,64]{0,1:T(8,128)(2,1)S(1)}, u32[]{:S(2)}, u32[]{:S(2)}) collective-permute-start(bf16[48,64]{0,1:T(8,128)(2,1)S(1)} %pad_maximum_fusion.4), channel_id=1, source_target_pairs={{0,64},{32,96},{64,0},{96,32},{1,65},{33,97},{65,1},{97,33},{2,66}... | collective-permute-start | bytes 18440 | tf_op jit(solution)/shard_map/ppermute | solution.py:29
  5.4 4.9 %collective-permute-start = (bf16[48,64]{0,1:T(8,128)(2,1)S(1)}, bf16[48,64]{0,1:T(8,128)(2,1)S(1)}, u32[]{:S(2)}, u32[]{:S(2)}) collective-permute-start(bf16[48,64]{0,1:T(8,128)(2,1)S(1)} %pad_maximum_fusion.4), channel_id=1, source_target_pairs={{0,32},{32,64},{64,96},{96,0},{1,33},{33,65},{65,97},{97,1},{2,34}... | collective-permute-start | bytes 18440 | tf_op jit(solution)/shard_map/ppermute | solution.py:29
  11.7 28.7 %all-to-all-start = ((bf16[32,80,128]{2,1,0:T(8,128)(2,1)}), bf16[32,80,128]{2,1,0:T(8,128)(2,1)S(1)}, u32[]{:S(2)}, u32[]{:S(2)}) async-start(bf16[32,80,128]{2,1,0:T(8,128)(2,1)} %pad_add_fusion), calls=%async_computation | async-start | bytes 1310720 | tf_op jit(solution)/shard_map/all_to_all | solution.py:383
  22.8 17.6 %copy-start.3 = (bf16[128,8,8]{0,2,1:T(8,128)(2,1)}, bf16[128,8,8]{0,2,1:T(8,128)(2,1)S(1)}, u32[]{:S(2)}) copy-start(bf16[128,8,8]{0,2,1:T(8,128)(2,1)S(1)} %copy.101) | copy-start | bytes 49156
  40.4 2.2 %copy-start.2 = (bf16[32,80,128]{2,1,0:T(8,128)(2,1)}, bf16[32,80,128]{2,1,0:T(8,128)(2,1)S(1)}, u32[]{:S(2)}) copy-start(bf16[32,80,128]{2,1,0:T(8,128)(2,1)S(1)} %all-to-all-done.arrived_any) | copy-start | bytes 1966084
  142.4 8.6 %copy-start.6 = (s32[4]{0:T(128)S(1)}, s32[4]{0:T(128)}, u32[]{:S(2)}) copy-start(s32[4]{0:T(128)} %param.18) | copy-start | bytes 52
  143.1 3.1 %collective-permute-start.5 = (f32[36,512]{1,0:T(8,128)S(1)}, f32[36,512]{1,0:T(8,128)S(1)}, u32[]{:S(2)}, u32[]{:S(2)}) collective-permute-start(f32[36,512]{1,0:T(8,128)S(1)} %get-tuple-element.4), channel_id=1, source_target_pairs={{0,32},{32,64},{64,96},{96,0},{1,33},{33,65},{65,97},{97,1},{2,34}... | collective-permute-start | bytes 221192 | tf_op jit(solution)/shard_map/ppermute | solution.py:29
  144.7 5.1 %collective-permute-start.3 = (f32[36,512]{1,0:T(8,128)S(1)}, f32[36,512]{1,0:T(8,128)S(1)}, u32[]{:S(2)}, u32[]{:S(2)}) collective-permute-start(f32[36,512]{1,0:T(8,128)S(1)} %get-tuple-element.5), channel_id=1, source_target_pairs={{0,64},{32,96},{64,0},{96,32},{1,65},{33,97},{65,1},{97,33},{2,66}... | collective-permute-start | bytes 221192 | tf_op jit(solution)/shard_map/ppermute | solution.py:29
  146.0 4.5 %collective-permute-start.4 = (f32[36,512]{1,0:T(8,128)S(1)}, f32[36,512]{1,0:T(8,128)S(1)}, u32[]{:S(2)}, u32[]{:S(2)}) collective-permute-start(f32[36,512]{1,0:T(8,128)S(1)} %get-tuple-element.6), channel_id=1, source_target_pairs={{0,96},{32,0},{64,32},{96,64},{1,97},{33,1},{65,33},{97,65},{2,98}... | collective-permute-start | bytes 221192 | tf_op jit(solution)/shard_map/ppermute | solution.py:29

commit v3 on v2

--- a/solution.py
+++ b/solution.py
@@ -25,15 +25,15 @@
 VMEM_SPEC = pl.BlockSpec(memory_space=pltpu.VMEM)
 
 
-def shifted(x, by):
-    return lax.ppermute(x, "blk", [(i, (i + by) % GROUPS) for i in range(GROUPS)])
+def swapped(x, by):
+    return lax.ppermute(x, "blk", [(i, i ^ by) for i in range(GROUPS)])
 
 
 def tower_kernel(weight_t, features, out):
     product = lax.dot_general(
         weight_t[...], features[...], (((1,), (1,)), ((), ())), preferred_element_type=F32
     ).astype(BF)
-    for c in range(2):
+    for c in range(out.shape[0]):
         for b in range(K):
             out[c, :, b * BLK : (b + 1) * BLK] = product[
                 b * H : (b + 1) * H, c * BLK : (c + 1) * BLK
@@ -42,14 +42,15 @@
 
 def tower_vectors(features, weight_t):
     width = features.shape[1]
+    blocks = 8
     return pl.pallas_call(
         tower_kernel,
-        grid=(OWN // 2,),
+        grid=(OWN // blocks,),
         in_specs=[
             pl.BlockSpec((E, width), lambda i: (0, 0)),
-            pl.BlockSpec((2 * BLK, width), lambda i: (i, 0)),
+            pl.BlockSpec((blocks * BLK, width), lambda i: (i, 0)),
         ],
-        out_specs=pl.BlockSpec((2, H, K * BLK), lambda i: (i, 0, 0)),
+        out_specs=pl.BlockSpec((blocks, H, K * BLK), lambda i: (i, 0, 0)),
         out_shape=jax.ShapeDtypeStruct((OWN, H, K * BLK), BF),
         compiler_params=pltpu.CompilerParams(vmem_limit_bytes=58 << 20),
         cost_estimate=pl.CostEstimate(
@@ -59,8 +60,9 @@
     )(weight_t, features)
 
 
-def pair_kernel(codes, arrived_any, vt_any, features_any, first_half, first, second_t,
-                second_half, bias1, bias2, out, arrived, vt, features, grads, deltas, total,
+def pair_kernel(codes, group, arrived_any, vt_any, features_any, gate_in, gate_in_bias,
+                gate_out, gate_out_bias, keep, send, first_half, first, second_t, second_half,
+                bias1, bias2, arrived, vt, features, grads, deltas, total,
                 entry_slot, entry_shard, entry_start, sems, *buffers):
     copies = [
         pltpu.make_async_copy(source, target, sems.at[i])
@@ -98,6 +100,23 @@
     grads[...] = jnp.zeros_like(grads)
     deltas[...] = jnp.zeros_like(deltas)
     lane = lax.broadcasted_iota(jnp.int32, (16, BLK), 1).astype(F32)
+    row = lax.broadcasted_iota(jnp.int32, (PAIRS, PAIRS), 0)
+    column = lax.broadcasted_iota(jnp.int32, (PAIRS, PAIRS), 1)
+    order = jnp.where(column == (row & (K - 1)) * K + (row >> 3), 1.0, 0.0).astype(BF)
+    across = (((1,), (1,)), ((), ()))
+    turned_in = jnp.dot(order, gate_in[...], preferred_element_type=F32)
+    turned_out = lax.dot_general(order, gate_out[...], across, preferred_element_type=F32)
+    first[...] = turned_in.astype(BF)
+    first_half[...] = (turned_in.T * 0.5).astype(BF)
+    second_t[...] = turned_out.astype(BF)
+    second_half[...] = (turned_out.T * 0.5).astype(BF)
+    bias1[...] = jnp.broadcast_to(gate_in_bias[...].astype(F32) * 0.5, bias1.shape).T
+    bias2[...] = lax.dot_general(
+        order,
+        jnp.broadcast_to(gate_out_bias[...], (BLK, PAIRS)),
+        across,
+        preferred_element_type=F32,
+    )
     copies[0].wait()
     copies[1].wait()
 
@@ -190,24 +209,18 @@
                     axis=0,
                 ).astype(BF)
 
-        previous = None
         for k in range(tiles):
             pair_back(k)
-            logit_grad = mix(k)
-            if k == 0:
-                scores()
-            else:
-                gate_back(k - 1, previous)
-            if k >= tiles // 2:
-                forward(2 * k - tiles)
-                forward(2 * k - tiles + 1)
-            previous = logit_grad
-        gate_back(tiles - 1, previous)
+        scores()
+        logit_grads = [mix(k) for k in range(tiles)]
         pgv = pair_grad[even][...]
         deltas[end_shard] += lax.dot_general(
             pgv, items_of(end_slot), (((1,), (1,)), ((), ())), preferred_element_type=F32
         )
         grads[end_slot] += jnp.dot(users_of(end_shard).T, pgv, preferred_element_type=F32)
+        for k in range(tiles):
+            forward(k)
+            gate_back(k, logit_grads[k])
 
     def step(i, carry):
         stages(2 * i, 0)
@@ -216,14 +229,17 @@
 
     lax.fori_loop(0, (count + 3) // 2, step, 0)
 
-    rows = out.shape[1] - ROWS // 8
+    rows = keep.shape[1] - K
     scaling = 1.0 / math.sqrt(H)
-    for c in range(4):
-        for half in range(2):
-            first_row = half * (ROWS // 2) + c * (ROWS // 8)
-            out[:, rows:, c * 2 * H + half * H : c * 2 * H + (half + 1) * H] = (
-                deltas[0:owners, first_row : first_row + ROWS // 8, :] * scaling
-            ).astype(BF)
+    piece = USERS * K
+    for c in range(2 * USERS):
+        columns = slice(c * H, (c + 1) * H)
+        first_row = 2 * piece * (c // USERS) + K * (c % USERS)
+        keep[:, rows:, columns] = deltas[0:owners, first_row : first_row + K, :] * scaling
+        first_row = first_row + piece
+        send[:, rows:, columns] = (
+            deltas[0:owners, first_row : first_row + K, :] * scaling
+        ).astype(BF)
     copies[2].wait()
     blocks = 4
 
@@ -257,28 +273,41 @@
         return carry
 
     lax.fori_loop(0, OWN // blocks, add, 0)
+    parity = group[0] & 1
     for part in range(total.shape[1] // BLK):
-        turned = total[:, part * BLK : (part + 1) * BLK].T.astype(BF)
-        for c in range(BLK // rows):
-            out[part * (BLK // rows) + c, 0:rows, :] = turned[c * rows : (c + 1) * rows, :]
-
-
-def pair_terms(codes, arrived, vt, features, gates):
+        turned = total[:, part * BLK : (part + 1) * BLK].T
+        for c in range(BLK // (2 * rows)):
+            lower = turned[2 * rows * c : 2 * rows * c + rows, :]
+            upper = turned[2 * rows * c + rows : 2 * rows * (c + 1), :]
+            owner = part * (BLK // (2 * rows)) + c
+            keep[owner, 0:rows, :] = jnp.where(parity == 0, lower, upper)
+            send[owner, 0:rows, :] = jnp.where(parity == 0, upper, lower).astype(BF)
+
+
+def pair_terms(codes, group, arrived, vt, features, gates):
     owners = codes.shape[0]
     width = features.shape[1]
     any_spec = pl.BlockSpec(memory_space=pl.ANY)
     columns = CIRCLE_USERS * BLK
-    hidden = gates[0].shape[0]
+    hidden = gates[0].shape[1]
+    shape = (owners, width // (2 * owners) + K, E)
+    smem = pl.BlockSpec(memory_space=pltpu.SMEM)
 
     def twice(shape, dtype):
         return [pltpu.VMEM(shape, dtype)] * 2
 
     return pl.pallas_call(
         pair_kernel,
-        out_shape=jax.ShapeDtypeStruct((owners, width // owners + ROWS // 8, E), BF),
-        in_specs=[pl.BlockSpec(memory_space=pltpu.SMEM)] + [any_spec] * 3 + [VMEM_SPEC] * 6,
-        out_specs=VMEM_SPEC,
+        out_shape=(jax.ShapeDtypeStruct(shape, F32), jax.ShapeDtypeStruct(shape, BF)),
+        in_specs=[smem] * 2 + [any_spec] * 3 + [VMEM_SPEC] * 4,
+        out_specs=(VMEM_SPEC, VMEM_SPEC),
         scratch_shapes=[
+            pltpu.VMEM((hidden, PAIRS), BF),
+            pltpu.VMEM((PAIRS, hidden), BF),
+            pltpu.VMEM((PAIRS, hidden), BF),
+            pltpu.VMEM((hidden, PAIRS), BF),
+            pltpu.VMEM((hidden, BLK), F32),
+            pltpu.VMEM((PAIRS, BLK), F32),
             pltpu.VMEM(arrived.shape, BF),
             pltpu.VMEM(vt.shape, BF),
             pltpu.VMEM(features.shape, BF),
@@ -301,23 +330,7 @@
             flops=40 << 30, bytes_accessed=16 << 20, transcendentals=1 << 24
         ),
         name="pairs",
-    )(codes, arrived, vt, features, *gates)
-
-
-def gate_layers(gate_in, gate_in_bias, gate_out, gate_out_bias):
-    hidden = gate_in.shape[1]
-    first = gate_in.reshape(K, K, hidden).transpose(1, 0, 2).reshape(PAIRS, hidden)
-    second = gate_out.reshape(hidden, K, K).transpose(0, 2, 1).reshape(hidden, PAIRS)
-    bias2 = gate_out_bias.reshape(K, K).T.reshape(PAIRS)
-    half = jnp.asarray(0.5, BF)
-    return (
-        first.T * half,
-        first,
-        second.T,
-        second * half,
-        jnp.broadcast_to(gate_in_bias.astype(F32)[:, None] * 0.5, (hidden, BLK)),
-        jnp.broadcast_to(bias2.astype(F32)[:, None], (PAIRS, BLK)),
-    )
+    )(codes, group, arrived, vt, features, *gates)
 
 
 def split_product(left_bf16, right_f32):
@@ -364,7 +377,7 @@
     positives = positive_item.T
     marks = jnp.concatenate([positives // BLK, positives % BLK], axis=1).astype(BF)
     own = jnp.concatenate([user_rows, jnp.pad(marks, ((0, 0), (0, H - 2 * USERS)))], axis=0)
-    pieces = [own] + [shifted(own, by) for by in range(1, GROUPS)]
+    pieces = [own] + [swapped(own, by) for by in range(1, GROUPS)]
     rows = [piece[: USERS * K] for piece in pieces]
     marks = [piece[USERS * K :] for piece in pieces]
     packed = jnp.concatenate(
@@ -384,25 +397,23 @@
     asked = arrived[:, ROWS // 2, 2 * CIRCLE_USERS : 2 * CIRCLE_USERS + 2 * CAP].astype(jnp.int32)
 
     vt = tower_vectors(item_features, tower_weight.T)
-    gates = gate_layers(gate_in, gate_in_bias, gate_out, gate_out_bias)
-    terms = pair_terms(asked, arrived, vt, item_features, gates)
+    gates = (gate_in, gate_in_bias[None, :], gate_out, gate_out_bias[None, :])
+    keep, send = pair_terms(asked, group[None], arrived, vt, item_features, gates)
+    terms = (keep + swapped(send, 1).astype(F32)).astype(BF)
     terms = lax.all_to_all(terms, "shard", split_axis=0, concat_axis=0, tiled=True)
     sums = jnp.sum(terms.astype(F32), axis=0)
-    rows = sums.shape[0] - ROWS // 8
-    user_sum = sums[rows:].reshape(ROWS // 8, 4, 2 * H).transpose(1, 0, 2)
-    user_sum = user_sum.reshape(ROWS // 2, 2 * H)
-    half_rows = ROWS // 4
-    quarters = [
-        user_sum[
-            half_rows * (q % 2) : half_rows * (q % 2 + 1), H * (q // 2) : H * (q // 2 + 1)
-        ].reshape(USERS, E)
-        for q in range(GROUPS)
-    ]
-    parts = [jnp.concatenate([sums[:rows], quarter], axis=0) for quarter in quarters]
-    parts = [parts[0]] + [shifted(parts[q], -q) for q in range(1, GROUPS)]
-    total = (parts[0] + parts[2]) + (parts[1] + parts[3])
-    tower_gradient = total[:rows]
-    user_gradient = split_product(row_match.astype(BF), total[rows:])
+    rows = sums.shape[0] - K
+    half = sums[:rows]
+    from_1, from_2, from_3 = swapped(half, 1), swapped(sums, 2), swapped(half, 3)
+    mine = half + from_2[:rows]
+    other = from_1 + from_3
+    even = group % 2 == 0
+    tower_gradient = jnp.concatenate(
+        [jnp.where(even, mine, other), jnp.where(even, other, mine)], axis=0
+    )
+    user_delta = sums[rows:, : USERS * H] + from_2[rows:, USERS * H :]
+    user_delta = user_delta.reshape(K, USERS, H).transpose(1, 0, 2).reshape(USERS, E)
+    user_gradient = split_product(row_match.astype(BF), user_delta)
     return (tower_gradient, user_gradient)
 
 

time: 155 us -> 137 us (0.88); the launches traced: 152 us -> 136 us
  blocking collectives: 74.7 us -> 45.1 us
  Pallas kernels: 40 us -> 51.9 us
  starting transfers between devices: 17.2 us -> 20.6 us
  local copies, waits for them, and re-layouts: 6.29 us -> 3.09 us
    all_to_all x1, blocking collectives: 74.7 us -> 45.1 us  [shards(): lax.all_to_all(terms, 'shard', split_axis=0, concat_axis=0, tiled=True)]
    pallas_call x2, Pallas kernels: 40 us -> 51.9 us  [the longest x1 42.9 us: pair_terms(): pl.pallas_call(pair_kernel, out_shape=(jax.ShapeDtypeStruct(shape, F32),...]
    ppermute x6 -> x7, starting transfers between devices: 6.97 us -> 10.1 us  [swapped(): return lax.ppermute(x, 'blk', [(i, i ^ by) for i in range(GROUPS)])]
    convert_element_type x0 -> x1, other arithmetic: none -> 1.72 us  [shards(): terms = (keep + swapped(send, 1).astype(F32)).astype(BF)]
    ppermute x6 -> x7, waiting for transfers between devices: 4.38 us -> 3.12 us  [swapped(): return lax.ppermute(x, 'blk', [(i, i ^ by) for i in range(GROUPS)])]
  transfers between devices with their start and end apart: 7 -> 8, of which waited for: 3 -> 3; matrix products, arithmetic and copies ran while one was open for 5% -> 5% of each run, Pallas kernels for 10% -> 7%
where the time goes in v3:
time: 137 us; the launch traced here: 136 us
  Pallas kernels  51.9 us (38%)
  blocking collectives  45.1 us (33%)
  starting transfers between devices  20.6 us (15%)
  other arithmetic  7.8 us (6%)
  waiting for transfers between devices  4.54 us (3%)
  local copies, waits for them, and re-layouts  3.09 us (2%)
  matrix products  2.13 us (2%)
    all_to_all x1, blocking collectives, shards(): lax.all_to_all(terms, 'shard', split_axis=0, concat_axis=0, tiled=True)  45.1 us
    pallas_call x1, Pallas kernels, pair_terms(): pl.pallas_call(pair_kernel, out_shape=(jax.ShapeDtypeStruct(shape, F32),...  42.9 us
    all_to_all x1, starting transfers between devices, shards(): lax.all_to_all(sent + codes, 'shard', split_axis=0, concat_axis=0, tiled=...  10.5 us
    ppermute x7, starting transfers between devices, swapped(): return lax.ppermute(x, 'blk', [(i, i ^ by) for i in range(GROUPS)])  10.1 us
    pallas_call x1, Pallas kernels, tower_vectors(): pl.pallas_call(tower_kernel, grid=(OWN // blocks,), in_specs=[pl.BlockSpe...  9 us
    ppermute x7, waiting for transfers between devices, swapped(): return lax.ppermute(x, 'blk', [(i, i ^ by) for i in range(GROUPS)])  3.12 us
  transfers between devices with their start and end apart: 8, of which 3 were waited for; matrix products, arithmetic and copies ran while one was open for 5% of the time, Pallas kernels for 7%

profile of v3, /device:TPU:1, one launch (start us, length us, event | category | flops | bytes accessed | tf_op | source)
XLA Modules:
  0.0 136.0 jit_solution(17203343571754651536)
XLA Ops:
  0.7 0.8 fusion.10
  1.5 0.8 fusion
  2.5 0.1 copy.51
  2.7 2.6 %collective-permute-start.2 = (bf16[48,64]{0,1:T(8,128)(2,1)S(1)}, bf16[48,64]{0,1:T(8,128)(2,1)S(1)}, u32[]{:S(2)}, u32[]{:S(2)}) collective-permute-start(bf16[48,64]{0,1:T(8,128)(2,1)S(1)} %pad_maximum_fusion.1), channel_id=1, source_target_pairs={{0,96},{32,64},{64,32},{96,0},{1,97},{33,65},{65,33},{97,1},{2,98}... | collective-permute-start | bytes 18440 | tf_op jit(solution)/shard_map/ppermute | solution.py:29
  5.3 0.2 collective-permute-start.1
  5.5 0.3 collective-permute-start
  5.8 0.9 convert_reduce_fusion.1
  6.7 0.7 iota_compare_fusion.4
  7.5 0.7 broadcast_add_fusion
  8.2 0.1 fusion.6
  8.3 0.1 copy.53
  8.7 0.1 concatenate.45
  9.0 1.0 pad_add_fusion
  10.0 10.5 %all-to-all-start = ((bf16[32,80,128]{2,1,0:T(8,128)(2,1)}), bf16[32,80,128]{2,1,0:T(8,128)(2,1)S(1)}, u32[]{:S(2)}, u32[]{:S(2)}) async-start(bf16[32,80,128]{2,1,0:T(8,128)(2,1)} %pad_add_fusion), calls=%async_computation | async-start | bytes 1310720 | tf_op jit(solution)/shard_map/all_to_all | solution.py:396
  20.5 1.3 copy.55
  21.8 0.7 copy.57.gate_out
  22.6 9.0 %tower.1.vt_any = bf16[32,64,1024]{2,1,0:T(8,128)(2,1)} custom-call(bf16[512,1024]{1,0:T(8,128)(2,1)} %bitcast.39, bf16[4096,1024]{1,0:T(8,128)(2,1)} %features_any.1), custom_call_target="tpu_custom_call" | custom-call | flops 4294967296 | bytes 13631488 | tf_op jit(solution)/shard_map/tower/pallas_call | solution.py:46
  31.6 1.4 %all-to-all-done.arrived_any = bf16[32,80,128]{2,1,0:T(8,128)(2,1)S(1)} async-done(((bf16[32,80,128]{2,1,0:T(8,128)(2,1)}), bf16[32,80,128]{2,1,0:T(8,128)(2,1)S(1)}, u32[]{:S(2)}, u32[]{:S(2)}) %all-to-all-start) | async-done | bytes 655392 | tf_op jit(solution)/shard_map/all_to_all | solution.py:396
  33.0 0.8 slice_convert_fusion
  33.9 42.9 %pairs.1 = (f32[32,24,512]{2,1,0:T(8,128)}, bf16[32,24,512]{2,1,0:T(8,128)(2,1)}) custom-call(s32[32,4]{1,0:T(8,128)} %bitcast.44, s32[1]{0:T(128)} %bitcast.5.group, bf16[32,80,128]{2,1,0:T(8,128)(2,1)} %copy-done.2, bf16[32,64,1024]{2,1,0:T(8,128)(2,1)} %tower.1.vt_any, bf16[4096,1024]{1,0:T(8,128)(2,1)} %features_any.1, bf16[64,128]{1,0:T(8,128)(2,1)} %gate_in.1, ...), custom_call_target="tpu_custom_call" | custom-call | flops 42949672960 | bytes 16777216 | tf_op jit(solution)/shard_map/pairs/pallas_call | solution.py:299
  76.8 2.8 %collective-permute-start.3 = (bf16[32,24,512]{2,1,0:T(8,128)(2,1)}, bf16[32,24,512]{2,1,0:T(8,128)(2,1)S(1)}, u32[]{:S(2)}, u32[]{:S(2)}) collective-permute-start(bf16[32,24,512]{2,1,0:T(8,128)(2,1)} %get-tuple-element.5), channel_id=1, source_target_pairs={{0,32},{32,0},{64,96},{96,64},{1,33},{33,1},{65,97},{97,65},{2,34}... | collective-permute-start | bytes 2359304 | tf_op jit(solution)/shard_map/ppermute | solution.py:29
  79.6 2.1 %collective-permute-done.3 = bf16[32,24,512]{2,1,0:T(8,128)(2,1)S(1)} collective-permute-done((bf16[32,24,512]{2,1,0:T(8,128)(2,1)}, bf16[32,24,512]{2,1,0:T(8,128)(2,1)S(1)}, u32[]{:S(2)}, u32[]{:S(2)}) %collective-permute-start.3) | collective-permute-done | bytes 786464 | tf_op jit(solution)/shard_map/ppermute | solution.py:29
  81.7 1.7 %add_convert_fusion = bf16[32,24,512]{2,1,0:T(8,128)(2,1)S(1)} fusion(f32[32,24,512]{2,1,0:T(8,128)} %get-tuple-element.4, bf16[32,24,512]{2,1,0:T(8,128)(2,1)S(1)} %collective-permute-done.3), kind=kLoop, calls=%fused_computation.1 | loop fusion | flops 1179648 | bytes 3145728 | tf_op jit(solution)/shard_map/convert_element_type | solution.py:402
  83.4 45.1 %all_to_all.10 = bf16[32,24,512]{2,1,0:T(8,128)(2,1)S(1)} all-to-all(bf16[32,24,512]{2,1,0:T(8,128)(2,1)S(1)} %add_convert_fusion), channel_id=1, replica_groups=mesh['blk'=4,'shard'=32] {'shard'}, dimensions={0} | all-to-all | bytes 1572864 | tf_op jit(solution)/shard_map/all_to_all | solution.py:403
  128.5 0.1 convert_reduce_fusion
  128.6 0.4 collective-permute-start.4
  129.0 2.8 %collective-permute-start.5 = (f32[16,512]{1,0:T(8,128)S(1)}, f32[16,512]{1,0:T(8,128)S(1)}, u32[]{:S(2)}, u32[]{:S(2)}) collective-permute-start(f32[16,512]{1,0:T(8,128)S(1)} %slice.85), channel_id=1, source_target_pairs={{0,32},{32,0},{64,96},{96,64},{1,33},{33,1},{65,97},{97,65},{2,34}... | collective-permute-start | bytes 98312 | tf_op jit(solution)/shard_map/ppermute | solution.py:29
  131.8 1.0 collective-permute-start.6
  133.0 0.3 fusion.13
  133.3 1.0 convolution_add_fusion
  134.3 1.0 collective-permute-done.6
  135.3 0.6 pad_maximum_fusion
  (33 shorter events, 1.0 us)
Async XLA Ops:
  0.6 0.9 copy-start
  0.6 19.9 %copy-start.1 = (bf16[1024,512]{1,0:T(8,128)(2,1)S(1)}, bf16[1024,512]{1,0:T(8,128)(2,1)}, u32[]{:S(2)}) copy-start(bf16[1024,512]{1,0:T(8,128)(2,1)} %param.12) | copy-start | bytes 3145732
  2.7 5.8 %collective-permute-start.2 = (bf16[48,64]{0,1:T(8,128)(2,1)S(1)}, bf16[48,64]{0,1:T(8,128)(2,1)S(1)}, u32[]{:S(2)}, u32[]{:S(2)}) collective-permute-start(bf16[48,64]{0,1:T(8,128)(2,1)S(1)} %pad_maximum_fusion.1), channel_id=1, source_target_pairs={{0,96},{32,64},{64,32},{96,0},{1,97},{33,65},{65,33},{97,1},{2,98}... | collective-permute-start | bytes 18440 | tf_op jit(solution)/shard_map/ppermute | solution.py:29
  5.3 3.2 %collective-permute-start.1 = (bf16[48,64]{0,1:T(8,128)(2,1)S(1)}, bf16[48,64]{0,1:T(8,128)(2,1)S(1)}, u32[]{:S(2)}, u32[]{:S(2)}) collective-permute-start(bf16[48,64]{0,1:T(8,128)(2,1)S(1)} %pad_maximum_fusion.1), channel_id=1, source_target_pairs={{0,64},{32,96},{64,0},{96,32},{1,65},{33,97},{65,1},{97,33},{2,66}... | collective-permute-start | bytes 18440 | tf_op jit(solution)/shard_map/ppermute | solution.py:29
  5.5 3.1 %collective-permute-start = (bf16[48,64]{0,1:T(8,128)(2,1)S(1)}, bf16[48,64]{0,1:T(8,128)(2,1)S(1)}, u32[]{:S(2)}, u32[]{:S(2)}) collective-permute-start(bf16[48,64]{0,1:T(8,128)(2,1)S(1)} %pad_maximum_fusion.1), channel_id=1, source_target_pairs={{0,32},{32,0},{64,96},{96,64},{1,33},{33,1},{65,97},{97,65},{2,34}... | collective-permute-start | bytes 18440 | tf_op jit(solution)/shard_map/ppermute | solution.py:29
  10.0 11.9 %copy-start.3 = (bf16[128,64]{0,1:T(8,128)(2,1)S(1)}, bf16[128,64]{0,1:T(8,128)(2,1)}, u32[]{:S(2)}) copy-start(bf16[128,64]{0,1:T(8,128)(2,1)} %param.15) | copy-start | bytes 49156
  10.0 23.0 %all-to-all-start = ((bf16[32,80,128]{2,1,0:T(8,128)(2,1)}), bf16[32,80,128]{2,1,0:T(8,128)(2,1)S(1)}, u32[]{:S(2)}, u32[]{:S(2)}) async-start(bf16[32,80,128]{2,1,0:T(8,128)(2,1)} %pad_add_fusion), calls=%async_computation | async-start | bytes 1310720 | tf_op jit(solution)/shard_map/all_to_all | solution.py:396
  33.0 0.9 copy-start.2
  76.8 4.9 %collective-permute-start.3 = (bf16[32,24,512]{2,1,0:T(8,128)(2,1)}, bf16[32,24,512]{2,1,0:T(8,128)(2,1)S(1)}, u32[]{:S(2)}, u32[]{:S(2)}) collective-permute-start(bf16[32,24,512]{2,1,0:T(8,128)(2,1)} %get-tuple-element.5), channel_id=1, source_target_pairs={{0,32},{32,0},{64,96},{96,64},{1,33},{33,1},{65,97},{97,65},{2,34}... | collective-permute-start | bytes 2359304 | tf_op jit(solution)/shard_map/ppermute | solution.py:29
  83.4 49.6 %copy-start.4 = (s32[4]{0:T(128)S(1)}, s32[4]{0:T(128)}, u32[]{:S(2)}) copy-start(s32[4]{0:T(128)} %param.18) | copy-start | bytes 52
  128.6 4.2 %collective-permute-start.4 = (f32[24,512]{1,0:T(8,128)S(1)}, f32[24,512]{1,0:T(8,128)S(1)}, u32[]{:S(2)}, u32[]{:S(2)}) collective-permute-start(f32[24,512]{1,0:T(8,128)S(1)} %convert_reduce_fusion), channel_id=1, source_target_pairs={{0,64},{32,96},{64,0},{96,32},{1,65},{33,97},{65,1},{97,33},{2,66}... | collective-permute-start | bytes 147464 | tf_op jit(solution)/shard_map/ppermute | solution.py:29
  129.0 5.3 %collective-permute-start.5 = (f32[16,512]{1,0:T(8,128)S(1)}, f32[16,512]{1,0:T(8,128)S(1)}, u32[]{:S(2)}, u32[]{:S(2)}) collective-permute-start(f32[16,512]{1,0:T(8,128)S(1)} %slice.85), channel_id=1, source_target_pairs={{0,32},{32,0},{64,96},{96,64},{1,33},{33,1},{65,97},{97,65},{2,34}... | collective-permute-start | bytes 98312 | tf_op jit(solution)/shard_map/ppermute | solution.py:29
  131.8 3.5 %collective-permute-start.6 = (f32[16,512]{1,0:T(8,128)S(1)}, f32[16,512]{1,0:T(8,128)S(1)}, u32[]{:S(2)}, u32[]{:S(2)}) collective-permute-start(f32[16,512]{1,0:T(8,128)S(1)} %slice.85), channel_id=1, source_target_pairs={{0,96},{32,64},{64,32},{96,0},{1,97},{33,65},{65,33},{97,1},{2,98}... | collective-permute-start | bytes 98312 | tf_op jit(solution)/shard_map/ppermute | solution.py:29

commit v4 on v3

--- a/solution.py
+++ b/solution.py
@@ -12,6 +12,10 @@
 BLK = 128
 CAP = 2
 OWN = 32
+STAY = 16
+MOVE = 4
+MOST = 5 * CAP
+SIDE = 4
 USERS = 4
 TILE_USERS = 2
 UTAB = 128
@@ -29,48 +33,86 @@
     return lax.ppermute(x, "blk", [(i, i ^ by) for i in range(GROUPS)])
 
 
-def tower_kernel(weight_t, features, out):
-    product = lax.dot_general(
-        weight_t[...], features[...], (((1,), (1,)), ((), ())), preferred_element_type=F32
-    ).astype(BF)
-    for c in range(out.shape[0]):
-        for b in range(K):
-            out[c, :, b * BLK : (b + 1) * BLK] = product[
-                b * H : (b + 1) * H, c * BLK : (c + 1) * BLK
-            ]
-
-
-def tower_vectors(features, weight_t):
-    width = features.shape[1]
-    blocks = 8
+NEIGHBOURS = ((1, 1), (1, -1), (SIDE, 1), (SIDE, -1))
+
+
+def neighbour(shard, stride, by):
+    digit = shard // stride % SIDE
+    return shard + ((digit + by) % SIDE - digit) * stride
+
+
+def along(x, devices, stride, by):
+    pairs = [(i, neighbour(i, stride, by)) for i in range(devices)]
+    return lax.ppermute(x, "shard", pairs)
+
+
+def serving_device(owner, slot):
+    device = owner
+    for i, (stride, by) in enumerate(NEIGHBOURS):
+        here = jnp.logical_and(slot >= STAY + i * MOVE, slot < STAY + (i + 1) * MOVE)
+        device = jnp.where(here, neighbour(owner, stride, by), device)
+    return device
+
+
+def tower_kernel(weight, *refs):
+    out = refs[-1]
+    blocks = out.shape[0] // (len(refs) - 1)
+    for part, features in enumerate(refs[:-1]):
+        product = jnp.dot(features[...], weight[...], preferred_element_type=F32).astype(BF)
+        for c in range(blocks):
+            turned = product[c * BLK : (c + 1) * BLK, :].T
+            for b in range(K):
+                out[part * blocks + c, :, b * BLK : (b + 1) * BLK] = turned[
+                    b * H : (b + 1) * H, :
+                ]
+
+
+def tower_vectors(weight, stay, parts):
+    width = weight.shape[0]
+    if stay is not None:
+        blocks = 8
+        grid = (STAY // blocks,)
+        operands = [stay]
+        specs = [pl.BlockSpec((blocks * BLK, width), lambda i: (i, 0))]
+    else:
+        blocks = MOVE * len(parts)
+        grid = (1,)
+        operands = parts
+        specs = [pl.BlockSpec((MOVE * BLK, width), lambda i: (0, 0))] * len(parts)
+    total = blocks * grid[0]
     return pl.pallas_call(
         tower_kernel,
-        grid=(OWN // blocks,),
-        in_specs=[
-            pl.BlockSpec((E, width), lambda i: (0, 0)),
-            pl.BlockSpec((blocks * BLK, width), lambda i: (i, 0)),
-        ],
+        grid=grid,
+        in_specs=[pl.BlockSpec((width, E), lambda i: (0, 0))] + specs,
         out_specs=pl.BlockSpec((blocks, H, K * BLK), lambda i: (i, 0, 0)),
-        out_shape=jax.ShapeDtypeStruct((OWN, H, K * BLK), BF),
+        out_shape=jax.ShapeDtypeStruct((total, H, K * BLK), BF),
         compiler_params=pltpu.CompilerParams(vmem_limit_bytes=58 << 20),
         cost_estimate=pl.CostEstimate(
-            flops=2 * OWN * BLK * E * width, bytes_accessed=13 << 20, transcendentals=0
+            flops=2 * total * BLK * E * width, bytes_accessed=7 << 20, transcendentals=0
         ),
-        name="tower",
-    )(weight_t, features)
-
-
-def pair_kernel(codes, group, arrived_any, vt_any, features_any, gate_in, gate_in_bias,
-                gate_out, gate_out_bias, keep, send, first_half, first, second_t, second_half,
+        name="tower_stay" if stay is not None else "tower_moved",
+    )(weight, *operands)
+
+
+def pair_kernel(codes, group, arrived_any, vt_stay, vt_moved, features_stay, moved_0, moved_1,
+                moved_2, moved_3, gate_in, gate_in_bias, gate_out_t, gate_out_bias, keep, send, first_half, first, second_t, second_half,
                 bias1, bias2, arrived, vt, features, grads, deltas, total,
                 entry_slot, entry_shard, entry_start, sems, *buffers):
+    step_rows = MOVE * BLK
+    pieces = [
+        (arrived_any, arrived),
+        (vt_stay, vt.at[pl.ds(0, STAY)]),
+        (vt_moved, vt.at[pl.ds(STAY, OWN - STAY)]),
+        (features_stay.at[pl.ds(0, STAY * BLK), :], features.at[pl.ds(0, STAY * BLK), :]),
+    ] + [
+        (part, features.at[pl.ds(STAY * BLK + i * step_rows, step_rows), :])
+        for i, part in enumerate((moved_0, moved_1, moved_2, moved_3))
+    ]
     copies = [
         pltpu.make_async_copy(source, target, sems.at[i])
-        for i, (source, target) in enumerate(
-            ((arrived_any, arrived), (vt_any, vt), (features_any, features))
-        )
+        for i, (source, target) in enumerate(pieces)
     ]
-    for copy in copies:
+    for copy in copies[:3]:
         copy.start()
     owners = codes.shape[0]
     logits, hidden, slope, weights, back, pair_grad = [
@@ -79,24 +121,23 @@
     tile = TILE_USERS * BLK
     tiles = CIRCLE_USERS // TILE_USERS
 
-    def clear(position, carry):
+    def idle(position):
         entry_slot[position] = OWN
         entry_shard[position] = owners
         entry_start[position] = 0
-        return carry
-
-    lax.fori_loop(0, owners * CAP + 8, clear, 0)
-
-    def enter(position, count):
-        shard = position // CAP
-        rank = position % CAP
-        slot = codes[shard, rank]
-        entry_slot[count + 2] = jnp.where(slot >= 0, slot, OWN)
-        entry_shard[count + 2] = jnp.where(slot >= 0, shard, owners)
-        entry_start[count + 2] = codes[shard, CAP + rank] * BLK
-        return count + jnp.where(slot >= 0, 1, 0)
-
-    count = lax.fori_loop(0, owners * CAP, enter, 0)
+
+    def enter_shard(shard, count):
+        def enter(rank, position):
+            entry_slot[position + 2] = codes[shard, 1 + rank]
+            entry_shard[position + 2] = shard
+            entry_start[position + 2] = codes[shard, 1 + MOST + rank] * BLK
+            return position + 1
+
+        return lax.fori_loop(0, jnp.minimum(codes[shard, 0], MOST), enter, count)
+
+    count = lax.fori_loop(0, owners, enter_shard, 0)
+    for position in (0, 1, count + 2, count + 3, count + 4):
+        idle(position)
     grads[...] = jnp.zeros_like(grads)
     deltas[...] = jnp.zeros_like(deltas)
     lane = lax.broadcasted_iota(jnp.int32, (16, BLK), 1).astype(F32)
@@ -105,7 +146,7 @@
     order = jnp.where(column == (row & (K - 1)) * K + (row >> 3), 1.0, 0.0).astype(BF)
     across = (((1,), (1,)), ((), ()))
     turned_in = jnp.dot(order, gate_in[...], preferred_element_type=F32)
-    turned_out = lax.dot_general(order, gate_out[...], across, preferred_element_type=F32)
+    turned_out = jnp.dot(order, gate_out_t[...], preferred_element_type=F32)
     first[...] = turned_in.astype(BF)
     first_half[...] = (turned_in.T * 0.5).astype(BF)
     second_t[...] = turned_out.astype(BF)
@@ -117,8 +158,10 @@
         across,
         preferred_element_type=F32,
     )
-    copies[0].wait()
-    copies[1].wait()
+    for copy in copies[:3]:
+        copy.wait()
+    for copy in copies[3:]:
+        copy.start()
 
     def users_of(shard):
         packed = arrived[jnp.minimum(shard, owners - 1), 0 : ROWS // 2, :]
@@ -240,8 +283,9 @@
         send[:, rows:, columns] = (
             deltas[0:owners, first_row : first_row + K, :] * scaling
         ).astype(BF)
-    copies[2].wait()
-    blocks = 4
+    for copy in copies[3:]:
+        copy.wait()
+    blocks = 8
 
     def add(i, carry):
         left = jnp.concatenate(
@@ -284,9 +328,9 @@
             send[owner, 0:rows, :] = jnp.where(parity == 0, upper, lower).astype(BF)
 
 
-def pair_terms(codes, group, arrived, vt, features, gates):
+def pair_terms(codes, group, arrived, vectors, features, gates):
     owners = codes.shape[0]
-    width = features.shape[1]
+    width = features[0].shape[1]
     any_spec = pl.BlockSpec(memory_space=pl.ANY)
     columns = CIRCLE_USERS * BLK
     hidden = gates[0].shape[1]
@@ -299,7 +343,7 @@
     return pl.pallas_call(
         pair_kernel,
         out_shape=(jax.ShapeDtypeStruct(shape, F32), jax.ShapeDtypeStruct(shape, BF)),
-        in_specs=[smem] * 2 + [any_spec] * 3 + [VMEM_SPEC] * 4,
+        in_specs=[smem] * 2 + [any_spec] * 8 + [VMEM_SPEC] * 4,
         out_specs=(VMEM_SPEC, VMEM_SPEC),
         scratch_shapes=[
             pltpu.VMEM((hidden, PAIRS), BF),
@@ -309,15 +353,15 @@
             pltpu.VMEM((hidden, BLK), F32),
             pltpu.VMEM((PAIRS, BLK), F32),
             pltpu.VMEM(arrived.shape, BF),
-            pltpu.VMEM(vt.shape, BF),
-            pltpu.VMEM(features.shape, BF),
+            pltpu.VMEM((OWN, H, K * BLK), BF),
+            pltpu.VMEM((OWN * BLK, width), BF),
             pltpu.VMEM((OWN + 1, H, K * BLK), F32),
             pltpu.VMEM((owners + 1, ROWS, H), F32),
             pltpu.VMEM((E, width), F32),
-            pltpu.SMEM((owners * CAP + 8,), jnp.int32),
-            pltpu.SMEM((owners * CAP + 8,), jnp.int32),
-            pltpu.SMEM((owners * CAP + 8,), jnp.int32),
-            pltpu.SemaphoreType.DMA((3,)),
+            pltpu.SMEM((owners * MOST + 8,), jnp.int32),
+            pltpu.SMEM((owners * MOST + 8,), jnp.int32),
+            pltpu.SMEM((owners * MOST + 8,), jnp.int32),
+            pltpu.SemaphoreType.DMA((8,)),
         ]
         + twice((ROWS, K * BLK), F32)
         + twice((hidden, columns), BF)
@@ -330,7 +374,7 @@
             flops=40 << 30, bytes_accessed=16 << 20, transcendentals=1 << 24
         ),
         name="pairs",
-    )(codes, group, arrived, vt, features, *gates)
+    )(codes, group, arrived, *vectors, *features, *gates)
 
 
 def split_product(left_bf16, right_f32):
@@ -357,19 +401,34 @@
 ):
     owner_count = lax.axis_size("shard")
     group = lax.axis_index("blk")
+    moved = [
+        along(
+            item_features[(STAY + i * MOVE) * BLK : (STAY + (i + 1) * MOVE) * BLK],
+            owner_count,
+            stride,
+            by,
+        )
+        for i, (stride, by) in enumerate(NEIGHBOURS)
+    ]
     listings = listed_slot.shape[0]
     owner_ids = listed_owner[:, 0]
+    served_by = serving_device(owner_ids, listed_slot)
     order = jnp.arange(listings, dtype=jnp.int32)
-    same_owner = owner_ids[:, None] == owner_ids[None, :]
+    same_device = served_by[:, None] == served_by[None, :]
     earlier = order[None, :] < order[:, None]
-    rank_within = jnp.sum(jnp.logical_and(same_owner, earlier), axis=1)
-    owner_match = owner_ids[:, None] == jnp.arange(owner_count, dtype=jnp.int32)[None, :]
-    rank_match = rank_within[:, None] == jnp.arange(CAP, dtype=jnp.int32)[None, :]
-    placement = jnp.logical_and(owner_match[:, :, None], rank_match[:, None, :])
-    wanted = jnp.sum(jnp.where(placement, listed_slot[:, None, None] + 1, 0), axis=0) - 1
+    rank_within = jnp.sum(jnp.logical_and(same_device, earlier), axis=1)
+    device_match = served_by[:, None] == jnp.arange(owner_count, dtype=jnp.int32)[None, :]
     place = group * listings + order
-    wanted_place = jnp.sum(jnp.where(placement, place[:, None, None], 0), axis=0)
-    codes = jnp.concatenate([wanted, wanted_place], axis=1).astype(BF)
+    column = jnp.arange(1 + 2 * MOST, dtype=jnp.int32)[None, :]
+    value = jnp.where(
+        column == 0,
+        1,
+        jnp.where(column == 1 + rank_within[:, None], listed_slot[:, None], 0)
+        + jnp.where(column == 1 + MOST + rank_within[:, None], place[:, None], 0),
+    )
+    codes = jnp.sum(
+        jnp.where(device_match[:, :, None], value[:, None, :], 0), axis=0
+    ).astype(BF)
 
     row_match = user_ids[:, None] == jnp.arange(UTAB, dtype=jnp.int32)[None, :]
     user_rows = jnp.dot(row_match.astype(BF), user_table, preferred_element_type=F32)
@@ -391,14 +450,19 @@
     sent = jnp.broadcast_to(common[None], (owner_count,) + common.shape)
     codes = jnp.pad(
         codes[:, None, :],
-        ((0, 0), (ROWS // 2, 15), (2 * CIRCLE_USERS, 2 * H - 2 * CIRCLE_USERS - 2 * CAP)),
+        ((0, 0), (ROWS // 2, 15), (2 * CIRCLE_USERS, 2 * H - 2 * CIRCLE_USERS - 1 - 2 * MOST)),
     )
     arrived = lax.all_to_all(sent + codes, "shard", split_axis=0, concat_axis=0, tiled=True)
-    asked = arrived[:, ROWS // 2, 2 * CIRCLE_USERS : 2 * CIRCLE_USERS + 2 * CAP].astype(jnp.int32)
-
-    vt = tower_vectors(item_features, tower_weight.T)
-    gates = (gate_in, gate_in_bias[None, :], gate_out, gate_out_bias[None, :])
-    keep, send = pair_terms(asked, group[None], arrived, vt, item_features, gates)
+    asked = arrived[:, ROWS // 2, 2 * CIRCLE_USERS : 2 * CIRCLE_USERS + 1 + 2 * MOST].astype(jnp.int32)
+
+    vectors = (
+        tower_vectors(tower_weight, item_features, None),
+        tower_vectors(tower_weight, None, moved),
+    )
+    gates = (gate_in, gate_in_bias[None, :], gate_out.T, gate_out_bias[None, :])
+    keep, send = pair_terms(
+        asked, group[None], arrived, vectors, (item_features, *moved), gates
+    )
     terms = (keep + swapped(send, 1).astype(F32)).astype(BF)
     terms = lax.all_to_all(terms, "shard", split_axis=0, concat_axis=0, tiled=True)
     sums = jnp.sum(terms.astype(F32), axis=0)

time: 137 us -> 138 us (level); the launches traced: 136 us -> 139 us
  Pallas kernels: 51.9 us -> 35.7 us
  waiting for transfers between devices: 4.54 us -> 20.2 us
  starting transfers between devices: 20.6 us -> 22.4 us
  local copies, waits for them, and re-layouts: 3.09 us -> 4.68 us
  blocking collectives: 45.1 us -> 46.6 us
  other arithmetic: 7.8 us -> 6.41 us
    pallas_call x1, Pallas kernels: 42.9 us -> 23.9 us  [pair_terms(): pl.pallas_call(pair_kernel, out_shape=(jax.ShapeDtypeStruct(shape, F32),...]
    all_to_all x1, waiting for transfers between devices: 1.43 us -> 17.4 us  [shards(): lax.all_to_all(sent + codes, 'shard', split_axis=0, concat_axis=0, tiled=...]
    ppermute x0 -> x4, starting transfers between devices: none -> 6.59 us  [along(): return lax.ppermute(x, 'shard', pairs)]
    all_to_all x1, starting transfers between devices: 10.5 us -> 6.92 us  [shards(): lax.all_to_all(sent + codes, 'shard', split_axis=0, concat_axis=0, tiled=...]
    slice x0 -> x1, local copies, waits for them, and re-layouts: none -> 3.58 us  [shards(): item_features[(STAY + i * MOVE) * BLK:(STAY + (i + 1) * MOVE) * BLK]]
    pallas_call x1 -> x2, Pallas kernels: 9 us -> 11.7 us  [tower_vectors(): pl.pallas_call(tower_kernel, grid=grid, in_specs=[pl.BlockSpec((width, E)...]
    unnamed x12 -> x8, local copies, waits for them, and re-layouts: 2.19 us -> 0.21 us
    all_to_all x1, blocking collectives: 45.1 us -> 46.6 us  [shards(): lax.all_to_all(terms, 'shard', split_axis=0, concat_axis=0, tiled=True)]
  transfers between devices with their start and end apart: 8 -> 12, of which waited for: 3 -> 3; matrix products, arithmetic and copies ran while one was open for 5% -> 6% of each run, Pallas kernels for 7% -> 4%
where the time goes in v4:
time: 138 us; the launch traced here: 139 us
  blocking collectives  46.6 us (34%)
  Pallas kernels  35.7 us (26%)
  starting transfers between devices  22.4 us (16%)
  waiting for transfers between devices  20.2 us (15%)
  other arithmetic  6.41 us (5%)
  local copies, waits for them, and re-layouts  4.68 us (3%)
  matrix products  2.13 us (2%)
    all_to_all x1, blocking collectives, shards(): lax.all_to_all(terms, 'shard', split_axis=0, concat_axis=0, tiled=True)  46.6 us
    pallas_call x1, Pallas kernels, pair_terms(): pl.pallas_call(pair_kernel, out_shape=(jax.ShapeDtypeStruct(shape, F32),...  23.9 us
    all_to_all x1, waiting for transfers between devices, shards(): lax.all_to_all(sent + codes, 'shard', split_axis=0, concat_axis=0, tiled=...  17.4 us
    pallas_call x2, Pallas kernels, tower_vectors(): pl.pallas_call(tower_kernel, grid=grid, in_specs=[pl.BlockSpec((width, E)...  11.7 us
    ppermute x7, starting transfers between devices, swapped(): return lax.ppermute(x, 'blk', [(i, i ^ by) for i in range(GROUPS)])  8.93 us
    all_to_all x1, starting transfers between devices, shards(): lax.all_to_all(sent + codes, 'shard', split_axis=0, concat_axis=0, tiled=...  6.92 us
    ppermute x4, starting transfers between devices, along(): return lax.ppermute(x, 'shard', pairs)  6.59 us
    slice x1, local copies, waits for them, and re-layouts, shards(): item_features[(STAY + i * MOVE) * BLK:(STAY + (i + 1) * MOVE) * BLK]  3.58 us
  transfers between devices with their start and end apart: 12, of which 3 were waited for; matrix products, arithmetic and copies ran while one was open for 6% of the time, Pallas kernels for 4%

profile of v4, /device:TPU:1, one launch (start us, length us, event | category | flops | bytes accessed | tf_op | source)
XLA Modules:
  0.0 139.0 jit_solution(12255151400424048344)
XLA Ops:
  0.6 0.7 fusion.8
  1.4 0.2 copy-done
  1.6 0.8 fusion
  2.7 2.7 %collective-permute-start.2 = (bf16[48,64]{0,1:T(8,128)(2,1)S(1)}, bf16[48,64]{0,1:T(8,128)(2,1)S(1)}, u32[]{:S(2)}, u32[]{:S(2)}) collective-permute-start(bf16[48,64]{0,1:T(8,128)(2,1)S(1)} %pad_maximum_fusion.1), channel_id=1, source_target_pairs={{0,96},{32,64},{64,32},{96,0},{1,97},{33,65},{65,33},{97,1},{2,98}... | collective-permute-start | bytes 18440 | tf_op jit(solution)/shard_map/ppermute | solution.py:33
  5.4 0.2 collective-permute-start.1
  5.5 0.3 collective-permute-start
  5.9 3.6 %fusion.27 = (bf16[512,1024]{1,0:T(8,128)(2,1)S(1)}, bf16[512,1024]{1,0:T(8,128)(2,1)S(1)}, bf16[512,1024]{1,0:T(8,128)(2,1)S(1)}, bf16[512,1024]{1,0:T(8,128)(2,1)}) fusion(bf16[4096,1024]{1,0:T(8,128)(2,1)} %features_stay.1), kind=kLoop, calls=%fused_computation.91 | loop fusion | bytes 8388608 | tf_op jit(solution)/shard_map/slice | solution.py:406
  9.4 1.6 %collective-permute-start.3 = (bf16[512,1024]{1,0:T(8,128)(2,1)}, bf16[512,1024]{1,0:T(8,128)(2,1)}, u32[]{:S(2)}, u32[]{:S(2)}) collective-permute-start(bf16[512,1024]{1,0:T(8,128)(2,1)} %get-tuple-element.9), channel_id=1, source_target_pairs={{0,1},{1,2},{2,3},{3,0},{4,5},{5,6},{6,7},{7,4},{8,9},{9,10},{10,1... | collective-permute-start | bytes 3145736 | tf_op jit(solution)/shard_map/ppermute | solution.py:46
  11.1 2.1 %collective-permute-start.4 = (bf16[512,1024]{1,0:T(8,128)(2,1)S(1)}, bf16[512,1024]{1,0:T(8,128)(2,1)}, u32[]{:S(2)}, u32[]{:S(2)}) collective-permute-start(bf16[512,1024]{1,0:T(8,128)(2,1)S(1)} %get-tuple-element.8), channel_id=1, source_target_pairs={{0,3},{1,0},{2,1},{3,2},{4,7},{5,4},{6,5},{7,6},{8,11},{9,8},{10,9... | collective-permute-start | bytes 3145736 | tf_op jit(solution)/shard_map/ppermute | solution.py:46
  13.3 0.2 convert_reduce_fusion.1
  13.6 0.1 select_reduce_fusion
  13.7 0.1 copy.24
  13.8 1.4 collective-permute-start.5
  15.3 1.5 %collective-permute-start.6 = (bf16[512,1024]{1,0:T(8,128)(2,1)S(1)}, bf16[512,1024]{1,0:T(8,128)(2,1)}, u32[]{:S(2)}, u32[]{:S(2)}) collective-permute-start(bf16[512,1024]{1,0:T(8,128)(2,1)S(1)} %get-tuple-element.6), channel_id=1, source_target_pairs={{0,12},{1,13},{2,14},{3,15},{4,0},{5,1},{6,2},{7,3},{8,4},{9,5},{1... | collective-permute-start | bytes 3145736 | tf_op jit(solution)/shard_map/ppermute | solution.py:46
  16.9 0.1 concatenate.30
  17.2 1.0 pad_add_fusion
  18.2 6.9 %all-to-all-start = ((bf16[32,80,128]{2,1,0:T(8,128)(2,1)}), bf16[32,80,128]{2,1,0:T(8,128)(2,1)}, u32[]{:S(2)}, u32[]{:S(2)}) async-start(bf16[32,80,128]{2,1,0:T(8,128)(2,1)} %pad_add_fusion), calls=%async_computation | async-start | bytes 1310720 | tf_op jit(solution)/shard_map/all_to_all | solution.py:455
  25.1 5.5 %tower_stay.1.vt_stay = bf16[16,64,1024]{2,1,0:T(8,128)(2,1)} custom-call(bf16[1024,512]{1,0:T(8,128)(2,1)} %weight.3, bf16[4096,1024]{1,0:T(8,128)(2,1)} %features_stay.1), custom_call_target="tpu_custom_call" | custom-call | flops 2147483648 | bytes 7340032 | tf_op jit(solution)/shard_map/tower_stay/pallas_call | solution.py:83
  30.6 17.4 %all-to-all-done.arrived_any = bf16[32,80,128]{2,1,0:T(8,128)(2,1)} async-done(((bf16[32,80,128]{2,1,0:T(8,128)(2,1)}), bf16[32,80,128]{2,1,0:T(8,128)(2,1)}, u32[]{:S(2)}, u32[]{:S(2)}) %all-to-all-start) | async-done | bytes 655392 | tf_op jit(solution)/shard_map/all_to_all | solution.py:455
  48.1 1.5 %slice_convert_fusion = s32[32,1,21]{2,1,0:T(1,128)} fusion(bf16[32,80,128]{2,1,0:T(8,128)(2,1)} %all-to-all-done.arrived_any), kind=kLoop, calls=%fused_computation.16 | loop fusion | flops 672 | bytes 4032 | tf_op jit(solution)/shard_map/convert_element_type | solution.py:456
  49.6 6.2 %tower_moved.1.vt_moved = bf16[16,64,1024]{2,1,0:T(8,128)(2,1)} custom-call(bf16[1024,512]{1,0:T(8,128)(2,1)} %weight.3, bf16[512,1024]{1,0:T(8,128)(2,1)} %collective-permute-done.3.refs_0_.moved_0, bf16[512,1024]{1,0:T(8,128)(2,1)} %collective-permute-done.4.refs_1_.moved_1, bf16[512,1024]{1,0:T(8,128)(2,1)} %collective-permute-done.5.refs_2_.moved_2, ...), custom_call_target="tpu_custom_call" | custom-call | flops 2147483648 | bytes 7340032 | tf_op jit(solution)/shard_map/tower_moved/pallas_call | solution.py:83
  55.9 23.9 %pairs.1 = (f32[32,24,512]{2,1,0:T(8,128)}, bf16[32,24,512]{2,1,0:T(8,128)(2,1)}) custom-call(s32[32,21]{1,0:T(8,128)} %bitcast.60, s32[1]{0:T(128)} %bitcast.4.group, bf16[32,80,128]{2,1,0:T(8,128)(2,1)} %all-to-all-done.arrived_any, bf16[16,64,1024]{2,1,0:T(8,128)(2,1)} %tower_stay.1.vt_stay, bf16[16,64,1024]{2,1,0:T(8,128)(2,1)} %tower_moved.1.vt_moved, ...), custom_call_target="tpu_custom_call" | custom-call | flops 42949672960 | bytes 16777216 | tf_op jit(solution)/shard_map/pairs/pallas_call | solution.py:343
  79.8 2.0 %collective-permute-start.7 = (bf16[32,24,512]{2,1,0:T(8,128)(2,1)}, bf16[32,24,512]{2,1,0:T(8,128)(2,1)S(1)}, u32[]{:S(2)}, u32[]{:S(2)}) collective-permute-start(bf16[32,24,512]{2,1,0:T(8,128)(2,1)} %get-tuple-element.5), channel_id=1, source_target_pairs={{0,32},{32,0},{64,96},{96,64},{1,33},{33,1},{65,97},{97,65},{2,34}... | collective-permute-start | bytes 2359304 | tf_op jit(solution)/shard_map/ppermute | solution.py:33
  81.8 2.1 %collective-permute-done.7 = bf16[32,24,512]{2,1,0:T(8,128)(2,1)S(1)} collective-permute-done((bf16[32,24,512]{2,1,0:T(8,128)(2,1)}, bf16[32,24,512]{2,1,0:T(8,128)(2,1)S(1)}, u32[]{:S(2)}, u32[]{:S(2)}) %collective-permute-start.7) | collective-permute-done | bytes 786464 | tf_op jit(solution)/shard_map/ppermute | solution.py:33
  83.9 1.7 %add_convert_fusion = bf16[32,24,512]{2,1,0:T(8,128)(2,1)S(1)} fusion(f32[32,24,512]{2,1,0:T(8,128)} %get-tuple-element.4, bf16[32,24,512]{2,1,0:T(8,128)(2,1)S(1)} %collective-permute-done.7), kind=kLoop, calls=%fused_computation.1 | loop fusion | flops 1179648 | bytes 3145728 | tf_op jit(solution)/shard_map/convert_element_type | solution.py:466
  85.7 46.6 %all_to_all.10 = bf16[32,24,512]{2,1,0:T(8,128)(2,1)S(1)} all-to-all(bf16[32,24,512]{2,1,0:T(8,128)(2,1)S(1)} %add_convert_fusion), channel_id=1, replica_groups=mesh['blk'=4,'shard'=32] {'shard'}, dimensions={0} | all-to-all | bytes 1572864 | tf_op jit(solution)/shard_map/all_to_all | solution.py:467
  132.3 0.1 convert_reduce_fusion
  132.5 3.7 %collective-permute-start.10 = (f32[16,512]{1,0:T(8,128)S(1)}, f32[16,512]{1,0:T(8,128)S(1)}, u32[]{:S(2)}, u32[]{:S(2)}) collective-permute-start(f32[16,512]{1,0:T(8,128)S(1)} %slice.101), channel_id=1, source_target_pairs={{0,96},{32,64},{64,32},{96,0},{1,97},{33,65},{65,33},{97,1},{2,98}... | collective-permute-start | bytes 98312 | tf_op jit(solution)/shard_map/ppermute | solution.py:33
  136.4 0.3 fusion.11
  136.7 1.0 convolution_add_fusion
  137.7 0.6 collective-permute-done.10
  138.3 0.6 pad_maximum_fusion
  (39 shorter events, 1.2 us)
Async XLA Ops:
  0.6 0.9 copy-start
  2.7 10.5 %copy-start.2 = (s32[14]{0:T(128)S(1)}, s32[14]{0:T(128)}, u32[]{:S(2)}) copy-start(s32[14]{0:T(128)} %param.21) | copy-start | bytes 172
  2.7 10.5 %copy-start.3 = (s32[14,1]{0,1:T(1,128)S(1)}, s32[14,1]{0,1:T(1,128)}, u32[]{:S(2)}) copy-start(s32[14,1]{0,1:T(1,128)} %param.20) | copy-start | bytes 172
  2.7 11.1 %collective-permute-start.2 = (bf16[48,64]{0,1:T(8,128)(2,1)S(1)}, bf16[48,64]{0,1:T(8,128)(2,1)S(1)}, u32[]{:S(2)}, u32[]{:S(2)}) collective-permute-start(bf16[48,64]{0,1:T(8,128)(2,1)S(1)} %pad_maximum_fusion.1), channel_id=1, source_target_pairs={{0,96},{32,64},{64,32},{96,0},{1,97},{33,65},{65,33},{97,1},{2,98}... | collective-permute-start | bytes 18440 | tf_op jit(solution)/shard_map/ppermute | solution.py:33
  5.4 9.9 %collective-permute-start.1 = (bf16[48,64]{0,1:T(8,128)(2,1)S(1)}, bf16[48,64]{0,1:T(8,128)(2,1)S(1)}, u32[]{:S(2)}, u32[]{:S(2)}) collective-permute-start(bf16[48,64]{0,1:T(8,128)(2,1)S(1)} %pad_maximum_fusion.1), channel_id=1, source_target_pairs={{0,64},{32,96},{64,0},{96,32},{1,65},{33,97},{65,1},{97,33},{2,66}... | collective-permute-start | bytes 18440 | tf_op jit(solution)/shard_map/ppermute | solution.py:33
  5.5 11.3 %collective-permute-start = (bf16[48,64]{0,1:T(8,128)(2,1)S(1)}, bf16[48,64]{0,1:T(8,128)(2,1)S(1)}, u32[]{:S(2)}, u32[]{:S(2)}) collective-permute-start(bf16[48,64]{0,1:T(8,128)(2,1)S(1)} %pad_maximum_fusion.1), channel_id=1, source_target_pairs={{0,32},{32,0},{64,96},{96,64},{1,33},{33,1},{65,97},{97,65},{2,34}... | collective-permute-start | bytes 18440 | tf_op jit(solution)/shard_map/ppermute | solution.py:33
  9.4 40.2 %collective-permute-start.3 = (bf16[512,1024]{1,0:T(8,128)(2,1)}, bf16[512,1024]{1,0:T(8,128)(2,1)}, u32[]{:S(2)}, u32[]{:S(2)}) collective-permute-start(bf16[512,1024]{1,0:T(8,128)(2,1)} %get-tuple-element.9), channel_id=1, source_target_pairs={{0,1},{1,2},{2,3},{3,0},{4,5},{5,6},{6,7},{7,4},{8,9},{9,10},{10,1... | collective-permute-start | bytes 3145736 | tf_op jit(solution)/shard_map/ppermute | solution.py:46
  11.1 38.5 %collective-permute-start.4 = (bf16[512,1024]{1,0:T(8,128)(2,1)S(1)}, bf16[512,1024]{1,0:T(8,128)(2,1)}, u32[]{:S(2)}, u32[]{:S(2)}) collective-permute-start(bf16[512,1024]{1,0:T(8,128)(2,1)S(1)} %get-tuple-element.8), channel_id=1, source_target_pairs={{0,3},{1,0},{2,1},{3,2},{4,7},{5,4},{6,5},{7,6},{8,11},{9,8},{10,9... | collective-permute-start | bytes 3145736 | tf_op jit(solution)/shard_map/ppermute | solution.py:46
  13.8 35.8 %collective-permute-start.5 = (bf16[512,1024]{1,0:T(8,128)(2,1)S(1)}, bf16[512,1024]{1,0:T(8,128)(2,1)}, u32[]{:S(2)}, u32[]{:S(2)}) collective-permute-start(bf16[512,1024]{1,0:T(8,128)(2,1)S(1)} %get-tuple-element.7), channel_id=1, source_target_pairs={{0,4},{1,5},{2,6},{3,7},{4,8},{5,9},{6,10},{7,11},{8,12},{9,13},{1... | collective-permute-start | bytes 3145736 | tf_op jit(solution)/shard_map/ppermute | solution.py:46
  15.3 34.3 %collective-permute-start.6 = (bf16[512,1024]{1,0:T(8,128)(2,1)S(1)}, bf16[512,1024]{1,0:T(8,128)(2,1)}, u32[]{:S(2)}, u32[]{:S(2)}) collective-permute-start(bf16[512,1024]{1,0:T(8,128)(2,1)S(1)} %get-tuple-element.6), channel_id=1, source_target_pairs={{0,12},{1,13},{2,14},{3,15},{4,0},{5,1},{6,2},{7,3},{8,4},{9,5},{1... | collective-permute-start | bytes 3145736 | tf_op jit(solution)/shard_map/ppermute | solution.py:46
  18.2 29.9 %all-to-all-start = ((bf16[32,80,128]{2,1,0:T(8,128)(2,1)}), bf16[32,80,128]{2,1,0:T(8,128)(2,1)}, u32[]{:S(2)}, u32[]{:S(2)}) async-start(bf16[32,80,128]{2,1,0:T(8,128)(2,1)} %pad_add_fusion), calls=%async_computation | async-start | bytes 1310720 | tf_op jit(solution)/shard_map/all_to_all | solution.py:455
  79.8 4.1 %collective-permute-start.7 = (bf16[32,24,512]{2,1,0:T(8,128)(2,1)}, bf16[32,24,512]{2,1,0:T(8,128)(2,1)S(1)}, u32[]{:S(2)}, u32[]{:S(2)}) collective-permute-start(bf16[32,24,512]{2,1,0:T(8,128)(2,1)} %get-tuple-element.5), channel_id=1, source_target_pairs={{0,32},{32,0},{64,96},{96,64},{1,33},{33,1},{65,97},{97,65},{2,34}... | collective-permute-start | bytes 2359304 | tf_op jit(solution)/shard_map/ppermute | solution.py:33
  85.7 50.7 %copy-start.1 = (s32[4]{0:T(128)S(1)}, s32[4]{0:T(128)}, u32[]{:S(2)}) copy-start(s32[4]{0:T(128)} %param.18) | copy-start | bytes 52
  132.4 3.8 %collective-permute-start.8 = (f32[24,512]{1,0:T(8,128)S(1)}, f32[24,512]{1,0:T(8,128)S(1)}, u32[]{:S(2)}, u32[]{:S(2)}) collective-permute-start(f32[24,512]{1,0:T(8,128)S(1)} %convert_reduce_fusion), channel_id=1, source_target_pairs={{0,64},{32,96},{64,0},{96,32},{1,65},{33,97},{65,1},{97,33},{2,66}... | collective-permute-start | bytes 147464 | tf_op jit(solution)/shard_map/ppermute | solution.py:33
  132.5 5.8 %collective-permute-start.10 = (f32[16,512]{1,0:T(8,128)S(1)}, f32[16,512]{1,0:T(8,128)S(1)}, u32[]{:S(2)}, u32[]{:S(2)}) collective-permute-start(f32[16,512]{1,0:T(8,128)S(1)} %slice.101), channel_id=1, source_target_pairs={{0,96},{32,64},{64,32},{96,0},{1,97},{33,65},{65,33},{97,1},{2,98}... | collective-permute-start | bytes 98312 | tf_op jit(solution)/shard_map/ppermute | solution.py:33
  136.2 2.1 %collective-permute-start.9 = (f32[16,512]{1,0:T(8,128)S(1)}, f32[16,512]{1,0:T(8,128)S(1)}, u32[]{:S(2)}, u32[]{:S(2)}) collective-permute-start(f32[16,512]{1,0:T(8,128)S(1)} %slice.101), channel_id=1, source_target_pairs={{0,32},{32,0},{64,96},{96,64},{1,33},{33,1},{65,97},{97,65},{2,34}... | collective-permute-start | bytes 98312 | tf_op jit(solution)/shard_map/ppermute | solution.py:33

commit v5 on v4

--- a/solution.py
+++ b/solution.py
@@ -14,6 +14,7 @@
 OWN = 32
 STAY = 16
 MOVE = 4
+HALF = MOVE // 2
 MOST = 5 * CAP
 SIDE = 4
 USERS = 4
@@ -75,10 +76,10 @@
         operands = [stay]
         specs = [pl.BlockSpec((blocks * BLK, width), lambda i: (i, 0))]
     else:
-        blocks = MOVE * len(parts)
+        blocks = HALF * len(parts)
         grid = (1,)
         operands = parts
-        specs = [pl.BlockSpec((MOVE * BLK, width), lambda i: (0, 0))] * len(parts)
+        specs = [pl.BlockSpec((HALF * BLK, width), lambda i: (0, 0))] * len(parts)
     total = blocks * grid[0]
     return pl.pallas_call(
         tower_kernel,
@@ -95,10 +96,11 @@
 
 
 def pair_kernel(codes, group, arrived_any, vt_stay, vt_moved, features_stay, moved_0, moved_1,
-                moved_2, moved_3, gate_in, gate_in_bias, gate_out_t, gate_out_bias, keep, send, first_half, first, second_t, second_half,
+                moved_2, moved_3, moved_4, moved_5, moved_6, moved_7, gate_in, gate_in_bias, gate_out_t, gate_out_bias, keep, send, first_half, first, second_t, second_half,
                 bias1, bias2, arrived, vt, features, grads, deltas, total,
                 entry_slot, entry_shard, entry_start, sems, *buffers):
-    step_rows = MOVE * BLK
+    step_rows = HALF * BLK
+    moved = (moved_0, moved_1, moved_2, moved_3, moved_4, moved_5, moved_6, moved_7)
     pieces = [
         (arrived_any, arrived),
         (vt_stay, vt.at[pl.ds(0, STAY)]),
@@ -106,7 +108,7 @@
         (features_stay.at[pl.ds(0, STAY * BLK), :], features.at[pl.ds(0, STAY * BLK), :]),
     ] + [
         (part, features.at[pl.ds(STAY * BLK + i * step_rows, step_rows), :])
-        for i, part in enumerate((moved_0, moved_1, moved_2, moved_3))
+        for i, part in enumerate(moved)
     ]
     copies = [
         pltpu.make_async_copy(source, target, sems.at[i])
@@ -128,7 +130,10 @@
 
     def enter_shard(shard, count):
         def enter(rank, position):
-            entry_slot[position + 2] = codes[shard, 1 + rank]
+            slot = codes[shard, 1 + rank]
+            upper = jnp.maximum(slot - STAY, 0) // HALF % 2
+            turn = jnp.where(upper == 0, HALF, -HALF) * (group[0] & 1)
+            entry_slot[position + 2] = slot + jnp.where(slot >= STAY, turn, 0)
             entry_shard[position + 2] = shard
             entry_start[position + 2] = codes[shard, 1 + MOST + rank] * BLK
             return position + 1
@@ -343,7 +348,7 @@
     return pl.pallas_call(
         pair_kernel,
         out_shape=(jax.ShapeDtypeStruct(shape, F32), jax.ShapeDtypeStruct(shape, BF)),
-        in_specs=[smem] * 2 + [any_spec] * 8 + [VMEM_SPEC] * 4,
+        in_specs=[smem] * 2 + [any_spec] * 12 + [VMEM_SPEC] * 4,
         out_specs=(VMEM_SPEC, VMEM_SPEC),
         scratch_shapes=[
             pltpu.VMEM((hidden, PAIRS), BF),
@@ -361,7 +366,7 @@
             pltpu.SMEM((owners * MOST + 8,), jnp.int32),
             pltpu.SMEM((owners * MOST + 8,), jnp.int32),
             pltpu.SMEM((owners * MOST + 8,), jnp.int32),
-            pltpu.SemaphoreType.DMA((8,)),
+            pltpu.SemaphoreType.DMA((12,)),
         ]
         + twice((ROWS, K * BLK), F32)
         + twice((hidden, columns), BF)
@@ -401,15 +406,15 @@
 ):
     owner_count = lax.axis_size("shard")
     group = lax.axis_index("blk")
-    moved = [
-        along(
-            item_features[(STAY + i * MOVE) * BLK : (STAY + (i + 1) * MOVE) * BLK],
-            owner_count,
-            stride,
-            by,
-        )
-        for i, (stride, by) in enumerate(NEIGHBOURS)
-    ]
+    halves = []
+    for i, (stride, by) in enumerate(NEIGHBOURS):
+        first = (STAY + i * MOVE + group % 2 * HALF) * BLK
+        half = lax.dynamic_slice_in_dim(item_features, first, HALF * BLK, axis=0)
+        halves.append(along(half, owner_count, stride, by))
+    halves, tower_weight = lax.optimization_barrier((halves, tower_weight))
+    moved = []
+    for half in halves:
+        moved += [half, swapped(half, 1)]
     listings = listed_slot.shape[0]
     owner_ids = listed_owner[:, 0]
     served_by = serving_device(owner_ids, listed_slot)

time: 138 us -> 132 us (0.957)
  waiting for transfers between devices: 20.2 us -> 7.76 us
  starting transfers between devices: 22.4 us -> 31.7 us
  blocking collectives: 46.6 us -> 39.8 us
  Pallas kernels: 35.7 us -> 39.3 us
    all_to_all x1, waiting for transfers between devices: 17.4 us -> 0.01 us  [shards(): lax.all_to_all(sent + codes, 'shard', split_axis=0, concat_axis=0, tiled=...]
    ppermute x7 -> x11, starting transfers between devices: 8.93 us -> 16 us  [swapped(): return lax.ppermute(x, 'blk', [(i, i ^ by) for i in range(GROUPS)])]
    all_to_all x1, blocking collectives: 46.6 us -> 39.8 us  [shards(): lax.all_to_all(terms, 'shard', split_axis=0, concat_axis=0, tiled=True)]
    pallas_call x1, Pallas kernels: 23.9 us -> 27.6 us  [pair_terms(): pl.pallas_call(pair_kernel, out_shape=(jax.ShapeDtypeStruct(shape, F32),...]
    slice x1 -> x0, local copies, waits for them, and re-layouts: 3.58 us -> none  [shards(): item_features[(STAY + i * MOVE) * BLK:(STAY + (i + 1) * MOVE) * BLK]]
    ppermute x4, waiting for transfers between devices: 0.01 us -> 3.4 us  [along(): return lax.ppermute(x, 'shard', pairs)]
    all_to_all x1, starting transfers between devices: 6.92 us -> 9.05 us  [shards(): lax.all_to_all(sent + codes, 'shard', split_axis=0, concat_axis=0, tiled=...]
    unnamed x8 -> x20, local copies, waits for them, and re-layouts: 0.21 us -> 2.11 us
  transfers between devices with their start and end apart: 12 -> 16, of which waited for: 3 -> 4; matrix products, arithmetic and copies ran while one was open for 6% -> 5% of each run, Pallas kernels for 4% -> 4%
where the time goes in v5:
time: 132 us
  blocking collectives  39.8 us (30%)
  Pallas kernels  39.3 us (30%)
  starting transfers between devices  31.7 us (24%)
  waiting for transfers between devices  7.76 us (6%)
  other arithmetic  5.68 us (4%)
  local copies, waits for them, and re-layouts  4.71 us (4%)
  matrix products  2.13 us (2%)
    all_to_all x1, blocking collectives, shards(): lax.all_to_all(terms, 'shard', split_axis=0, concat_axis=0, tiled=True)  39.8 us
    pallas_call x1, Pallas kernels, pair_terms(): pl.pallas_call(pair_kernel, out_shape=(jax.ShapeDtypeStruct(shape, F32),...  27.6 us
    ppermute x11, starting transfers between devices, swapped(): return lax.ppermute(x, 'blk', [(i, i ^ by) for i in range(GROUPS)])  16 us
    pallas_call x2, Pallas kernels, tower_vectors(): pl.pallas_call(tower_kernel, grid=grid, in_specs=[pl.BlockSpec((width, E)...  11.6 us
    all_to_all x1, starting transfers between devices, shards(): lax.all_to_all(sent + codes, 'shard', split_axis=0, concat_axis=0, tiled=...  9.05 us
    ppermute x4, starting transfers between devices, along(): return lax.ppermute(x, 'shard', pairs)  6.64 us
    ppermute x11, waiting for transfers between devices, swapped(): return lax.ppermute(x, 'blk', [(i, i ^ by) for i in range(GROUPS)])  4.36 us
    ppermute x4, waiting for transfers between devices, along(): return lax.ppermute(x, 'shard', pairs)  3.4 us
  transfers between devices with their start and end apart: 16, of which 4 were waited for; matrix products, arithmetic and copies ran while one was open for 5% of the time, Pallas kernels for 4%

profile of v5, /device:TPU:1, one launch (start us, length us, event | category | flops | bytes accessed | tf_op | source)
XLA Modules:
  0.0 131.9 jit_solution(15171974280165384096)
XLA Ops:
  0.6 0.7 fusion.8
  1.4 0.2 copy-done
  1.6 0.8 fusion
  2.7 2.6 %collective-permute-start.2 = (bf16[48,64]{0,1:T(8,128)(2,1)S(1)}, bf16[48,64]{0,1:T(8,128)(2,1)S(1)}, u32[]{:S(2)}, u32[]{:S(2)}) collective-permute-start(bf16[48,64]{0,1:T(8,128)(2,1)S(1)} %pad_maximum_fusion.1), channel_id=1, source_target_pairs={{0,96},{32,64},{64,32},{96,0},{1,97},{33,65},{65,33},{97,1},{2,98}... | collective-permute-start | bytes 18440 | tf_op jit(solution)/shard_map/ppermute | solution.py:34
  5.3 0.2 collective-permute-start.1
  5.5 0.3 collective-permute-start
  5.8 1.7 %constant_dynamic-slice_fusion.3 = (bf16[256,1024]{1,0:T(8,128)(2,1)S(1)}, bf16[256,1024]{1,0:T(8,128)(2,1)S(1)}, bf16[256,1024]{1,0:T(8,128)(2,1)S(1)}, bf16[256,1024]{1,0:T(8,128)(2,1)S(1)}) fusion(bf16[4096,1024]{1,0:T(8,128)(2,1)} %features_stay.1, s32[]{:T(128)S(6)} %select_n.149, s32[]{:T(128)S(6)} %select_n.148, s32[]{:T(128)S(6)} %select_n.147, ...), kind=kLoop, calls=%fused_computation.77 | loop fusion | bytes 4194320 | tf_op jit(solution)/shard_map/dynamic_slice | solution.py:412
  7.5 2.8 %collective-permute-start.6 = (bf16[256,1024]{1,0:T(8,128)(2,1)S(1)}, bf16[256,1024]{1,0:T(8,128)(2,1)S(1)}, u32[]{:S(2)}, u32[]{:S(2)}) collective-permute-start(bf16[256,1024]{1,0:T(8,128)(2,1)S(1)} %get-tuple-element.16), channel_id=1, source_target_pairs={{0,12},{1,13},{2,14},{3,15},{4,0},{5,1},{6,2},{7,3},{8,4},{9,5},{1... | collective-permute-start | bytes 1572872 | tf_op jit(solution)/shard_map/ppermute | solution.py:47
  10.4 0.2 convert_reduce_fusion.1
  11.0 3.8 %collective-permute-start.4 = (bf16[256,1024]{1,0:T(8,128)(2,1)S(1)}, bf16[256,1024]{1,0:T(8,128)(2,1)}, u32[]{:S(2)}, u32[]{:S(2)}) collective-permute-start(bf16[256,1024]{1,0:T(8,128)(2,1)S(1)} %get-tuple-element.18), channel_id=1, source_target_pairs={{0,3},{1,0},{2,1},{3,2},{4,7},{5,4},{6,5},{7,6},{8,11},{9,8},{10,9... | collective-permute-start | bytes 1572872 | tf_op jit(solution)/shard_map/ppermute | solution.py:47
  15.4 1.0 pad_add_fusion
  16.3 9.0 %all-to-all-start = ((bf16[32,80,128]{2,1,0:T(8,128)(2,1)}), bf16[32,80,128]{2,1,0:T(8,128)(2,1)S(1)}, u32[]{:S(2)}, u32[]{:S(2)}) async-start(bf16[32,80,128]{2,1,0:T(8,128)(2,1)} %pad_add_fusion), calls=%async_computation | async-start | bytes 1310720 | tf_op jit(solution)/shard_map/all_to_all | solution.py:460
  25.5 3.3 %collective-permute-done.3.refs_0_.moved_0 = bf16[256,1024]{1,0:T(8,128)(2,1)} collective-permute-done((bf16[256,1024]{1,0:T(8,128)(2,1)S(1)}, bf16[256,1024]{1,0:T(8,128)(2,1)}, u32[]{:S(2)}, u32[]{:S(2)}) %collective-permute-start.3) | collective-permute-done | bytes 524320 | tf_op jit(solution)/shard_map/ppermute | solution.py:47
  28.8 2.2 %collective-permute-start.7 = (bf16[256,1024]{1,0:T(8,128)(2,1)}, bf16[256,1024]{1,0:T(8,128)(2,1)S(1)}, u32[]{:S(2)}, u32[]{:S(2)}) collective-permute-start(bf16[256,1024]{1,0:T(8,128)(2,1)} %collective-permute-done.3.refs_0_.moved_0), channel_id=1, source_target_pairs={{0,32},{32,0},{64,96},{96,64},{1,33},{33,1},{65,97},{97,65},{2,34}... | collective-permute-start | bytes 1572872 | tf_op jit(solution)/shard_map/ppermute | solution.py:34
  31.0 0.5 collective-permute-start.9
  31.5 5.5 %tower_stay.1.vt_stay = bf16[16,64,1024]{2,1,0:T(8,128)(2,1)} custom-call(bf16[1024,512]{1,0:T(8,128)(2,1)} %weight.1, bf16[4096,1024]{1,0:T(8,128)(2,1)} %features_stay.1), custom_call_target="tpu_custom_call" | custom-call | flops 2147483648 | bytes 7340032 | tf_op jit(solution)/shard_map/tower_stay/pallas_call | solution.py:84
  37.0 0.8 slice_convert_fusion
  37.8 0.8 copy-done.5
  38.6 0.2 copy-done.6
  38.8 0.2 copy-done.7
  38.9 0.8 copy-done.8
  39.7 6.2 %tower_moved.1.vt_moved = bf16[16,64,1024]{2,1,0:T(8,128)(2,1)} custom-call(bf16[1024,512]{1,0:T(8,128)(2,1)} %weight.1, bf16[256,1024]{1,0:T(8,128)(2,1)} %collective-permute-done.3.refs_0_.moved_0, bf16[256,1024]{1,0:T(8,128)(2,1)} %copy-done.5, bf16[256,1024]{1,0:T(8,128)(2,1)} %collective-permute-done.4.refs_2_.moved_2, bf16[256,1024]{1,0:T(8,128)(2,1)} %copy-done.6, ...), custom_call_target="tpu_custom_call" | custom-call | flops 2147483648 | bytes 7340032 | tf_op jit(solution)/shard_map/tower_moved/pallas_call | solution.py:84
  45.9 27.6 %pairs.1 = (f32[32,24,512]{2,1,0:T(8,128)}, bf16[32,24,512]{2,1,0:T(8,128)(2,1)}) custom-call(s32[32,21]{1,0:T(8,128)} %bitcast.60, s32[1]{0:T(128)} %bitcast.4.group, bf16[32,80,128]{2,1,0:T(8,128)(2,1)} %copy-done.1, bf16[16,64,1024]{2,1,0:T(8,128)(2,1)} %tower_stay.1.vt_stay, bf16[16,64,1024]{2,1,0:T(8,128)(2,1)} %tower_moved.1.vt_moved, ...), custom_call_target="tpu_custom_call" | custom-call | flops 42949672960 | bytes 16777216 | tf_op jit(solution)/shard_map/pairs/pallas_call | solution.py:348
  73.7 2.5 %collective-permute-done.11 = bf16[32,24,512]{2,1,0:T(8,128)(2,1)S(1)} collective-permute-done((bf16[32,24,512]{2,1,0:T(8,128)(2,1)}, bf16[32,24,512]{2,1,0:T(8,128)(2,1)S(1)}, u32[]{:S(2)}, u32[]{:S(2)}) %collective-permute-start.11) | collective-permute-done | bytes 786464 | tf_op jit(solution)/shard_map/ppermute | solution.py:34
  76.1 1.7 %add_convert_fusion = bf16[32,24,512]{2,1,0:T(8,128)(2,1)S(1)} fusion(f32[32,24,512]{2,1,0:T(8,128)} %get-tuple-element.14, bf16[32,24,512]{2,1,0:T(8,128)(2,1)S(1)} %collective-permute-done.11), kind=kLoop, calls=%fused_computation.1 | loop fusion | flops 1179648 | bytes 3145728 | tf_op jit(solution)/shard_map/convert_element_type | solution.py:471
  77.9 39.8 %all_to_all.10 = bf16[32,24,512]{2,1,0:T(8,128)(2,1)S(1)} all-to-all(bf16[32,24,512]{2,1,0:T(8,128)(2,1)S(1)} %add_convert_fusion), channel_id=1, replica_groups=mesh['blk'=4,'shard'=32] {'shard'}, dimensions={0} | all-to-all | bytes 1572864 | tf_op jit(solution)/shard_map/all_to_all | solution.py:472
  117.8 7.3 %collective-permute-start.12 = (f32[24,512]{1,0:T(8,128)S(1)}, f32[24,512]{1,0:T(8,128)S(1)}, u32[]{:S(2)}, u32[]{:S(2)}) collective-permute-start(f32[24,512]{1,0:T(8,128)S(1)} %convert_reduce_fusion), channel_id=1, source_target_pairs={{0,64},{32,96},{64,0},{96,32},{1,65},{33,97},{65,1},{97,33},{2,66}... | collective-permute-start | bytes 147464 | tf_op jit(solution)/shard_map/ppermute | solution.py:34
  125.2 2.8 %collective-permute-start.13 = (f32[16,512]{1,0:T(8,128)S(1)}, f32[16,512]{1,0:T(8,128)S(1)}, u32[]{:S(2)}, u32[]{:S(2)}) collective-permute-start(f32[16,512]{1,0:T(8,128)S(1)} %slice.85), channel_id=1, source_target_pairs={{0,32},{32,0},{64,96},{96,64},{1,33},{33,1},{65,97},{97,65},{2,34}... | collective-permute-start | bytes 98312 | tf_op jit(solution)/shard_map/ppermute | solution.py:34
  128.1 0.3 fusion.11
  128.4 1.0 convolution_add_fusion
  129.4 1.9 %collective-permute-done.14 = f32[16,512]{1,0:T(8,128)S(1)} collective-permute-done((f32[16,512]{1,0:T(8,128)S(1)}, f32[16,512]{1,0:T(8,128)S(1)}, u32[]{:S(2)}, u32[]{:S(2)}) %collective-permute-start.14) | collective-permute-done | bytes 32800 | tf_op jit(solution)/shard_map/ppermute | solution.py:34
  131.3 0.6 pad_maximum_fusion
  (59 shorter events, 1.8 us)
Async XLA Ops:
  0.6 0.9 copy-start
  2.7 8.3 %collective-permute-start.2 = (bf16[48,64]{0,1:T(8,128)(2,1)S(1)}, bf16[48,64]{0,1:T(8,128)(2,1)S(1)}, u32[]{:S(2)}, u32[]{:S(2)}) collective-permute-start(bf16[48,64]{0,1:T(8,128)(2,1)S(1)} %pad_maximum_fusion.1), channel_id=1, source_target_pairs={{0,96},{32,64},{64,32},{96,0},{1,97},{33,65},{65,33},{97,1},{2,98}... | collective-permute-start | bytes 18440 | tf_op jit(solution)/shard_map/ppermute | solution.py:34
  5.3 9.6 %collective-permute-start.1 = (bf16[48,64]{0,1:T(8,128)(2,1)S(1)}, bf16[48,64]{0,1:T(8,128)(2,1)S(1)}, u32[]{:S(2)}, u32[]{:S(2)}) collective-permute-start(bf16[48,64]{0,1:T(8,128)(2,1)S(1)} %pad_maximum_fusion.1), channel_id=1, source_target_pairs={{0,64},{32,96},{64,0},{96,32},{1,65},{33,97},{65,1},{97,33},{2,66}... | collective-permute-start | bytes 18440 | tf_op jit(solution)/shard_map/ppermute | solution.py:34
  5.5 9.5 %collective-permute-start = (bf16[48,64]{0,1:T(8,128)(2,1)S(1)}, bf16[48,64]{0,1:T(8,128)(2,1)S(1)}, u32[]{:S(2)}, u32[]{:S(2)}) collective-permute-start(bf16[48,64]{0,1:T(8,128)(2,1)S(1)} %pad_maximum_fusion.1), channel_id=1, source_target_pairs={{0,32},{32,0},{64,96},{96,64},{1,33},{33,1},{65,97},{97,65},{2,34}... | collective-permute-start | bytes 18440 | tf_op jit(solution)/shard_map/ppermute | solution.py:34
  5.8 4.5 %copy-start.3 = (s32[14]{0:T(128)S(1)}, s32[14]{0:T(128)}, u32[]{:S(2)}) copy-start(s32[14]{0:T(128)} %param.21) | copy-start | bytes 172
  5.8 4.5 %copy-start.9 = (s32[14,1]{0,1:T(1,128)S(1)}, s32[14,1]{0,1:T(1,128)}, u32[]{:S(2)}) copy-start(s32[14,1]{0,1:T(1,128)} %param.20) | copy-start | bytes 172
  7.5 17.9 %collective-permute-start.6 = (bf16[256,1024]{1,0:T(8,128)(2,1)S(1)}, bf16[256,1024]{1,0:T(8,128)(2,1)S(1)}, u32[]{:S(2)}, u32[]{:S(2)}) collective-permute-start(bf16[256,1024]{1,0:T(8,128)(2,1)S(1)} %get-tuple-element.16), channel_id=1, source_target_pairs={{0,12},{1,13},{2,14},{3,15},{4,0},{5,1},{6,2},{7,3},{8,4},{9,5},{1... | collective-permute-start | bytes 1572872 | tf_op jit(solution)/shard_map/ppermute | solution.py:47
  10.3 15.1 %collective-permute-start.5 = (bf16[256,1024]{1,0:T(8,128)(2,1)S(1)}, bf16[256,1024]{1,0:T(8,128)(2,1)}, u32[]{:S(2)}, u32[]{:S(2)}) collective-permute-start(bf16[256,1024]{1,0:T(8,128)(2,1)S(1)} %get-tuple-element.17), channel_id=1, source_target_pairs={{0,4},{1,5},{2,6},{3,7},{4,8},{5,9},{6,10},{7,11},{8,12},{9,13},{1... | collective-permute-start | bytes 1572872 | tf_op jit(solution)/shard_map/ppermute | solution.py:47
  11.0 14.5 %collective-permute-start.4 = (bf16[256,1024]{1,0:T(8,128)(2,1)S(1)}, bf16[256,1024]{1,0:T(8,128)(2,1)}, u32[]{:S(2)}, u32[]{:S(2)}) collective-permute-start(bf16[256,1024]{1,0:T(8,128)(2,1)S(1)} %get-tuple-element.18), channel_id=1, source_target_pairs={{0,3},{1,0},{2,1},{3,2},{4,7},{5,4},{6,5},{7,6},{8,11},{9,8},{10,9... | collective-permute-start | bytes 1572872 | tf_op jit(solution)/shard_map/ppermute | solution.py:47
  14.9 13.9 %collective-permute-start.3 = (bf16[256,1024]{1,0:T(8,128)(2,1)S(1)}, bf16[256,1024]{1,0:T(8,128)(2,1)}, u32[]{:S(2)}, u32[]{:S(2)}) collective-permute-start(bf16[256,1024]{1,0:T(8,128)(2,1)S(1)} %get-tuple-element.19), channel_id=1, source_target_pairs={{0,1},{1,2},{2,3},{3,0},{4,5},{5,6},{6,7},{7,4},{8,9},{9,10},{10,1... | collective-permute-start | bytes 1572872 | tf_op jit(solution)/shard_map/ppermute | solution.py:47
  16.3 20.6 %all-to-all-start = ((bf16[32,80,128]{2,1,0:T(8,128)(2,1)}), bf16[32,80,128]{2,1,0:T(8,128)(2,1)S(1)}, u32[]{:S(2)}, u32[]{:S(2)}) async-start(bf16[32,80,128]{2,1,0:T(8,128)(2,1)} %pad_add_fusion), calls=%async_computation | async-start | bytes 1310720 | tf_op jit(solution)/shard_map/all_to_all | solution.py:460
  25.4 11.6 %copy-start.4 = (bf16[256,1024]{1,0:T(8,128)(2,1)}, bf16[256,1024]{1,0:T(8,128)(2,1)S(1)}, u32[]{:S(2)}) copy-start(bf16[256,1024]{1,0:T(8,128)(2,1)S(1)} %collective-permute-done.6.refs_6_.moved_6) | copy-start | bytes 1572868
  28.8 9.0 %collective-permute-start.7 = (bf16[256,1024]{1,0:T(8,128)(2,1)}, bf16[256,1024]{1,0:T(8,128)(2,1)S(1)}, u32[]{:S(2)}, u32[]{:S(2)}) collective-permute-start(bf16[256,1024]{1,0:T(8,128)(2,1)} %collective-permute-done.3.refs_0_.moved_0), channel_id=1, source_target_pairs={{0,32},{32,0},{64,96},{96,64},{1,33},{33,1},{65,97},{97,65},{2,34}... | collective-permute-start | bytes 1572872 | tf_op jit(solution)/shard_map/ppermute | solution.py:34
  31.0 6.8 %collective-permute-start.8 = (bf16[256,1024]{1,0:T(8,128)(2,1)}, bf16[256,1024]{1,0:T(8,128)(2,1)S(1)}, u32[]{:S(2)}, u32[]{:S(2)}) collective-permute-start(bf16[256,1024]{1,0:T(8,128)(2,1)} %collective-permute-done.4.refs_2_.moved_2), channel_id=1, source_target_pairs={{0,32},{32,0},{64,96},{96,64},{1,33},{33,1},{65,97},{97,65},{2,34}... | collective-permute-start | bytes 1572872 | tf_op jit(solution)/shard_map/ppermute | solution.py:34
  31.0 6.9 %collective-permute-start.9 = (bf16[256,1024]{1,0:T(8,128)(2,1)}, bf16[256,1024]{1,0:T(8,128)(2,1)S(1)}, u32[]{:S(2)}, u32[]{:S(2)}) collective-permute-start(bf16[256,1024]{1,0:T(8,128)(2,1)} %collective-permute-done.5.refs_4_.moved_4), channel_id=1, source_target_pairs={{0,32},{32,0},{64,96},{96,64},{1,33},{33,1},{65,97},{97,65},{2,34}... | collective-permute-start | bytes 1572872 | tf_op jit(solution)/shard_map/ppermute | solution.py:34
  31.5 6.4 %collective-permute-start.10 = (bf16[256,1024]{1,0:T(8,128)(2,1)S(1)}, bf16[256,1024]{1,0:T(8,128)(2,1)S(1)}, u32[]{:S(2)}, u32[]{:S(2)}) collective-permute-start(bf16[256,1024]{1,0:T(8,128)(2,1)S(1)} %collective-permute-done.6.refs_6_.moved_6), channel_id=1, source_target_pairs={{0,32},{32,0},{64,96},{96,64},{1,33},{33,1},{65,97},{97,65},{2,34}... | collective-permute-start | bytes 1572872 | tf_op jit(solution)/shard_map/ppermute | solution.py:34
  37.0 9.0 %copy-start.1 = (bf16[32,80,128]{2,1,0:T(8,128)(2,1)}, bf16[32,80,128]{2,1,0:T(8,128)(2,1)S(1)}, u32[]{:S(2)}) copy-start(bf16[32,80,128]{2,1,0:T(8,128)(2,1)S(1)} %all-to-all-done.arrived_any) | copy-start | bytes 1966084
  37.8 0.8 copy-start.5
  37.8 1.0 copy-start.6
  37.8 1.1 copy-start.7
  38.9 0.8 copy-start.8
  73.6 2.6 %collective-permute-start.11 = (bf16[32,24,512]{2,1,0:T(8,128)(2,1)}, bf16[32,24,512]{2,1,0:T(8,128)(2,1)S(1)}, u32[]{:S(2)}, u32[]{:S(2)}) collective-permute-start(bf16[32,24,512]{2,1,0:T(8,128)(2,1)} %get-tuple-element.15), channel_id=1, source_target_pairs={{0,32},{32,0},{64,96},{96,64},{1,33},{33,1},{65,97},{97,65},{2,34}... | collective-permute-start | bytes 2359304 | tf_op jit(solution)/shard_map/ppermute | solution.py:34
  77.9 50.3 %copy-start.2 = (s32[4]{0:T(128)S(1)}, s32[4]{0:T(128)}, u32[]{:S(2)}) copy-start(s32[4]{0:T(128)} %param.18) | copy-start | bytes 52
  117.8 10.1 %collective-permute-start.12 = (f32[24,512]{1,0:T(8,128)S(1)}, f32[24,512]{1,0:T(8,128)S(1)}, u32[]{:S(2)}, u32[]{:S(2)}) collective-permute-start(f32[24,512]{1,0:T(8,128)S(1)} %convert_reduce_fusion), channel_id=1, source_target_pairs={{0,64},{32,96},{64,0},{96,32},{1,65},{33,97},{65,1},{97,33},{2,66}... | collective-permute-start | bytes 147464 | tf_op jit(solution)/shard_map/ppermute | solution.py:34
  125.2 4.3 %collective-permute-start.13 = (f32[16,512]{1,0:T(8,128)S(1)}, f32[16,512]{1,0:T(8,128)S(1)}, u32[]{:S(2)}, u32[]{:S(2)}) collective-permute-start(f32[16,512]{1,0:T(8,128)S(1)} %slice.85), channel_id=1, source_target_pairs={{0,32},{32,0},{64,96},{96,64},{1,33},{33,1},{65,97},{97,65},{2,34}... | collective-permute-start | bytes 98312 | tf_op jit(solution)/shard_map/ppermute | solution.py:34
  128.0 3.3 %collective-permute-start.14 = (f32[16,512]{1,0:T(8,128)S(1)}, f32[16,512]{1,0:T(8,128)S(1)}, u32[]{:S(2)}, u32[]{:S(2)}) collective-permute-start(f32[16,512]{1,0:T(8,128)S(1)} %slice.85), channel_id=1, source_target_pairs={{0,96},{32,64},{64,32},{96,0},{1,97},{33,65},{65,33},{97,1},{2,98}... | collective-permute-start | bytes 98312 | tf_op jit(solution)/shard_map/ppermute | solution.py:34

commit v6 on v5

--- a/solution.py
+++ b/solution.py
@@ -12,8 +12,8 @@
 BLK = 128
 CAP = 2
 OWN = 32
-STAY = 16
-MOVE = 4
+STAY = 8
+MOVE = 6
 HALF = MOVE // 2
 MOST = 5 * CAP
 SIDE = 4

time: 132 us -> 130 us (0.985)
  blocking collectives: 39.8 us -> 21.2 us
  waiting for transfers between devices: 7.76 us -> 18.2 us
  Pallas kernels: 39.3 us -> 48.7 us
  starting transfers between devices: 31.7 us -> 26.3 us
    all_to_all x1, blocking collectives: 39.8 us -> 21.2 us  [shards(): lax.all_to_all(terms, 'shard', split_axis=0, concat_axis=0, tiled=True)]
    ppermute x4, waiting for transfers between devices: 3.4 us -> 14.8 us  [along(): return lax.ppermute(x, 'shard', pairs)]
    pallas_call x1, Pallas kernels: 27.6 us -> 36.3 us  [pair_terms(): pl.pallas_call(pair_kernel, out_shape=(jax.ShapeDtypeStruct(shape, F32),...]
    ppermute x11, starting transfers between devices: 16 us -> 10.5 us  [swapped(): return lax.ppermute(x, 'blk', [(i, i ^ by) for i in range(GROUPS)])]
  transfers between devices with their start and end apart: 16 -> 16, of which waited for: 4 -> 6; matrix products, arithmetic and copies ran while one was open for 5% -> 6% of each run, Pallas kernels for 4% -> 3%
where the time goes in v6:
time: 130 us; the launch traced here: 129 us
  Pallas kernels  48.7 us (37%)
  starting transfers between devices  26.3 us (20%)
  blocking collectives  21.2 us (16%)
  waiting for transfers between devices  18.2 us (14%)
  other arithmetic  6.39 us (5%)
  local copies, waits for them, and re-layouts  5.53 us (4%)
  matrix products  2.13 us (2%)
    pallas_call x1, Pallas kernels, pair_terms(): pl.pallas_call(pair_kernel, out_shape=(jax.ShapeDtypeStruct(shape, F32),...  36.3 us
    all_to_all x1, blocking collectives, shards(): lax.all_to_all(terms, 'shard', split_axis=0, concat_axis=0, tiled=True)  21.2 us
    ppermute x4, waiting for transfers between devices, along(): return lax.ppermute(x, 'shard', pairs)  14.8 us
    pallas_call x2, Pallas kernels, tower_vectors(): pl.pallas_call(tower_kernel, grid=grid, in_specs=[pl.BlockSpec((width, E)...  12.4 us
    ppermute x11, starting transfers between devices, swapped(): return lax.ppermute(x, 'blk', [(i, i ^ by) for i in range(GROUPS)])  10.5 us
    all_to_all x1, starting transfers between devices, shards(): lax.all_to_all(sent + codes, 'shard', split_axis=0, concat_axis=0, tiled=...  9.16 us
    ppermute x4, starting transfers between devices, along(): return lax.ppermute(x, 'shard', pairs)  6.64 us
    ppermute x11, waiting for transfers between devices, swapped(): return lax.ppermute(x, 'blk', [(i, i ^ by) for i in range(GROUPS)])  3.32 us
  transfers between devices with their start and end apart: 16, of which 6 were waited for; matrix products, arithmetic and copies ran while one was open for 6% of the time, Pallas kernels for 3%

profile of v6, /device:TPU:1, one launch (start us, length us, event | category | flops | bytes accessed | tf_op | source)
XLA Modules:
  0.0 129.2 jit_solution(11433745127547868232)
XLA Ops:
  0.6 0.7 fusion.8
  1.6 0.8 fusion
  2.7 2.6 %collective-permute-start.2 = (bf16[48,64]{0,1:T(8,128)(2,1)S(1)}, bf16[48,64]{0,1:T(8,128)(2,1)S(1)}, u32[]{:S(2)}, u32[]{:S(2)}) collective-permute-start(bf16[48,64]{0,1:T(8,128)(2,1)S(1)} %pad_maximum_fusion.1), channel_id=1, source_target_pairs={{0,96},{32,64},{64,32},{96,0},{1,97},{33,65},{65,33},{97,1},{2,98}... | collective-permute-start | bytes 18440 | tf_op jit(solution)/shard_map/ppermute | solution.py:34
  5.5 0.3 collective-permute-start
  5.8 2.2 %constant_dynamic-slice_fusion.3 = (bf16[384,1024]{1,0:T(8,128)(2,1)S(1)}, bf16[384,1024]{1,0:T(8,128)(2,1)S(1)}, bf16[384,1024]{1,0:T(8,128)(2,1)S(1)}, bf16[384,1024]{1,0:T(8,128)(2,1)S(1)}) fusion(bf16[4096,1024]{1,0:T(8,128)(2,1)} %features_stay.1, s32[]{:T(128)S(6)} %select_n.149, s32[]{:T(128)S(6)} %select_n.148, s32[]{:T(128)S(6)} %select_n.147, ...), kind=kLoop, calls=%fused_computation.77 | loop fusion | bytes 6291472 | tf_op jit(solution)/shard_map/dynamic_slice | solution.py:412
  8.0 2.8 %collective-permute-start.6 = (bf16[384,1024]{1,0:T(8,128)(2,1)S(1)}, bf16[384,1024]{1,0:T(8,128)(2,1)}, u32[]{:S(2)}, u32[]{:S(2)}) collective-permute-start(bf16[384,1024]{1,0:T(8,128)(2,1)S(1)} %get-tuple-element.16), channel_id=1, source_target_pairs={{0,12},{1,13},{2,14},{3,15},{4,0},{5,1},{6,2},{7,3},{8,4},{9,5},{1... | collective-permute-start | bytes 2359304 | tf_op jit(solution)/shard_map/ppermute | solution.py:47
  11.4 3.8 %collective-permute-start.4 = (bf16[384,1024]{1,0:T(8,128)(2,1)S(1)}, bf16[384,1024]{1,0:T(8,128)(2,1)}, u32[]{:S(2)}, u32[]{:S(2)}) collective-permute-start(bf16[384,1024]{1,0:T(8,128)(2,1)S(1)} %get-tuple-element.18), channel_id=1, source_target_pairs={{0,3},{1,0},{2,1},{3,2},{4,7},{5,4},{6,5},{7,6},{8,11},{9,8},{10,9... | collective-permute-start | bytes 2359304 | tf_op jit(solution)/shard_map/ppermute | solution.py:47
  15.8 1.0 pad_add_fusion
  16.8 9.2 %all-to-all-start = ((bf16[32,80,128]{2,1,0:T(8,128)(2,1)}), bf16[32,80,128]{2,1,0:T(8,128)(2,1)}, u32[]{:S(2)}, u32[]{:S(2)}) async-start(bf16[32,80,128]{2,1,0:T(8,128)(2,1)} %pad_add_fusion), calls=%async_computation | async-start | bytes 1310720 | tf_op jit(solution)/shard_map/all_to_all | solution.py:460
  25.9 1.5 %collective-permute-done.6.refs_6_.moved_6 = bf16[384,1024]{1,0:T(8,128)(2,1)} collective-permute-done((bf16[384,1024]{1,0:T(8,128)(2,1)S(1)}, bf16[384,1024]{1,0:T(8,128)(2,1)}, u32[]{:S(2)}, u32[]{:S(2)}) %collective-permute-start.6) | collective-permute-done | bytes 786464 | tf_op jit(solution)/shard_map/ppermute | solution.py:47
  27.4 3.4 %collective-permute-done.5.refs_4_.moved_4 = bf16[384,1024]{1,0:T(8,128)(2,1)} collective-permute-done((bf16[384,1024]{1,0:T(8,128)(2,1)S(1)}, bf16[384,1024]{1,0:T(8,128)(2,1)}, u32[]{:S(2)}, u32[]{:S(2)}) %collective-permute-start.5) | collective-permute-done | bytes 786464 | tf_op jit(solution)/shard_map/ppermute | solution.py:47
  30.9 6.9 %collective-permute-done.4.refs_2_.moved_2 = bf16[384,1024]{1,0:T(8,128)(2,1)} collective-permute-done((bf16[384,1024]{1,0:T(8,128)(2,1)S(1)}, bf16[384,1024]{1,0:T(8,128)(2,1)}, u32[]{:S(2)}, u32[]{:S(2)}) %collective-permute-start.4) | collective-permute-done | bytes 786464 | tf_op jit(solution)/shard_map/ppermute | solution.py:47
  37.8 3.0 %collective-permute-done.3.refs_0_.moved_0 = bf16[384,1024]{1,0:T(8,128)(2,1)} collective-permute-done((bf16[384,1024]{1,0:T(8,128)(2,1)S(1)}, bf16[384,1024]{1,0:T(8,128)(2,1)}, u32[]{:S(2)}, u32[]{:S(2)}) %collective-permute-start.3) | collective-permute-done | bytes 786464 | tf_op jit(solution)/shard_map/ppermute | solution.py:47
  40.8 2.6 %collective-permute-start.7 = (bf16[384,1024]{1,0:T(8,128)(2,1)}, bf16[384,1024]{1,0:T(8,128)(2,1)S(1)}, u32[]{:S(2)}, u32[]{:S(2)}) collective-permute-start(bf16[384,1024]{1,0:T(8,128)(2,1)} %collective-permute-done.3.refs_0_.moved_0), channel_id=1, source_target_pairs={{0,32},{32,0},{64,96},{96,64},{1,33},{33,1},{65,97},{97,65},{2,34}... | collective-permute-start | bytes 2359304 | tf_op jit(solution)/shard_map/ppermute | solution.py:34
  43.4 0.5 collective-permute-start.9
  43.9 1.5 %slice_convert_fusion = s32[32,1,21]{2,1,0:T(1,128)} fusion(bf16[32,80,128]{2,1,0:T(8,128)(2,1)} %all-to-all-done.arrived_any), kind=kLoop, calls=%fused_computation.16 | loop fusion | flops 672 | bytes 4032 | tf_op jit(solution)/shard_map/convert_element_type | solution.py:461
  45.5 4.2 %tower_stay.1.vt_stay = bf16[8,64,1024]{2,1,0:T(8,128)(2,1)} custom-call(bf16[1024,512]{1,0:T(8,128)(2,1)} %weight.1, bf16[4096,1024]{1,0:T(8,128)(2,1)} %features_stay.1), custom_call_target="tpu_custom_call" | custom-call | flops 1073741824 | bytes 7340032 | tf_op jit(solution)/shard_map/tower_stay/pallas_call | solution.py:84
  49.8 0.8 copy-done.3
  50.6 0.3 copy-done.4
  50.9 0.2 copy-done.5
  51.1 0.9 copy-done.6
  52.0 8.2 %tower_moved.1.vt_moved = bf16[24,64,1024]{2,1,0:T(8,128)(2,1)} custom-call(bf16[1024,512]{1,0:T(8,128)(2,1)} %weight.1, bf16[384,1024]{1,0:T(8,128)(2,1)} %collective-permute-done.3.refs_0_.moved_0, bf16[384,1024]{1,0:T(8,128)(2,1)} %copy-done.3, bf16[384,1024]{1,0:T(8,128)(2,1)} %collective-permute-done.4.refs_2_.moved_2, bf16[384,1024]{1,0:T(8,128)(2,1)} %copy-done.4, ...), custom_call_target="tpu_custom_call" | custom-call | flops 3221225472 | bytes 7340032 | tf_op jit(solution)/shard_map/tower_moved/pallas_call | solution.py:84
  60.2 36.3 %pairs.1 = (f32[32,24,512]{2,1,0:T(8,128)}, bf16[32,24,512]{2,1,0:T(8,128)(2,1)}) custom-call(s32[32,21]{1,0:T(8,128)} %bitcast.60, s32[1]{0:T(128)} %bitcast.4.group, bf16[32,80,128]{2,1,0:T(8,128)(2,1)} %all-to-all-done.arrived_any, bf16[8,64,1024]{2,1,0:T(8,128)(2,1)} %tower_stay.1.vt_stay, bf16[24,64,1024]{2,1,0:T(8,128)(2,1)} %tower_moved.1.vt_moved, ...), custom_call_target="tpu_custom_call" | custom-call | flops 42949672960 | bytes 16777216 | tf_op jit(solution)/shard_map/pairs/pallas_call | solution.py:348
  96.6 2.5 %collective-permute-done.11 = bf16[32,24,512]{2,1,0:T(8,128)(2,1)S(1)} collective-permute-done((bf16[32,24,512]{2,1,0:T(8,128)(2,1)}, bf16[32,24,512]{2,1,0:T(8,128)(2,1)S(1)}, u32[]{:S(2)}, u32[]{:S(2)}) %collective-permute-start.11) | collective-permute-done | bytes 786464 | tf_op jit(solution)/shard_map/ppermute | solution.py:34
  99.1 1.7 %add_convert_fusion = bf16[32,24,512]{2,1,0:T(8,128)(2,1)S(1)} fusion(f32[32,24,512]{2,1,0:T(8,128)} %get-tuple-element.14, bf16[32,24,512]{2,1,0:T(8,128)(2,1)S(1)} %collective-permute-done.11), kind=kLoop, calls=%fused_computation.1 | loop fusion | flops 1179648 | bytes 3145728 | tf_op jit(solution)/shard_map/convert_element_type | solution.py:471
  100.8 21.2 %all_to_all.10 = bf16[32,24,512]{2,1,0:T(8,128)(2,1)S(1)} all-to-all(bf16[32,24,512]{2,1,0:T(8,128)(2,1)S(1)} %add_convert_fusion), channel_id=1, replica_groups=mesh['blk'=4,'shard'=32] {'shard'}, dimensions={0} | all-to-all | bytes 1572864 | tf_op jit(solution)/shard_map/all_to_all | solution.py:472
  122.2 2.6 %collective-permute-start.13 = (f32[16,512]{1,0:T(8,128)S(1)}, f32[16,512]{1,0:T(8,128)S(1)}, u32[]{:S(2)}, u32[]{:S(2)}) collective-permute-start(f32[16,512]{1,0:T(8,128)S(1)} %slice.85), channel_id=1, source_target_pairs={{0,32},{32,0},{64,96},{96,64},{1,33},{33,1},{65,97},{97,65},{2,34}... | collective-permute-start | bytes 98312 | tf_op jit(solution)/shard_map/ppermute | solution.py:34
  124.8 1.5 %collective-permute-start.14 = (f32[16,512]{1,0:T(8,128)S(1)}, f32[16,512]{1,0:T(8,128)S(1)}, u32[]{:S(2)}, u32[]{:S(2)}) collective-permute-start(f32[16,512]{1,0:T(8,128)S(1)} %slice.85), channel_id=1, source_target_pairs={{0,96},{32,64},{64,32},{96,0},{1,97},{33,65},{65,33},{97,1},{2,98}... | collective-permute-start | bytes 98312 | tf_op jit(solution)/shard_map/ppermute | solution.py:34
  126.5 0.3 fusion.11
  126.8 1.0 convolution_add_fusion
  127.8 0.8 collective-permute-done.14
  128.6 0.6 pad_maximum_fusion
  (55 shorter events, 2.3 us)
Async XLA Ops:
  0.6 0.9 copy-start
  2.7 8.7 %collective-permute-start.2 = (bf16[48,64]{0,1:T(8,128)(2,1)S(1)}, bf16[48,64]{0,1:T(8,128)(2,1)S(1)}, u32[]{:S(2)}, u32[]{:S(2)}) collective-permute-start(bf16[48,64]{0,1:T(8,128)(2,1)S(1)} %pad_maximum_fusion.1), channel_id=1, source_target_pairs={{0,96},{32,64},{64,32},{96,0},{1,97},{33,65},{65,33},{97,1},{2,98}... | collective-permute-start | bytes 18440 | tf_op jit(solution)/shard_map/ppermute | solution.py:34
  5.3 10.0 %collective-permute-start.1 = (bf16[48,64]{0,1:T(8,128)(2,1)S(1)}, bf16[48,64]{0,1:T(8,128)(2,1)S(1)}, u32[]{:S(2)}, u32[]{:S(2)}) collective-permute-start(bf16[48,64]{0,1:T(8,128)(2,1)S(1)} %pad_maximum_fusion.1), channel_id=1, source_target_pairs={{0,64},{32,96},{64,0},{96,32},{1,65},{33,97},{65,1},{97,33},{2,66}... | collective-permute-start | bytes 18440 | tf_op jit(solution)/shard_map/ppermute | solution.py:34
  5.5 9.9 %collective-permute-start = (bf16[48,64]{0,1:T(8,128)(2,1)S(1)}, bf16[48,64]{0,1:T(8,128)(2,1)S(1)}, u32[]{:S(2)}, u32[]{:S(2)}) collective-permute-start(bf16[48,64]{0,1:T(8,128)(2,1)S(1)} %pad_maximum_fusion.1), channel_id=1, source_target_pairs={{0,32},{32,0},{64,96},{96,64},{1,33},{33,1},{65,97},{97,65},{2,34}... | collective-permute-start | bytes 18440 | tf_op jit(solution)/shard_map/ppermute | solution.py:34
  5.8 5.0 %copy-start.2 = (s32[14]{0:T(128)S(1)}, s32[14]{0:T(128)}, u32[]{:S(2)}) copy-start(s32[14]{0:T(128)} %param.21) | copy-start | bytes 172
  5.8 5.0 %copy-start.7 = (s32[14,1]{0,1:T(1,128)S(1)}, s32[14,1]{0,1:T(1,128)}, u32[]{:S(2)}) copy-start(s32[14,1]{0,1:T(1,128)} %param.20) | copy-start | bytes 172
  8.0 19.5 %collective-permute-start.6 = (bf16[384,1024]{1,0:T(8,128)(2,1)S(1)}, bf16[384,1024]{1,0:T(8,128)(2,1)}, u32[]{:S(2)}, u32[]{:S(2)}) collective-permute-start(bf16[384,1024]{1,0:T(8,128)(2,1)S(1)} %get-tuple-element.16), channel_id=1, source_target_pairs={{0,12},{1,13},{2,14},{3,15},{4,0},{5,1},{6,2},{7,3},{8,4},{9,5},{1... | collective-permute-start | bytes 2359304 | tf_op jit(solution)/shard_map/ppermute | solution.py:47
  10.8 20.1 %collective-permute-start.5 = (bf16[384,1024]{1,0:T(8,128)(2,1)S(1)}, bf16[384,1024]{1,0:T(8,128)(2,1)}, u32[]{:S(2)}, u32[]{:S(2)}) collective-permute-start(bf16[384,1024]{1,0:T(8,128)(2,1)S(1)} %get-tuple-element.17), channel_id=1, source_target_pairs={{0,4},{1,5},{2,6},{3,7},{4,8},{5,9},{6,10},{7,11},{8,12},{9,13},{1... | collective-permute-start | bytes 2359304 | tf_op jit(solution)/shard_map/ppermute | solution.py:47
  11.4 26.4 %collective-permute-start.4 = (bf16[384,1024]{1,0:T(8,128)(2,1)S(1)}, bf16[384,1024]{1,0:T(8,128)(2,1)}, u32[]{:S(2)}, u32[]{:S(2)}) collective-permute-start(bf16[384,1024]{1,0:T(8,128)(2,1)S(1)} %get-tuple-element.18), channel_id=1, source_target_pairs={{0,3},{1,0},{2,1},{3,2},{4,7},{5,4},{6,5},{7,6},{8,11},{9,8},{10,9... | collective-permute-start | bytes 2359304 | tf_op jit(solution)/shard_map/ppermute | solution.py:47
  15.3 25.5 %collective-permute-start.3 = (bf16[384,1024]{1,0:T(8,128)(2,1)S(1)}, bf16[384,1024]{1,0:T(8,128)(2,1)}, u32[]{:S(2)}, u32[]{:S(2)}) collective-permute-start(bf16[384,1024]{1,0:T(8,128)(2,1)S(1)} %get-tuple-element.19), channel_id=1, source_target_pairs={{0,1},{1,2},{2,3},{3,0},{4,5},{5,6},{6,7},{7,4},{8,9},{9,10},{10,1... | collective-permute-start | bytes 2359304 | tf_op jit(solution)/shard_map/ppermute | solution.py:47
  16.8 27.2 %all-to-all-start = ((bf16[32,80,128]{2,1,0:T(8,128)(2,1)}), bf16[32,80,128]{2,1,0:T(8,128)(2,1)}, u32[]{:S(2)}, u32[]{:S(2)}) async-start(bf16[32,80,128]{2,1,0:T(8,128)(2,1)} %pad_add_fusion), calls=%async_computation | async-start | bytes 1310720 | tf_op jit(solution)/shard_map/all_to_all | solution.py:460
  40.8 8.9 %collective-permute-start.7 = (bf16[384,1024]{1,0:T(8,128)(2,1)}, bf16[384,1024]{1,0:T(8,128)(2,1)S(1)}, u32[]{:S(2)}, u32[]{:S(2)}) collective-permute-start(bf16[384,1024]{1,0:T(8,128)(2,1)} %collective-permute-done.3.refs_0_.moved_0), channel_id=1, source_target_pairs={{0,32},{32,0},{64,96},{96,64},{1,33},{33,1},{65,97},{97,65},{2,34}... | collective-permute-start | bytes 2359304 | tf_op jit(solution)/shard_map/ppermute | solution.py:34
  43.4 6.3 %collective-permute-start.8 = (bf16[384,1024]{1,0:T(8,128)(2,1)}, bf16[384,1024]{1,0:T(8,128)(2,1)S(1)}, u32[]{:S(2)}, u32[]{:S(2)}) collective-permute-start(bf16[384,1024]{1,0:T(8,128)(2,1)} %collective-permute-done.4.refs_2_.moved_2), channel_id=1, source_target_pairs={{0,32},{32,0},{64,96},{96,64},{1,33},{33,1},{65,97},{97,65},{2,34}... | collective-permute-start | bytes 2359304 | tf_op jit(solution)/shard_map/ppermute | solution.py:34
  43.4 6.3 %collective-permute-start.9 = (bf16[384,1024]{1,0:T(8,128)(2,1)}, bf16[384,1024]{1,0:T(8,128)(2,1)S(1)}, u32[]{:S(2)}, u32[]{:S(2)}) collective-permute-start(bf16[384,1024]{1,0:T(8,128)(2,1)} %collective-permute-done.5.refs_4_.moved_4), channel_id=1, source_target_pairs={{0,32},{32,0},{64,96},{96,64},{1,33},{33,1},{65,97},{97,65},{2,34}... | collective-permute-start | bytes 2359304 | tf_op jit(solution)/shard_map/ppermute | solution.py:34
  43.9 5.8 %collective-permute-start.10 = (bf16[384,1024]{1,0:T(8,128)(2,1)}, bf16[384,1024]{1,0:T(8,128)(2,1)S(1)}, u32[]{:S(2)}, u32[]{:S(2)}) collective-permute-start(bf16[384,1024]{1,0:T(8,128)(2,1)} %collective-permute-done.6.refs_6_.moved_6), channel_id=1, source_target_pairs={{0,32},{32,0},{64,96},{96,64},{1,33},{33,1},{65,97},{97,65},{2,34}... | collective-permute-start | bytes 2359304 | tf_op jit(solution)/shard_map/ppermute | solution.py:34
  49.7 0.9 copy-start.3
  49.7 1.1 copy-start.4
  49.7 1.4 %copy-start.5 = (bf16[384,1024]{1,0:T(8,128)(2,1)}, bf16[384,1024]{1,0:T(8,128)(2,1)S(1)}, u32[]{:S(2)}) copy-start(bf16[384,1024]{1,0:T(8,128)(2,1)S(1)} %collective-permute-done.9.refs_5_.moved_5) | copy-start | bytes 2359300
  51.1 0.9 copy-start.6
  96.5 2.6 %collective-permute-start.11 = (bf16[32,24,512]{2,1,0:T(8,128)(2,1)}, bf16[32,24,512]{2,1,0:T(8,128)(2,1)S(1)}, u32[]{:S(2)}, u32[]{:S(2)}) collective-permute-start(bf16[32,24,512]{2,1,0:T(8,128)(2,1)} %get-tuple-element.15), channel_id=1, source_target_pairs={{0,32},{32,0},{64,96},{96,64},{1,33},{33,1},{65,97},{97,65},{2,34}... | collective-permute-start | bytes 2359304 | tf_op jit(solution)/shard_map/ppermute | solution.py:34
  100.8 25.7 %copy-start.1 = (s32[4]{0:T(128)S(1)}, s32[4]{0:T(128)}, u32[]{:S(2)}) copy-start(s32[4]{0:T(128)} %param.18) | copy-start | bytes 52
  122.1 4.2 %collective-permute-start.12 = (f32[24,512]{1,0:T(8,128)S(1)}, f32[24,512]{1,0:T(8,128)S(1)}, u32[]{:S(2)}, u32[]{:S(2)}) collective-permute-start(f32[24,512]{1,0:T(8,128)S(1)} %convert_reduce_fusion), channel_id=1, source_target_pairs={{0,64},{32,96},{64,0},{96,32},{1,65},{33,97},{65,1},{97,33},{2,66}... | collective-permute-start | bytes 147464 | tf_op jit(solution)/shard_map/ppermute | solution.py:34
  122.2 5.6 %collective-permute-start.13 = (f32[16,512]{1,0:T(8,128)S(1)}, f32[16,512]{1,0:T(8,128)S(1)}, u32[]{:S(2)}, u32[]{:S(2)}) collective-permute-start(f32[16,512]{1,0:T(8,128)S(1)} %slice.85), channel_id=1, source_target_pairs={{0,32},{32,0},{64,96},{96,64},{1,33},{33,1},{65,97},{97,65},{2,34}... | collective-permute-start | bytes 98312 | tf_op jit(solution)/shard_map/ppermute | solution.py:34
  124.8 3.8 %collective-permute-start.14 = (f32[16,512]{1,0:T(8,128)S(1)}, f32[16,512]{1,0:T(8,128)S(1)}, u32[]{:S(2)}, u32[]{:S(2)}) collective-permute-start(f32[16,512]{1,0:T(8,128)S(1)} %slice.85), channel_id=1, source_target_pairs={{0,96},{32,64},{64,32},{96,0},{1,97},{33,65},{65,33},{97,1},{2,98}... | collective-permute-start | bytes 98312 | tf_op jit(solution)/shard_map/ppermute | solution.py:34
